TPU v7x, 32 devices: a whole 2x2x4 slice. The times are simulated.
32 devices in a mesh: grp: 8 (over z, core), tp: 4 (over y, x).
Axes of the slice: x: 2, y: 2, z: 4, core: 2. Of those that a mesh axis runs over, the one named last changes fastest.
Arguments:
- tokens: bfloat16 [8192, 1280], P('grp', 'tp'), may hold values from -40 to 40
- segment: int32 [8192], P('grp'), may hold values from 0 to 31, as said below
- ln_gain: float32 [1280], replicated, may hold values from 0.1 to 1.9
- w_qkv: bfloat16 [3, 1280, 1280], P(None, None, 'tp'), may hold values from -4.6 to 4.6
- w_out: bfloat16 [1280, 1280], P('tp'), may hold values from -0.25 to 0.25
- merge_gain: float32 [1280], replicated, may hold values from 0.1 to 1.9
- w_merge: bfloat16 [4, 1280, 1280], P(None, 'tp'), may hold values from -0.078125 to 0.078125
- owner: int32 [2048, 1], P('grp'), may hold values from 0 to 7; in each aligned block of 256 rows (0 to 255, 256 to 511, ...) at most 64 rows name the same one
Outputs:
- hidden_out: bfloat16 [8192, 1280], P('grp', 'tp')
- routed: bfloat16 [8, 8, 64, 1280], P('grp', None, None, 'tp')
Inputs may be any that keep to these rules, and one draw needn't show every extreme that they name: `segment`: along each group's rows the ids never fall and come in runs of whole multiples of 4 rows, each run of 4 being one 2x2 patch block of that image; rows of one id lie in one group g or in the two groups g and g + 4, and every group shares one image with that partner group. Among the merged blocks of one group no owner is named more than 64 times; in some group one owner is named exactly 64 times.
All inputs are finite; a program needn't handle non-finite values.
Results may differ from a plain program's by a relative error of at most 0.023.
Values may be sent and summed in bfloat16 or wider, within the bound.
No kernel may reach another device: no remote copies, remote signals or barrier semaphores. Data moves between devices by JAX's collectives and lax.ppermute only.
A program may use at most 64 MiB of HBM per device.

v0:
```python
import jax
import jax.numpy as jnp
from jax import lax
from jax.sharding import PartitionSpec as P

HD = 80


EPS = 1e-06


def swapped(x, axis, distance):
    return lax.ppermute(x, axis, [(i, i ^ 1 << distance) for i in range(lax.axis_size(axis))])


def layer_norm(rows_in, gain):
    values_f = rows_in.astype(jnp.float32)
    center = jnp.mean(values_f, axis=-1, keepdims=True)
    spread = jnp.mean((values_f - center) ** 2, axis=-1, keepdims=True)
    return (values_f - center) * lax.rsqrt(spread + EPS) * gain


def shards(tokens, segment, ln_gain, w_qkv, w_out, merge_gain, w_merge, owner):
    row_count, local_width = tokens.shape
    tp_count = lax.axis_size("tp")
    grp_count = lax.axis_size("grp")
    full_width = local_width * tp_count
    head_count = local_width // HD
    gathered = lax.all_gather(tokens, "tp", axis=1, tiled=True)
    normed = layer_norm(gathered, ln_gain).astype(jnp.bfloat16)
    triple = jnp.einsum("td,jde->jte", normed, w_qkv, preferred_element_type=jnp.float32).astype(
        jnp.bfloat16
    )
    far_pair, far_segment = swapped((triple[1:], segment), "grp", grp_count.bit_length() - 2)
    key_rows = jnp.concatenate([triple[1], far_pair[0]], axis=0)
    value_rows = jnp.concatenate([triple[2], far_pair[1]], axis=0)
    key_segment = jnp.concatenate([segment, far_segment], axis=0)
    block_rows = min(512, row_count)
    block_count = row_count // block_rows
    score_scale = HD ** (-0.5)

    def one_block(block_index):
        block_start = block_index * block_rows
        query_rows = lax.dynamic_slice_in_dim(triple[0], block_start, block_rows, 0)
        query_segment = lax.dynamic_slice_in_dim(segment, block_start, block_rows, 0)
        same_image = query_segment[:, None] == key_segment[None, :]
        head_outputs = []
        for head_number in range(head_count):
            low_col = head_number * HD
            score_block = (
                jnp.dot(
                    query_rows[:, low_col : low_col + HD],
                    key_rows[:, low_col : low_col + HD].T,
                    preferred_element_type=jnp.float32,
                )
                * score_scale
            )
            score_block = jnp.where(same_image, score_block, -1e30)
            row_top = jnp.max(score_block, axis=1, keepdims=True)
            raw_weights = jnp.exp(score_block - row_top)
            sums_total = jnp.sum(raw_weights, axis=1, keepdims=True)
            mixed_rows = jnp.dot(
                raw_weights.astype(jnp.bfloat16),
                value_rows[:, low_col : low_col + HD],
                preferred_element_type=jnp.float32,
            )
            head_outputs.append(mixed_rows / sums_total)
        return jnp.concatenate(head_outputs, axis=1).astype(jnp.bfloat16)

    context = lax.map(one_block, jnp.arange(block_count, dtype=jnp.int32)).reshape(
        row_count, local_width
    )
    out_terms = jnp.dot(context, w_out, preferred_element_type=jnp.float32)
    summed = lax.psum_scatter(
        out_terms.astype(jnp.bfloat16), "tp", scatter_dimension=1, tiled=True
    ).astype(jnp.float32)
    hidden_out = (tokens.astype(jnp.float32) + summed).astype(jnp.bfloat16)
    offset = lax.axis_index("tp") * local_width
    gain_part = lax.dynamic_slice_in_dim(merge_gain, offset, local_width, 0)
    local_rows = hidden_out.astype(jnp.float32)
    full_rows = lax.all_gather(hidden_out, "tp", axis=1, tiled=True).astype(jnp.float32)
    center = jnp.mean(full_rows, axis=1, keepdims=True)
    spread = jnp.mean((full_rows - center) ** 2, axis=1, keepdims=True)
    merge_normed = ((local_rows - center) * lax.rsqrt(spread + EPS) * gain_part).astype(
        jnp.bfloat16
    )
    merged_count = row_count // 4
    block_inputs = merge_normed.reshape(merged_count, 4 * local_width)
    flat_weight = w_merge.reshape(4 * local_width, full_width)
    cap_slots = max(2, merged_count // grp_count * 2)
    targets = owner[:, 0]
    onehot = (targets[:, None] == jnp.arange(grp_count, dtype=jnp.int32)[None, :]).astype(
        jnp.float32
    )
    lower_mask = (jnp.arange(merged_count)[:, None] > jnp.arange(merged_count)[None, :]).astype(
        jnp.float32
    )
    earlier = jnp.dot(lower_mask, onehot, precision=lax.Precision.HIGHEST)
    slot_index = jnp.sum(earlier * onehot, axis=1).astype(jnp.int32)
    slot_place = targets * cap_slots + slot_index
    dispatch = (
        jnp.arange(grp_count * cap_slots, dtype=jnp.int32)[:, None] == slot_place[None, :]
    ).astype(jnp.bfloat16)
    merge_terms = jnp.dot(block_inputs, flat_weight, preferred_element_type=jnp.float32)
    merged_rows = lax.psum_scatter(
        merge_terms.astype(jnp.bfloat16), "tp", scatter_dimension=1, tiled=True
    )
    outgoing = (
        jnp.dot(dispatch, merged_rows, preferred_element_type=jnp.float32)
        .astype(jnp.bfloat16)
        .reshape(grp_count, cap_slots, local_width)
    )
    routed = lax.all_to_all(outgoing, "grp", split_axis=0, concat_axis=0, tiled=True)
    return (hidden_out, routed[None])


def solution(mesh):
    return jax.shard_map(
        shards,
        mesh=mesh,
        in_specs=(
            P("grp", "tp"),
            P("grp"),
            P(),
            P(None, None, "tp"),
            P("tp", None),
            P(),
            P(None, "tp", None),
            P("grp", None),
        ),
        out_specs=(P("grp", "tp"), P("grp", None, None, "tp")),
        check_vma=False,
    )
```

profile of v0, /device:TPU:0, one launch (start us, length us, event | category | flops | bytes accessed | tf_op | source)
XLA Modules:
  0.0 318.8 jit_solution(18328325174139308212)
XLA Ops:
  7.2 0.7 all-gather.3.cloned.1.call-update
  8.0 44.3 %all-gather.3.cloned.1.call-done = bf16[1024,1280]{0,1:T(8,128)(2,1)} async-done(((bf16[1024,320]{0,1:T(8,128)(2,1)}), bf16[1024,1280]{0,1:T(8,128)(2,1)}) %all-gather.3.cloned.1.call-update) | async-done | bytes 2621456 | tf_op jit(solution)/shard_map/all_gather | solution.py:29
  52.2 2.3 convert_reduce_fusion.1
  54.8 0.7 fusion.70
  55.5 3.1 convert_bitcast_fusion
  58.6 1.3 copy-done.2
  59.9 1.2 slice.64
  61.1 2.4 collective-permute-start.1
  63.5 0.5 collective-permute-start
  64.0 57.0 %collective-permute-done = s32[1024]{0:T(1024)S(1)} collective-permute-done((s32[1024]{0:T(1024)S(1)}, s32[1024]{0:T(1024)S(1)}, u32[]{:S(2)}, u32[]{:S(2)}) %collective-permute-start) | collective-permute-done | bytes 4128 | tf_op jit(solution)/shard_map/ppermute | solution.py:13
  121.0 4.1 %copy.23 = bf16[3,1024,320]{2,1,0:T(8,128)(2,1)} copy(bf16[3,1024,320]{1,2,0:T(8,128)(2,1)} %copy-done.2) | data formatting | bytes 3932160 | tf_op jit(solution)/shard_map/while | solution.py:70
  125.1 1.4 slice_bitcast_fusion.1
  126.5 1.4 slice_bitcast_fusion
  127.9 1.8 pad_maximum_fusion
  129.6 2.5 copy.24
  132.2 2.5 copy.25
  134.7 30.5 %while.10 = (s32[]{:T(128)}, bf16[2,512,320]{1,2,0:T(8,128)(2,1)}, s32[2]{0:T(128)S(1)}, s32[1024]{0:T(1024)S(1)}, s32[2048]{0:T(1024)S(1)}, /*index=5*/bf16[3,1...) while((s32[]{:T(128)}, bf16[2,512,320]{1,2,0:T(8,128)(2,1)}, ...), condition=%wide.region_11.12_spmd, body=%wide.region_2.11_spmd.sunk | while | flops 1377366016 | bytes 68571888 | solution.py:70
  134.7 0.6 dynamic_slice.21
  135.8 1.2 slice.137
  137.2 2.1 fusion.134
  139.3 0.7 fusion.135
  140.0 0.9 fusion.136
  140.9 1.0 fusion.131
  141.9 0.7 fusion.132
  142.6 1.1 fusion.133
  143.7 1.0 fusion.128
  144.7 0.7 fusion.129
  145.4 1.0 fusion.130
  146.4 1.0 fusion.125
  147.5 0.7 fusion.126
  148.2 1.1 fusion.127
  149.2 0.8 maximum_dynamic-update-slice_fusion.2
  150.0 0.5 dynamic_slice.21
  151.1 1.2 slice.137
  152.4 2.1 fusion.134
  154.5 0.7 fusion.135
  155.2 0.9 fusion.136
  156.1 1.0 fusion.131
  157.1 0.7 fusion.132
  157.9 1.1 fusion.133
  158.9 1.0 fusion.128
  159.9 0.7 fusion.129
  160.6 1.0 fusion.130
  161.7 1.0 fusion.125
  162.7 0.7 fusion.126
  163.4 1.1 fusion.127
  164.5 0.8 maximum_dynamic-update-slice_fusion.2
  165.2 1.2 copy.34
  166.4 4.2 %convolution_convert_fusion = bf16[1024,1280]{0,1:T(8,128)(2,1)} fusion(bf16[1024,320]{0,1:T(8,128)(2,1)S(1)} %bitcast.57, bf16[320,1280]{1,0:T(8,128)(2,1)} %param.14), kind=kOutput, calls=%fused_computation.61 | convolution fusion | flops 840171520 | bytes 4096000 | tf_op jit(solution)/shard_map/dot_general | solution.py:73
  170.7 39.7 %reduce-scatter.5.cloned.1.call-done = bf16[1024,320]{0,1:T(8,128)(2,1)} async-done(((bf16[1024,1280]{0,1:T(8,128)(2,1)}), bf16[1024,320]{0,1:T(8,128)(2,1)}) %reduce-scatter.5.cloned.1.call-update) | async-done | bytes 655376 | tf_op jit(solution)/shard_map/reduce_scatter | solution.py:74
  210.4 2.4 add_convert_fusion
  212.8 0.8 dynamic_slice.15
  213.6 39.0 %all-gather.5.cloned.1.call-done = bf16[1024,1280]{0,1:T(8,128)(2,1)} async-done(((bf16[1024,320]{0,1:T(8,128)(2,1)}), bf16[1024,1280]{0,1:T(8,128)(2,1)}) %all-gather.5.cloned.1.call-update) | async-done | bytes 2621456 | tf_op jit(solution)/shard_map/all_gather | solution.py:81
  252.6 2.3 convert_reduce_fusion
  255.1 0.7 fusion.74
  255.9 1.1 multiply_convert_fusion
  256.9 2.2 copy.27
  259.1 2.5 reshape.124
  261.7 3.3 %fusion.81 = bf16[1280,256]{1,0:T(8,128)(2,1)} fusion(bf16[256,1280]{1,0:T(8,128)(2,1)} %reshape.124, bf16[1280,1280]{1,0:T(8,128)(2,1)S(1)} %bitcast.54), kind=kOutput, calls=%fused_computation.68 | convolution fusion | flops 839188480 | bytes 4587520 | tf_op jit(solution)/shard_map/dot_general | solution.py:104
  265.2 25.3 %reduce-scatter.7.cloned.1.call-done = bf16[320,256]{1,0:T(8,128)(2,1)} async-done(((bf16[1280,256]{1,0:T(8,128)(2,1)}), bf16[320,256]{1,0:T(8,128)(2,1)}) %reduce-scatter.7.cloned.1.call-update) | async-done | bytes 163856
  290.5 1.9 convolution_convert_fusion.2
  292.5 1.9 copy.29
  294.4 17.2 %all_to_all.5 = bf16[8,64,320]{2,1,0:T(8,128)(2,1)S(1)} all-to-all(bf16[8,64,320]{2,1,0:T(8,128)(2,1)} %bitcast.56), channel_id=1, replica_groups=mesh['grp'=8,'tp'=4] {'grp'}, dimensions={0} | all-to-all | bytes 655360 | tf_op jit(solution)/shard_map/all_to_all | solution.py:113
  311.5 0.7 copy.43
  (46 shorter events, 1.1 us)
Async XLA Ops:
  7.2 254.5 %copy-start = (bf16[4,320,1280]{2,1,0:T(8,128)(2,1)S(1)}, bf16[4,320,1280]{2,1,0:T(8,128)(2,1)}, u32[]{:S(2)}) copy-start(bf16[4,320,1280]{2,1,0:T(8,128)(2,1)} %param.16) | copy-start | bytes 9830404
  7.2 48.3 %copy-start.10 = (f32[1280]{0:T(1024)S(1)}, f32[1280]{0:T(1024)}, u32[]{:S(2)}) copy-start(f32[1280]{0:T(1024)} %param.12) | copy-start | bytes 15364
  7.2 45.1 %all-gather.3.cloned.1.call-start = ((), (), s32[]{:S(2)}) async-start(), calls=%async_computation.3 | async-start | bytes 3276800 | tf_op jit(solution)/shard_map/all_gather | solution.py:29
  7.9 202.5 %reduce-scatter.5.cloned.1.call-start = ((), (), s32[]{:S(2)}) async-start(), calls=%async_computation.4 | async-start | bytes 3276800 | tf_op jit(solution)/shard_map/reduce_scatter | solution.py:74
  52.2 2.5 copy-start.4
  52.2 3.3 %copy-start.9 = (bf16[3,1280,320]{1,2,0:T(8,128)(2,1)S(1)}, bf16[3,1280,320]{1,2,0:T(8,128)(2,1)}, u32[]{:S(2)}) copy-start(bf16[3,1280,320]{1,2,0:T(8,128)(2,1)} %param.13) | copy-start | bytes 7372804
  55.5 7.9 %copy-start.7 = (s32[1024]{0:T(1024)S(1)}, s32[1024]{0:T(1024)}, u32[]{:S(2)}) copy-start(s32[1024]{0:T(1024)} %param.11) | copy-start | bytes 12292
  58.6 1.3 copy-start.2
  61.1 65.4 %collective-permute-start.1 = (bf16[2,1024,320]{1,2,0:T(8,128)(2,1)}, bf16[2,1024,320]{1,2,0:T(8,128)(2,1)}, u32[]{:S(2)}, u32[]{:S(2)}) collective-permute-start(bf16[2,1024,320]{1,2,0:T(8,128)(2,1)} %slice.64), channel_id=1, source_target_pairs={{0,16},{4,20},{8,24},{12,28},{16,0},{20,4},{24,8},{28,12},{1,17},{... | collective-permute-start | bytes 3932168 | tf_op jit(solution)/shard_map/ppermute | solution.py:13
  63.5 57.5 %collective-permute-start = (s32[1024]{0:T(1024)S(1)}, s32[1024]{0:T(1024)S(1)}, u32[]{:S(2)}, u32[]{:S(2)}) collective-permute-start(s32[1024]{0:T(1024)S(1)} %copy-done.7), channel_id=1, source_target_pairs={{0,16},{4,20},{8,24},{12,28},{16,0},{20,4},{24,8},{28,12},{1,17},{... | collective-permute-start | bytes 12296 | tf_op jit(solution)/shard_map/ppermute | solution.py:13
  137.2 2.8 copy-start.1
  139.3 1.6 copy-start.6
  152.4 2.8 copy-start.1
  154.5 1.6 copy-start.6
  170.7 81.9 %all-gather.5.cloned.1.call-start = ((), (), s32[]{:S(2)}) async-start(), calls=%async_computation.5 | async-start | bytes 3276800 | tf_op jit(solution)/shard_map/all_gather | solution.py:81
  212.8 77.8 %reduce-scatter.7.cloned.1.call-start = ((), (), s32[]{:S(2)}) async-start(), calls=%async_computation.6 | async-start | bytes 819200
  252.6 2.5 copy-start.3
  252.6 3.3 %copy-start.5 = (bf16[1024,320]{0,1:T(8,128)(2,1)S(1)}, bf16[1024,320]{0,1:T(8,128)(2,1)}, u32[]{:S(2)}) copy-start(bf16[1024,320]{0,1:T(8,128)(2,1)} %add_convert_fusion) | copy-start | bytes 1966084
  259.1 5.8 %copy-start.8 = (s32[256,1]{0,1:T(1,128)S(1)}, s32[256,1]{0,1:T(1,128)}, u32[]{:S(2)}) copy-start(s32[256,1]{0,1:T(1,128)} %param.17) | copy-start | bytes 3076
Sparse Core Ops, SparseCore 0:
  9.9 42.3 all-gather.2
  170.8 39.5 reduce-scatter.4
  212.9 39.6 all-gather.4
  265.1 25.3 reduce-scatter.6
where the time goes:
time: 320 us; the launch traced here: 319 us
  waiting for transfers between devices  206 us (64%)
  matrix products  31.1 us (10%)
  local copies, waits for them, and re-layouts  27.8 us (9%)
  other arithmetic  18.6 us (6%)
  blocking collectives  17.2 us (5%)
  between operations  13.9 us (4%)
    ppermute x2, waiting for transfers between devices, swapped(): lax.ppermute(x, axis, [(i, i ^ 1 << distance) for i in range(lax.axis_siz...  57 us
    all_gather x1, waiting for transfers between devices, shards(): gathered = lax.all_gather(tokens, 'tp', axis=1, tiled=True)  44.3 us
    reduce_scatter x1, waiting for transfers between devices, shards(): lax.psum_scatter(out_terms.astype(jnp.bfloat16), 'tp', scatter_dimension=...  39.7 us
    all_gather x1, waiting for transfers between devices, shards(): lax.all_gather(hidden_out, 'tp', axis=1, tiled=True).astype(jnp.float32)  39 us
    unnamed x5, waiting for transfers between devices  26.1 us
    all_to_all x1, blocking collectives, shards(): lax.all_to_all(outgoing, 'grp', split_axis=0, concat_axis=0, tiled=True)  17.2 us
    dot_general x8, matrix products, one_block(): jnp.dot(query_rows[:, low_col:low_col + HD], key_rows[:, low_col:low_col...  10.3 us
    while x3, local copies, waits for them, and re-layouts, shards(): lax.map(one_block, jnp.arange(block_count, dtype=jnp.int32))  9.17 us
  transfers between devices with their start and end apart: 6, of which 5 were waited for; matrix products, arithmetic and copies ran while one was open for 2% of the time, Pallas kernels for 0%

commit v1 on v0

v1 whole, which is shorter than its diff:
```python
import functools
import math

import jax
import jax.numpy as jnp
from jax import lax
from jax.experimental import pallas as pl
from jax.experimental.pallas import tpu as pltpu
from jax.sharding import PartitionSpec as P

HD = 80
PAD = 128
CODE_BITS = 16
FAR = 2.0**100
EPS = 1e-06
BLOCK = 256
BF = jnp.bfloat16
F32 = jnp.float32


def hop(x, axis, distance):
    return lax.ppermute(x, axis, [(i, i ^ distance) for i in range(lax.axis_size(axis))])


def params(limit):
    return pltpu.CompilerParams(vmem_limit_bytes=limit << 20)


def project_body(n_parts, n_proj, heads, scale, *refs):
    parts = refs[:n_parts]
    gain, w, qcode, kcode = refs[n_parts : n_parts + 4]
    outs = refs[n_parts + 4 : n_parts + 4 + n_proj]
    normed = refs[-1]
    values = [p[...].astype(F32) for p in parts]
    width = values[0].shape[1]
    total = width * n_parts
    center = sum(jnp.sum(v, axis=1, keepdims=True) for v in values) * (1.0 / total)
    values = [v - center for v in values]
    spread = sum(jnp.sum(v * v, axis=1, keepdims=True) for v in values) * (1.0 / total)
    inv = lax.rsqrt(spread + EPS)
    for k, v in enumerate(values):
        lo = k * width
        normed[:, lo : lo + width] = (v * inv * gain[0:1, lo : lo + width]).astype(BF)
    first = 3 - n_proj
    lane = lax.broadcasted_iota(jnp.int32, (1, PAD), 1)
    ones = jnp.where(lane == HD, 1.0, 0.0).astype(F32)
    for i in range(n_proj):
        kind = first + i
        acc = jnp.dot(normed[...], w[kind], preferred_element_type=F32)
        if kind == 0:
            acc = acc * scale
            extra = qcode[...].astype(F32)
        elif kind == 1:
            extra = kcode[...].astype(F32)
        else:
            extra = ones
        for h in range(heads):
            lo = h * PAD
            outs[i][:, lo : lo + PAD] = (acc[:, lo : lo + PAD] + extra).astype(BF)


def project(parts, gain, w, qcode, kcode, n_proj, row_start):
    rows, width = parts[0].shape
    wide = w.shape[2]
    heads = wide // PAD
    block = min(BLOCK, rows)
    steps = rows // block
    full = width * len(parts)
    first = row_start // block
    body = functools.partial(
        project_body, len(parts), n_proj, heads, HD**-0.5 * math.log2(math.e)
    )
    row = lambda i: (i, 0)
    code = pl.BlockSpec((block, PAD), lambda i: (first + i, 0))
    return pl.pallas_call(
        body,
        grid=(steps,),
        in_specs=[pl.BlockSpec((block, width), row) for _ in parts]
        + [
            pl.BlockSpec((1, full), lambda i: (0, 0)),
            pl.BlockSpec(w.shape, lambda i: (0, 0, 0), pipeline_mode=pl.Buffered(1)),
            code,
            code,
        ],
        out_specs=[pl.BlockSpec((block, wide), row) for _ in range(n_proj)],
        out_shape=[jax.ShapeDtypeStruct((rows, wide), BF) for _ in range(n_proj)],
        scratch_shapes=[pltpu.VMEM((block, full), BF)],
        compiler_params=params(24),
        cost_estimate=pl.CostEstimate(
            flops=2 * rows * full * wide * n_proj,
            bytes_accessed=2 * rows * (full + wide * n_proj) + 2 * full * wide * 3,
            transcendentals=rows,
        ),
        name="project",
    )(*parts, gain, w, qcode, kcode)


def attend_body(n_keys, heads, n_out, first_block, *refs):
    flags = refs[0]
    q = refs[1]
    keys = refs[2 : 2 + n_keys]
    vals = refs[2 + n_keys : 2 + 2 * n_keys]
    w = refs[2 + 2 * n_keys]
    outs = refs[3 + 2 * n_keys : 3 + 2 * n_keys + n_out]
    acc, top, ctx = refs[-3:]
    row_block = pl.program_id(0) + first_block
    acc[...] = jnp.zeros_like(acc)
    top[...] = jnp.full_like(top, -1e20)
    chunk = 0
    for kr, vr in zip(keys, vals):
        for lo in range(0, kr.shape[0], BLOCK):

            @pl.when(flags[row_block, chunk] > 0)
            def _(kr=kr, vr=vr, lo=lo):
                for h in range(heads):
                    c = h * PAD
                    s = lax.dot_general(
                        q[:, c : c + PAD],
                        kr[lo : lo + BLOCK, c : c + PAD],
                        (((1,), (1,)), ((), ())),
                        preferred_element_type=F32,
                    )
                    old = top[:, c : c + PAD]
                    new = jnp.maximum(old, jnp.max(s, axis=1, keepdims=True))
                    shrink = jnp.exp2(old - new)
                    wide_new = jnp.concatenate([new] * (BLOCK // PAD), axis=1)
                    p = jnp.exp2(s - wide_new).astype(BF)
                    acc[:, c : c + PAD] = acc[:, c : c + PAD] * shrink + jnp.dot(
                        p, vr[lo : lo + BLOCK, c : c + PAD], preferred_element_type=F32
                    )
                    top[:, c : c + PAD] = new

            chunk += 1
    for h in range(heads):
        c = h * PAD
        a = acc[:, c : c + PAD]
        ctx[:, c : c + PAD] = (a / a[:, HD : HD + 1]).astype(BF)
    terms = jnp.dot(ctx[...], w[...], preferred_element_type=F32)
    width = terms.shape[1] // n_out
    for k in range(n_out):
        outs[k][...] = terms[:, k * width : (k + 1) * width].astype(BF)


def attend(flags, q, keys, vals, w, n_out, first_block):
    rows, wide = q.shape
    heads = wide // PAD
    full = w.shape[1]
    n_keys = len(keys)
    kv = lambda a: pl.BlockSpec(a.shape, lambda i, f: (0, 0), pipeline_mode=pl.Buffered(1))
    key_count = sum(k.shape[0] for k in keys)
    return pl.pallas_call(
        functools.partial(attend_body, n_keys, heads, n_out, first_block),
        grid_spec=pltpu.PrefetchScalarGridSpec(
            num_scalar_prefetch=1,
            grid=(rows // BLOCK,),
            in_specs=[pl.BlockSpec((BLOCK, wide), lambda i, f: (i, 0))]
            + [kv(a) for a in keys]
            + [kv(a) for a in vals]
            + [kv(w)],
            out_specs=[
                pl.BlockSpec((BLOCK, full // n_out), lambda i, f: (i, 0)) for _ in range(n_out)
            ],
            scratch_shapes=[
                pltpu.VMEM((BLOCK, wide), F32),
                pltpu.VMEM((BLOCK, wide), F32),
                pltpu.VMEM((BLOCK, wide), BF),
            ],
        ),
        out_shape=[jax.ShapeDtypeStruct((rows, full // n_out), BF) for _ in range(n_out)],
        compiler_params=params(24),
        cost_estimate=pl.CostEstimate(
            flops=4 * rows * key_count * wide + 2 * rows * wide * full,
            bytes_accessed=2 * (rows * wide + 2 * key_count * wide + wide * full + rows * full),
            transcendentals=rows * key_count * heads,
        ),
        name="attend",
    )(flags, q, *keys, *vals, w)


def merge_body(n_out, hidden, center, inv, gain, w, *refs):
    outs = refs[:n_out]
    scaled = refs[n_out]
    values = (hidden[...].astype(F32) - center[...]) * inv[...] * gain[...]
    count = values.shape[0] // 4
    pieces = [(lo, min(PAD, values.shape[1] - lo)) for lo in range(0, values.shape[1], PAD)]
    for t, (lo, size) in enumerate(pieces):
        scaled[t, :, :size] = values[:, lo : lo + size]
    acc = None
    for j in range(4):
        rows = jnp.concatenate(
            [
                scaled.at[t][pl.ds(j, count, stride=4), :][:, :size]
                for t, (_, size) in enumerate(pieces)
            ],
            axis=1,
        ).astype(BF)
        part = jnp.dot(rows, w[j], preferred_element_type=F32)
        acc = part if acc is None else acc + part
    width = acc.shape[1] // n_out
    for k in range(n_out):
        outs[k][...] = acc[:, k * width : (k + 1) * width].astype(BF)


def merge(hidden, center, inv, gain, w, n_out):
    rows, width = hidden.shape
    full = w.shape[2]
    return pl.pallas_call(
        functools.partial(merge_body, n_out),
        out_shape=[jax.ShapeDtypeStruct((rows // 4, full // n_out), BF) for _ in range(n_out)],
        scratch_shapes=[pltpu.VMEM((pl.cdiv(width, PAD), rows, PAD), F32)],
        compiler_params=params(24),
        cost_estimate=pl.CostEstimate(
            flops=2 * rows * width * full,
            bytes_accessed=2 * (rows * width + 4 * width * full + rows * full // 4),
            transcendentals=0,
        ),
        name="merge",
    )(hidden, center, inv, gain, w)


def place_body(n_in, *refs):
    merged = sum(r[...].astype(F32) for r in refs[:n_in]).astype(BF)
    dispatch, out = refs[n_in:]
    out[...] = jnp.dot(dispatch[...], merged, preferred_element_type=F32).astype(BF)


def place(terms, dispatch):
    return pl.pallas_call(
        functools.partial(place_body, len(terms)),
        out_shape=jax.ShapeDtypeStruct((dispatch.shape[0], terms[0].shape[1]), BF),
        compiler_params=params(16),
        name="place",
    )(*terms, dispatch)


def segment_codes(ids):
    lane = jnp.arange(PAD, dtype=jnp.int32)[None, :] - HD
    used = (lane >= 0) & (lane < 2 * CODE_BITS)
    bit = (ids[:, None] >> jnp.clip(lane // 2, 0, CODE_BITS - 1)) & 1
    hit = bit == (lane & 1)
    return (
        jnp.where(used & ~hit, -FAR, 0.0).astype(BF),
        jnp.where(used & hit, 1.0, 0.0).astype(BF),
    )


def spread_square(halves):
    low, high = halves
    a0 = hop(low, "tp", 1)
    b1 = hop(high, "tp", 2)
    a1 = hop(high, "tp", 1)
    b0 = hop(low, "tp", 2)
    c = hop(a0, "tp", 2)
    d = hop(b1, "tp", 1)
    return [(low, a0, b0, c), (high, a1, b1, d)]


def shards(tokens, segment, ln_gain, w_qkv, w_out, merge_gain, w_merge, owner):
    row_count, local_width = tokens.shape
    tp_count = lax.axis_size("tp")
    grp_count = lax.axis_size("grp")
    full_width = local_width * tp_count
    heads = local_width // HD
    half = row_count // 2
    square = tp_count == 4
    me = lax.axis_index("tp")
    partner = grp_count // 2

    halves = [tokens[:half], tokens[half:]]
    far_segment = hop(segment, "grp", partner)
    far_halves = [hop(t, "grp", partner) for t in halves]
    if square:
        own_parts = spread_square(halves)
        far_parts = spread_square(far_halves)
        order = [me ^ k for k in range(4)]
    else:
        own_parts = [(lax.all_gather(t, "tp", axis=1, tiled=True),) for t in halves]
        far_parts = [(lax.all_gather(t, "tp", axis=1, tiled=True),) for t in far_halves]
        order = None

    def slices(x, axis):
        if order is None:
            return x
        return jnp.concatenate(
            [lax.dynamic_slice_in_dim(x, o * local_width, local_width, axis) for o in order],
            axis=axis,
        )

    gain = slices(ln_gain, 0)[None, :]
    w_in = slices(w_qkv, 1)
    w_in = jnp.pad(
        w_in.reshape(3, full_width, heads, HD), ((0, 0), (0, 0), (0, 0), (0, PAD - HD))
    ).reshape(3, full_width, heads * PAD)
    w_back = jnp.pad(
        slices(w_out, 1).reshape(heads, HD, full_width), ((0, 0), (0, PAD - HD), (0, 0))
    ).reshape(heads * PAD, full_width)
    w_blocks = slices(w_merge, 2)
    gain_part = lax.dynamic_slice_in_dim(merge_gain, me * local_width, local_width, 0)[None, :]

    qcode, kcode = segment_codes(segment)
    _, far_kcode = segment_codes(far_segment)
    low_ids, high_ids = segment[::BLOCK], segment[BLOCK - 1 :: BLOCK]
    key_low = jnp.concatenate([low_ids, far_segment[::BLOCK]])
    key_high = jnp.concatenate([high_ids, far_segment[BLOCK - 1 :: BLOCK]])
    flags = (
        (key_low[None, :] <= high_ids[:, None]) & (key_high[None, :] >= low_ids[:, None])
    ).astype(jnp.int32)

    merged_count = row_count // 4
    cap_slots = max(2, merged_count // grp_count * 2)
    targets = owner[:, 0]
    onehot = (targets[:, None] == jnp.arange(grp_count, dtype=jnp.int32)[None, :]).astype(F32)
    lower_mask = (
        jnp.arange(merged_count)[:, None] > jnp.arange(merged_count)[None, :]
    ).astype(F32)
    earlier = jnp.dot(lower_mask, onehot, precision=lax.Precision.HIGHEST)
    slot_index = jnp.sum(earlier * onehot, axis=1).astype(jnp.int32)
    slot_place = targets * cap_slots + slot_index
    dispatch = (
        jnp.arange(grp_count * cap_slots, dtype=jnp.int32)[:, None] == slot_place[None, :]
    ).astype(BF)

    own = [project(p, gain, w_in, qcode, kcode, 3, i * half) for i, p in enumerate(own_parts)]
    far = [
        project(p, gain, w_in, far_kcode, far_kcode, 2, i * half)
        for i, p in enumerate(far_parts)
    ]
    keys = [o[1] for o in own] + [f[0] for f in far]
    vals = [o[2] for o in own] + [f[1] for f in far]
    n_out = 4 if square else 1
    terms = [
        attend(flags, own[i][0], keys, vals, w_back, n_out, i * (half // BLOCK)) for i in range(2)
    ]

    if square:
        sums = []
        for i, (near, next_) in enumerate(((1, 2), (2, 1))):
            mine, other = terms[i][0], terms[i][next_]
            corner = hop(terms[i][3], "tp", near)
            side = hop(terms[i][near], "tp", near)
            passed = (other.astype(F32) + corner.astype(F32)).astype(BF)
            last = hop(passed, "tp", next_)
            sums.append(mine.astype(F32) + side.astype(F32) + last.astype(F32))
        summed = jnp.concatenate(sums, axis=0)
    else:
        summed = lax.psum_scatter(
            jnp.concatenate([t[0] for t in terms], axis=0),
            "tp",
            scatter_dimension=1,
            tiled=True,
        ).astype(F32)
    hidden_out = (tokens.astype(F32) + summed).astype(BF)

    local_rows = hidden_out.astype(F32)
    local_center = jnp.mean(local_rows, axis=1)
    local_spread = jnp.mean((local_rows - local_center[:, None]) ** 2, axis=1)
    stats = jnp.stack([local_center, local_spread])
    if square:
        all_stats = jnp.stack([stats] + [hop(stats, "tp", k) for k in (1, 2, 3)])
    else:
        all_stats = lax.all_gather(stats, "tp")
    center = jnp.mean(all_stats[:, 0], axis=0)
    spread = jnp.mean(all_stats[:, 1] + (all_stats[:, 0] - center[None]) ** 2, axis=0)
    inv = lax.rsqrt(spread + EPS)

    merge_terms = merge(
        hidden_out, center[:, None], inv[:, None], gain_part, w_blocks, n_out
    )
    if square:
        received = [merge_terms[0]] + [hop(merge_terms[k], "tp", k) for k in (1, 2, 3)]
    else:
        received = [lax.psum_scatter(merge_terms[0], "tp", scatter_dimension=1, tiled=True)]
    outgoing = place(received, dispatch).reshape(grp_count, cap_slots, local_width)
    routed = lax.all_to_all(outgoing, "grp", split_axis=0, concat_axis=0, tiled=True)
    return (hidden_out, routed[None])


def solution(mesh):
    return jax.shard_map(
        shards,
        mesh=mesh,
        in_specs=(
            P("grp", "tp"),
            P("grp"),
            P(),
            P(None, None, "tp"),
            P("tp", None),
            P(),
            P(None, "tp", None),
            P("grp", None),
        ),
        out_specs=(P("grp", "tp"), P("grp", None, None, "tp")),
        check_vma=False,
    )
```

time: 320 us -> 197 us (0.62)
  waiting for transfers between devices: 206 us -> 60 us
  Pallas kernels: 0 us -> 37.1 us
  starting transfers between devices: 3.08 us -> 35.4 us
  local copies, waits for them, and re-layouts: 27.8 us -> 59.5 us
  matrix products: 31.1 us -> 0.19 us
  blocking collectives: 17.2 us -> 0 us
  other arithmetic: 18.6 us -> 2.38 us
  between operations: 13.9 us -> 1.07 us
    all_gather x2 -> x0, waiting for transfers between devices: 83.2 us -> none  [the longest x1 44.3 us: shards(): gathered = lax.all_gather(tokens, 'tp', axis=1, tiled=True)]
    reduce_scatter x1 -> x0, waiting for transfers between devices: 39.7 us -> none  [shards(): lax.psum_scatter(out_terms.astype(jnp.bfloat16), 'tp', scatter_dimension=...]
    pallas_call x0 -> x8, Pallas kernels: none -> 37.1 us  [the longest x2 19.7 us: attend(): pl.pallas_call(functools.partial(attend_body, n_keys, heads, n_out, first...]
    dot_general x20 -> x0, matrix products: 30.9 us -> none  [the longest x8 10.3 us: one_block(): jnp.dot(query_rows[:, low_col:low_col + HD], key_rows[:, low_col:low_col...]
    ppermute x2 -> x27, starting transfers between devices: 2.92 us -> 31.9 us  [hop(): lax.ppermute(x, axis, [(i, i ^ distance) for i in range(lax.axis_size(axi...]
    unnamed x5 -> x0, waiting for transfers between devices: 26.1 us -> none
    all_to_all x1 -> x0, blocking collectives: 17.2 us -> none  [shards(): lax.all_to_all(outgoing, 'grp', split_axis=0, concat_axis=0, tiled=True)]
    concatenate x0 -> x4, local copies, waits for them, and re-layouts: none -> 12.5 us  [slices(): jnp.concatenate([lax.dynamic_slice_in_dim(x, o * local_width, local_width...]
  transfers between devices with their start and end apart: 6 -> 28, of which waited for: 5 -> 11; matrix products, arithmetic and copies ran while one was open for 2% -> 25% of each run, Pallas kernels for 0% -> 10%
where the time goes in v1:
time: 197 us; the launch traced here: 196 us
  waiting for transfers between devices  60 us (30%)
  local copies, waits for them, and re-layouts  59.5 us (30%)
  Pallas kernels  37.1 us (19%)
  starting transfers between devices  35.4 us (18%)
  other arithmetic  2.38 us (1%)
    ppermute x27, waiting for transfers between devices, hop(): lax.ppermute(x, axis, [(i, i ^ distance) for i in range(lax.axis_size(axi...  48.6 us
    ppermute x27, starting transfers between devices, hop(): lax.ppermute(x, axis, [(i, i ^ distance) for i in range(lax.axis_size(axi...  31.9 us
    pallas_call x2, Pallas kernels, attend(): pl.pallas_call(functools.partial(attend_body, n_keys, heads, n_out, first...  19.7 us
    pallas_call x4, Pallas kernels, project(): pl.pallas_call(body, grid=(steps,), in_specs=[pl.BlockSpec((block, width)...  14.3 us
    concatenate x4, local copies, waits for them, and re-layouts, slices(): jnp.concatenate([lax.dynamic_slice_in_dim(x, o * local_width, local_width...  12.5 us
    all_to_all x1, waiting for transfers between devices, shards(): lax.all_to_all(outgoing, 'grp', split_axis=0, concat_axis=0, tiled=True)  11.3 us
    unnamed x39, local copies, waits for them, and re-layouts  11.2 us
    dynamic_slice x4, local copies, waits for them, and re-layouts, slices(): lax.dynamic_slice_in_dim(x, o * local_width, local_width, axis)  10.5 us
  transfers between devices with their start and end apart: 28, of which 11 were waited for; matrix products, arithmetic and copies ran while one was open for 25% of the time, Pallas kernels for 10%

profile of v1, /device:TPU:0, one launch (start us, length us, event | category | flops | bytes accessed | tf_op | source)
XLA Modules:
  0.0 195.5 jit_solution(12578735150415168503)
XLA Ops:
  0.6 1.4 copy.24
  2.2 0.9 copy-done.7
  3.1 2.9 %collective-permute-start.4 = (bf16[512,320]{1,0:T(8,128)(2,1)S(1)}, bf16[512,320]{1,0:T(8,128)(2,1)S(1)}, u32[]{:S(2)}, u32[]{:S(2)}) collective-permute-start(bf16[512,320]{1,0:T(8,128)(2,1)S(1)} %get-tuple-element.67.refs_0_), channel_id=1, source_target_pairs={{0,1},{1,0},{2,3},{3,2},{4,5},{5,4},{6,7},{7,6},{8,9},{9,8},{10,11... | collective-permute-start | bytes 983048 | tf_op jit(solution)/shard_map/ppermute | solution.py:22
  6.0 1.5 collective-permute-start.5
  7.5 2.6 %collective-permute-start.11 = (bf16[512,320]{1,0:T(8,128)(2,1)S(1)}, bf16[512,320]{1,0:T(8,128)(2,1)S(1)}, u32[]{:S(2)}, u32[]{:S(2)}) collective-permute-start(bf16[512,320]{1,0:T(8,128)(2,1)S(1)} %get-tuple-element.67.refs_0_), channel_id=1, source_target_pairs={{0,16},{4,20},{8,24},{12,28},{16,0},{20,4},{24,8},{28,12},{1,17},{... | collective-permute-start | bytes 983048 | tf_op jit(solution)/shard_map/ppermute | solution.py:22
  10.5 2.6 %collective-permute-start.7 = (bf16[512,320]{1,0:T(8,128)(2,1)S(1)}, bf16[512,320]{1,0:T(8,128)(2,1)S(1)}, u32[]{:S(2)}, u32[]{:S(2)}) collective-permute-start(bf16[512,320]{1,0:T(8,128)(2,1)S(1)} %get-tuple-element.66.refs_0_), channel_id=1, source_target_pairs={{0,16},{4,20},{8,24},{12,28},{16,0},{20,4},{24,8},{28,12},{1,17},{... | collective-permute-start | bytes 983048 | tf_op jit(solution)/shard_map/ppermute | solution.py:22
  13.2 4.9 %constant_dynamic-slice_fusion.8 = (bf16[3,320,320]{1,2,0:T(8,128)(2,1)S(1)}, bf16[3,320,320]{1,2,0:T(8,128)(2,1)S(1)}, bf16[3,320,320]{1,2,0:T(8,128)(2,1)}, bf16[3,320,320]{1,2,0:T(8,128)(2,1)}) fusion(bf16[3,1280,320]{1,2,0:T(8,128)(2,1)} %param.11, s32[]{:T(128)S(6)} %select_n.51, s32[]{:T(128)S(6)} %select_n.49, s32[]{:T(128)S(6)} %select_n.48, ...), kind=kLoop, calls=%fused_computation.40 | loop fusion | bytes 4915216 | tf_op jit(solution)/shard_map/dynamic_slice | solution.py:285
  18.0 1.4 constant_dynamic-slice_fusion.4
  19.7 5.3 %concatenate.24 = bf16[3,1280,320]{1,2,0:T(8,128)(2,1)} concatenate(bf16[3,320,320]{1,2,0:T(8,128)(2,1)} %get-tuple-element.60, bf16[3,320,320]{1,2,0:T(8,128)(2,1)S(1)} %get-tuple-element.59, bf16[3,320,320]{1,2,0:T(8,128)(2,1)} %get-tuple-element.61, bf16[3,320,320]{1,2,0:T(8,128)(2,1)S(1)} %get-tuple-element.58), dimensions={1} | concatenate | bytes 4915200 | tf_op jit(solution)/shard_map/concatenate | solution.py:284
  24.9 7.6 %copy.26 = bf16[3,1280,4,80]{3,2,1,0:T(4,128)(2,1)} copy(bf16[3,1280,4,80]{1,3,2,0:T(8,128)(2,1)} %bitcast.28) | data formatting | bytes 4915200 | tf_op jit(solution)/shard_map/reshape | solution.py:292
  32.5 5.6 %pad.8 = bf16[3,1280,4,128]{3,2,1,0:T(4,128)(2,1)} pad(bf16[3,1280,4,80]{3,2,1,0:T(4,128)(2,1)} %copy.26, bf16[]{:T(256)} %constant.48.clone.1), padding=0_0x0_0x0_0x0_48 | pad | bytes 6389762 | tf_op jit(solution)/shard_map/jit(_pad)/pad | solution.py:291
  38.1 7.5 %reshape.136.refs_5_ = bf16[3,1280,512]{2,1,0:T(8,128)(2,1)} reshape(bf16[3,1280,4,128]{3,2,1,0:T(4,128)(2,1)} %pad.8) | data formatting | bytes 7864320 | tf_op jit(solution)/shard_map/reshape | solution.py:293
  45.7 1.3 concatenate.25
  46.9 1.2 pad.9
  48.2 0.6 collective-permute-start.1
  48.9 0.7 select_convert_fusion.1
  49.7 0.6 collective-permute-start.2
  50.3 1.5 collective-permute-start.6
  51.8 0.5 collective-permute-start.8
  52.3 1.5 collective-permute-start.13
  53.9 6.5 %collective-permute-done.1.refs_1_ = bf16[512,320]{1,0:T(8,128)(2,1)} collective-permute-done((bf16[512,320]{1,0:T(8,128)(2,1)S(1)}, bf16[512,320]{1,0:T(8,128)(2,1)}, u32[]{:S(2)}, u32[]{:S(2)}) %collective-permute-start.1) | collective-permute-done | bytes 327712 | tf_op jit(solution)/shard_map/ppermute | solution.py:22
  61.0 0.8 collective-permute-done.2.refs_2_
  61.8 0.7 collective-permute-start.9
  62.5 6.2 %collective-permute-done.6.refs_3_ = bf16[512,320]{1,0:T(8,128)(2,1)S(1)} collective-permute-done((bf16[512,320]{1,0:T(8,128)(2,1)}, bf16[512,320]{1,0:T(8,128)(2,1)S(1)}, u32[]{:S(2)}, u32[]{:S(2)}) %collective-permute-start.6) | collective-permute-done | bytes 327712 | tf_op jit(solution)/shard_map/ppermute | solution.py:22
  69.3 7.9 %collective-permute-done.8.refs_1_ = bf16[512,320]{1,0:T(8,128)(2,1)S(1)} collective-permute-done((bf16[512,320]{1,0:T(8,128)(2,1)S(1)}, bf16[512,320]{1,0:T(8,128)(2,1)S(1)}, u32[]{:S(2)}, u32[]{:S(2)}) %collective-permute-start.8) | collective-permute-done | bytes 327712 | tf_op jit(solution)/shard_map/ppermute | solution.py:22
  77.7 0.5 collective-permute-start.14
  78.2 2.1 %copy-done = bf16[3,1280,512]{2,1,0:T(8,128)(2,1)S(1)} copy-done((bf16[3,1280,512]{2,1,0:T(8,128)(2,1)S(1)}, bf16[3,1280,512]{2,1,0:T(8,128)(2,1)}, u32[]{:S(2)}) %copy-start) | copy-done | bytes 3932184
  80.3 4.5 %project.5 = (bf16[512,512]{1,0:T(8,128)(2,1)S(1)}, bf16[512,512]{1,0:T(8,128)(2,1)S(1)}, bf16[512,512]{1,0:T(8,128)(2,1)S(1)}) custom-call(bf16[512,320]{1,0:T(8,128)(2,1)S(1)} %get-tuple-element.67.refs_0_, bf16[512,320]{1,0:T(8,128)(2,1)S(1)} %collective-permute-done.4.refs_1_, bf16[512,320]{1,0:T(8,128)(2,1)} %collective-permute-done.5.refs_2_, ...), custom_call_target="tpu_custom_call" | custom-call | flops 2013265920 | bytes 6815744 | tf_op jit(solution)/shard_map/project/pallas_call | solution.py:75
  84.8 4.4 %project.4 = (bf16[512,512]{1,0:T(8,128)(2,1)S(1)}, bf16[512,512]{1,0:T(8,128)(2,1)S(1)}, bf16[512,512]{1,0:T(8,128)(2,1)S(1)}) custom-call(bf16[512,320]{1,0:T(8,128)(2,1)S(1)} %get-tuple-element.66.refs_0_, bf16[512,320]{1,0:T(8,128)(2,1)} %collective-permute-done.1.refs_1_, bf16[512,320]{1,0:T(8,128)(2,1)S(1)} %collective-permute-done.2.refs_2_, ...), custom_call_target="tpu_custom_call" | custom-call | flops 2013265920 | bytes 6815744 | tf_op jit(solution)/shard_map/project/pallas_call | solution.py:75
  89.2 3.4 %collective-permute-done.10.refs_3_ = bf16[512,320]{1,0:T(8,128)(2,1)S(1)} collective-permute-done((bf16[512,320]{1,0:T(8,128)(2,1)S(1)}, bf16[512,320]{1,0:T(8,128)(2,1)S(1)}, u32[]{:S(2)}, u32[]{:S(2)}) %collective-permute-start.10) | collective-permute-done | bytes 327712 | tf_op jit(solution)/shard_map/ppermute | solution.py:22
  92.7 2.7 %project.6 = (bf16[512,512]{1,0:T(8,128)(2,1)S(1)}, bf16[512,512]{1,0:T(8,128)(2,1)S(1)}) custom-call(bf16[512,320]{1,0:T(8,128)(2,1)S(1)} %collective-permute-done.7.refs_0_, bf16[512,320]{1,0:T(8,128)(2,1)S(1)} %collective-permute-done.8.refs_1_, bf16[512,320]{1,0:T(8,128)(2,1)S(1)} %collective-permute-done.9.refs_2_, ...), custom_call_target="tpu_custom_call" | custom-call | flops 1342177280 | bytes 6291456 | tf_op jit(solution)/shard_map/project/pallas_call | solution.py:75
  95.4 2.7 %project.7 = (bf16[512,512]{1,0:T(8,128)(2,1)S(1)}, bf16[512,512]{1,0:T(8,128)(2,1)S(1)}) custom-call(bf16[512,320]{1,0:T(8,128)(2,1)S(1)} %collective-permute-done.11.refs_0_, bf16[512,320]{1,0:T(8,128)(2,1)S(1)} %collective-permute-done.12.refs_1_, bf16[512,320]{1,0:T(8,128)(2,1)S(1)} %collective-permute-done.13.refs_2_, ...), custom_call_target="tpu_custom_call" | custom-call | flops 1342177280 | bytes 6291456 | tf_op jit(solution)/shard_map/project/pallas_call | solution.py:75
  98.2 10.8 %attend.3 = (bf16[512,320]{1,0:T(8,128)(2,1)S(1)}, bf16[512,320]{1,0:T(8,128)(2,1)S(1)}, bf16[512,320]{1,0:T(8,128)(2,1)S(1)}, bf16[512,320]{1,0:T(8,128)(2,1)S(1)}) custom-call(s32[4,8]{1,0:T(4,128)S(1)} %and_convert_fusion.refs_0_, bf16[512,512]{1,0:T(8,128)(2,1)S(1)} %get-tuple-element.37.refs_1_, bf16[512,512]{1,0:T(8,128)(2,1)S(1)} %get-tuple-element.25.refs_2_, ...), custom_call_target="tpu_custom_call" | custom-call | flops 2818572288 | bytes 7340032 | tf_op jit(solution)/shard_map/attend/pallas_call | solution.py:151
  108.9 0.6 collective-permute-start.19
  109.5 9.0 %attend.2 = (bf16[512,320]{1,0:T(8,128)(2,1)S(1)}, bf16[512,320]{1,0:T(8,128)(2,1)S(1)}, bf16[512,320]{1,0:T(8,128)(2,1)S(1)}, bf16[512,320]{1,0:T(8,128)(2,1)S(1)}) custom-call(s32[4,8]{1,0:T(4,128)S(1)} %and_convert_fusion.refs_0_, bf16[512,512]{1,0:T(8,128)(2,1)S(1)} %get-tuple-element.24.refs_1_, bf16[512,512]{1,0:T(8,128)(2,1)S(1)} %get-tuple-element.25.refs_2_, ...), custom_call_target="tpu_custom_call" | custom-call | flops 2818572288 | bytes 7340032 | tf_op jit(solution)/shard_map/attend/pallas_call | solution.py:151
  118.5 1.6 collective-permute-start.16
  120.2 1.6 collective-permute-start.18
  122.5 1.6 collective-permute-start.20
  124.0 6.6 %collective-permute-done.16 = bf16[512,320]{1,0:T(8,128)(2,1)S(1)} collective-permute-done((bf16[512,320]{1,0:T(8,128)(2,1)S(1)}, bf16[512,320]{1,0:T(8,128)(2,1)S(1)}, u32[]{:S(2)}, u32[]{:S(2)}) %collective-permute-start.16) | collective-permute-done | bytes 327712 | tf_op jit(solution)/shard_map/ppermute | solution.py:22
  130.7 1.6 collective-permute-start.17
  132.3 11.1 %collective-permute-done.20 = bf16[512,320]{1,0:T(8,128)(2,1)S(1)} collective-permute-done((bf16[512,320]{1,0:T(8,128)(2,1)S(1)}, bf16[512,320]{1,0:T(8,128)(2,1)S(1)}, u32[]{:S(2)}, u32[]{:S(2)}) %collective-permute-start.20) | collective-permute-done | bytes 327712 | tf_op jit(solution)/shard_map/ppermute | solution.py:22
  143.7 0.8 copy-done.8
  145.3 0.9 copy-done.2
  146.2 2.5 %collective-permute-start.23 = (f32[2,1024]{1,0:T(2,128)S(1)}, f32[2,1024]{1,0:T(2,128)S(1)}, u32[]{:S(2)}, u32[]{:S(2)}) collective-permute-start(f32[2,1024]{1,0:T(2,128)S(1)} %get-tuple-element.69), channel_id=1, source_target_pairs={{0,3},{1,2},{2,1},{3,0},{4,7},{5,6},{6,5},{7,4},{8,11},{9,10},{10,... | collective-permute-start | bytes 24584 | tf_op jit(solution)/shard_map/ppermute | solution.py:22
  149.2 0.5 collective-permute-start.21
  149.8 4.2 %constant_dynamic-slice_fusion = (bf16[4,320,320]{2,1,0:T(8,128)(2,1)}, bf16[4,320,320]{2,1,0:T(8,128)(2,1)}, bf16[4,320,320]{2,1,0:T(8,128)(2,1)}, bf16[4,320,320]{2,1,0:T(8,128)(2,1)}) fusion(bf16[4,320,1280]{2,1,0:T(8,128)(2,1)S(1)} %copy-done.9, s32[]{:T(128)S(6)} %select_n.51, s32[]{:T(128)S(6)} %select_n.49, s32[]{:T(128)S(6)} %select_n.48, ...), kind=kLoop, calls=%fused_computation.32 | loop fusion | bytes 6553616 | tf_op jit(solution)/shard_map/dynamic_slice | solution.py:285
  154.0 0.8 dynamic_slice.63
  154.8 5.9 %concatenate.27.w = bf16[4,320,1280]{2,1,0:T(8,128)(2,1)S(1)} concatenate(bf16[4,320,320]{2,1,0:T(8,128)(2,1)} %get-tuple-element.56, bf16[4,320,320]{2,1,0:T(8,128)(2,1)} %get-tuple-element.55, bf16[4,320,320]{2,1,0:T(8,128)(2,1)} %get-tuple-element.57, bf16[4,320,320]{2,1,0:T(8,128)(2,1)} %get-tuple-element.54), dimensions={2} | concatenate | bytes 6553600 | tf_op jit(solution)/shard_map/concatenate | solution.py:284
  160.9 1.0 copy.31.center
  161.9 1.0 copy.32.inv
  162.9 1.1 copy-done.3
  164.1 1.0 copy-done.5
  165.1 1.0 copy-done.6
  166.2 1.9 merge.1
  168.1 1.5 collective-permute-start.24
  169.6 1.5 collective-permute-start.25
  171.7 2.1 %collective-permute-done.24.refs_1_ = bf16[256,320]{1,0:T(8,128)(2,1)S(1)} collective-permute-done((bf16[256,320]{1,0:T(8,128)(2,1)S(1)}, bf16[256,320]{1,0:T(8,128)(2,1)S(1)}, u32[]{:S(2)}, u32[]{:S(2)}) %collective-permute-start.24) | collective-permute-done | bytes 163872 | tf_op jit(solution)/shard_map/ppermute | solution.py:22
  173.8 2.7 %collective-permute-done.25.refs_2_ = bf16[256,320]{1,0:T(8,128)(2,1)S(1)} collective-permute-done((bf16[256,320]{1,0:T(8,128)(2,1)S(1)}, bf16[256,320]{1,0:T(8,128)(2,1)S(1)}, u32[]{:S(2)}, u32[]{:S(2)}) %collective-permute-start.25) | collective-permute-done | bytes 163872 | tf_op jit(solution)/shard_map/ppermute | solution.py:22
  176.5 1.2 collective-permute-done.26.refs_3_
  177.7 1.1 place.1
  178.9 3.5 %all-to-all-start = ((bf16[8,64,320]{2,1,0:T(8,128)(2,1)}), bf16[8,64,320]{2,1,0:T(8,128)(2,1)S(1)}, u32[]{:S(2)}, u32[]{:S(2)}) async-start(bf16[8,64,320]{2,1,0:T(8,128)(2,1)} %bitcast.13), calls=%async_computation | async-start | bytes 786432 | tf_op jit(solution)/shard_map/all_to_all | solution.py:374
  182.3 1.1 copy.33
  183.4 11.3 %all-to-all-done = bf16[8,64,320]{2,1,0:T(8,128)(2,1)S(1)} async-done(((bf16[8,64,320]{2,1,0:T(8,128)(2,1)}), bf16[8,64,320]{2,1,0:T(8,128)(2,1)S(1)}, u32[]{:S(2)}, u32[]{:S(2)}) %all-to-all-start) | async-done | bytes 327712 | tf_op jit(solution)/shard_map/all_to_all | solution.py:374
  194.8 0.7 copy.35
  (87 shorter events, 6.0 us)
Async XLA Ops:
  0.6 9.5 %copy-start.16 = (s32[1024]{0:T(1024)S(1)}, s32[1024]{0:T(1024)}, u32[]{:S(2)}) copy-start(s32[1024]{0:T(1024)} %param.9) | copy-start | bytes 12292
  0.6 12.4 %copy-start.15 = (f32[1280]{0:T(1024)S(1)}, f32[1280]{0:T(1024)}, u32[]{:S(2)}) copy-start(f32[1280]{0:T(1024)} %param.10) | copy-start | bytes 15364
  2.1 1.0 copy-start.7
  3.1 46.6 %collective-permute-start.4 = (bf16[512,320]{1,0:T(8,128)(2,1)S(1)}, bf16[512,320]{1,0:T(8,128)(2,1)S(1)}, u32[]{:S(2)}, u32[]{:S(2)}) collective-permute-start(bf16[512,320]{1,0:T(8,128)(2,1)S(1)} %get-tuple-element.67.refs_0_), channel_id=1, source_target_pairs={{0,1},{1,0},{2,3},{3,2},{4,5},{5,4},{6,7},{7,6},{8,9},{9,8},{10,11... | collective-permute-start | bytes 983048 | tf_op jit(solution)/shard_map/ppermute | solution.py:22
  6.0 44.3 %collective-permute-start.5 = (bf16[512,320]{1,0:T(8,128)(2,1)S(1)}, bf16[512,320]{1,0:T(8,128)(2,1)}, u32[]{:S(2)}, u32[]{:S(2)}) collective-permute-start(bf16[512,320]{1,0:T(8,128)(2,1)S(1)} %get-tuple-element.67.refs_0_), channel_id=1, source_target_pairs={{0,2},{1,3},{2,0},{3,1},{4,6},{5,7},{6,4},{7,5},{8,10},{9,11},{10,... | collective-permute-start | bytes 983048 | tf_op jit(solution)/shard_map/ppermute | solution.py:22
  7.5 44.8 %collective-permute-start.11 = (bf16[512,320]{1,0:T(8,128)(2,1)S(1)}, bf16[512,320]{1,0:T(8,128)(2,1)S(1)}, u32[]{:S(2)}, u32[]{:S(2)}) collective-permute-start(bf16[512,320]{1,0:T(8,128)(2,1)S(1)} %get-tuple-element.67.refs_0_), channel_id=1, source_target_pairs={{0,16},{4,20},{8,24},{12,28},{16,0},{20,4},{24,8},{28,12},{1,17},{... | collective-permute-start | bytes 983048 | tf_op jit(solution)/shard_map/ppermute | solution.py:22
  10.1 38.1 %collective-permute-start = (s32[1024]{0:T(1024)S(1)}, s32[1024]{0:T(1024)S(1)}, u32[]{:S(2)}, u32[]{:S(2)}) collective-permute-start(s32[1024]{0:T(1024)S(1)} %copy-done.16), channel_id=1, source_target_pairs={{0,16},{4,20},{8,24},{12,28},{16,0},{20,4},{24,8},{28,12},{1,17},{... | collective-permute-start | bytes 12296 | tf_op jit(solution)/shard_map/ppermute | solution.py:22
  10.5 41.3 %collective-permute-start.7 = (bf16[512,320]{1,0:T(8,128)(2,1)S(1)}, bf16[512,320]{1,0:T(8,128)(2,1)S(1)}, u32[]{:S(2)}, u32[]{:S(2)}) collective-permute-start(bf16[512,320]{1,0:T(8,128)(2,1)S(1)} %get-tuple-element.66.refs_0_), channel_id=1, source_target_pairs={{0,16},{4,20},{8,24},{12,28},{16,0},{20,4},{24,8},{28,12},{1,17},{... | collective-permute-start | bytes 983048 | tf_op jit(solution)/shard_map/ppermute | solution.py:22
  13.2 4.9 %copy-start.10 = (bf16[320,1280]{1,0:T(8,128)(2,1)S(1)}, bf16[320,1280]{1,0:T(8,128)(2,1)}, u32[]{:S(2)}) copy-start(bf16[320,1280]{1,0:T(8,128)(2,1)} %param.12) | copy-start | bytes 2457604
  38.1 7.5 %copy-start.11 = (bf16[320,320]{1,0:T(8,128)(2,1)S(1)}, bf16[320,320]{1,0:T(8,128)(2,1)}, u32[]{:S(2)}) copy-start(bf16[320,320]{1,0:T(8,128)(2,1)} %get-tuple-element.62) | copy-start | bytes 614404
  38.1 7.5 %copy-start.12 = (bf16[320,320]{1,0:T(8,128)(2,1)S(1)}, bf16[320,320]{1,0:T(8,128)(2,1)}, u32[]{:S(2)}) copy-start(bf16[320,320]{1,0:T(8,128)(2,1)} %get-tuple-element.63) | copy-start | bytes 614404
  38.1 7.5 %copy-start.13 = (bf16[320,320]{1,0:T(8,128)(2,1)S(1)}, bf16[320,320]{1,0:T(8,128)(2,1)}, u32[]{:S(2)}) copy-start(bf16[320,320]{1,0:T(8,128)(2,1)} %get-tuple-element.64) | copy-start | bytes 614404
  38.1 7.5 %copy-start.14 = (bf16[320,320]{1,0:T(8,128)(2,1)S(1)}, bf16[320,320]{1,0:T(8,128)(2,1)}, u32[]{:S(2)}) copy-start(bf16[320,320]{1,0:T(8,128)(2,1)} %get-tuple-element.65) | copy-start | bytes 614404
  48.2 12.2 %collective-permute-start.1 = (bf16[512,320]{1,0:T(8,128)(2,1)S(1)}, bf16[512,320]{1,0:T(8,128)(2,1)}, u32[]{:S(2)}, u32[]{:S(2)}) collective-permute-start(bf16[512,320]{1,0:T(8,128)(2,1)S(1)} %get-tuple-element.66.refs_0_), channel_id=1, source_target_pairs={{0,1},{1,0},{2,3},{3,2},{4,5},{5,4},{6,7},{7,6},{8,9},{9,8},{10,11... | collective-permute-start | bytes 983048 | tf_op jit(solution)/shard_map/ppermute | solution.py:22
  49.7 12.1 %collective-permute-start.2 = (bf16[512,320]{1,0:T(8,128)(2,1)S(1)}, bf16[512,320]{1,0:T(8,128)(2,1)S(1)}, u32[]{:S(2)}, u32[]{:S(2)}) collective-permute-start(bf16[512,320]{1,0:T(8,128)(2,1)S(1)} %get-tuple-element.66.refs_0_), channel_id=1, source_target_pairs={{0,2},{1,3},{2,0},{3,1},{4,6},{5,7},{6,4},{7,5},{8,10},{9,11},{10,... | collective-permute-start | bytes 983048 | tf_op jit(solution)/shard_map/ppermute | solution.py:22
  50.3 18.4 %collective-permute-start.6 = (bf16[512,320]{1,0:T(8,128)(2,1)}, bf16[512,320]{1,0:T(8,128)(2,1)S(1)}, u32[]{:S(2)}, u32[]{:S(2)}) collective-permute-start(bf16[512,320]{1,0:T(8,128)(2,1)} %collective-permute-done.5.refs_2_), channel_id=1, source_target_pairs={{0,1},{1,0},{2,3},{3,2},{4,5},{5,4},{6,7},{7,6},{8,9},{9,8},{10,11... | collective-permute-start | bytes 983048 | tf_op jit(solution)/shard_map/ppermute | solution.py:22
  51.8 25.4 %collective-permute-start.8 = (bf16[512,320]{1,0:T(8,128)(2,1)S(1)}, bf16[512,320]{1,0:T(8,128)(2,1)S(1)}, u32[]{:S(2)}, u32[]{:S(2)}) collective-permute-start(bf16[512,320]{1,0:T(8,128)(2,1)S(1)} %collective-permute-done.7.refs_0_), channel_id=1, source_target_pairs={{0,1},{1,0},{2,3},{3,2},{4,5},{5,4},{6,7},{7,6},{8,9},{9,8},{10,11... | collective-permute-start | bytes 983048 | tf_op jit(solution)/shard_map/ppermute | solution.py:22
  52.3 25.3 %collective-permute-start.13 = (bf16[512,320]{1,0:T(8,128)(2,1)S(1)}, bf16[512,320]{1,0:T(8,128)(2,1)S(1)}, u32[]{:S(2)}, u32[]{:S(2)}) collective-permute-start(bf16[512,320]{1,0:T(8,128)(2,1)S(1)} %collective-permute-done.11.refs_0_), channel_id=1, source_target_pairs={{0,2},{1,3},{2,0},{3,1},{4,6},{5,7},{6,4},{7,5},{8,10},{9,11},{10,... | collective-permute-start | bytes 983048 | tf_op jit(solution)/shard_map/ppermute | solution.py:22
  60.4 24.4 %collective-permute-start.3 = (bf16[512,320]{1,0:T(8,128)(2,1)}, bf16[512,320]{1,0:T(8,128)(2,1)S(1)}, u32[]{:S(2)}, u32[]{:S(2)}) collective-permute-start(bf16[512,320]{1,0:T(8,128)(2,1)} %collective-permute-done.1.refs_1_), channel_id=1, source_target_pairs={{0,2},{1,3},{2,0},{3,1},{4,6},{5,7},{6,4},{7,5},{8,10},{9,11},{10,... | collective-permute-start | bytes 983048 | tf_op jit(solution)/shard_map/ppermute | solution.py:22
  61.8 27.4 %collective-permute-start.9 = (bf16[512,320]{1,0:T(8,128)(2,1)S(1)}, bf16[512,320]{1,0:T(8,128)(2,1)S(1)}, u32[]{:S(2)}, u32[]{:S(2)}) collective-permute-start(bf16[512,320]{1,0:T(8,128)(2,1)S(1)} %collective-permute-done.7.refs_0_), channel_id=1, source_target_pairs={{0,2},{1,3},{2,0},{3,1},{4,6},{5,7},{6,4},{7,5},{8,10},{9,11},{10,... | collective-permute-start | bytes 983048 | tf_op jit(solution)/shard_map/ppermute | solution.py:22
  68.7 26.7 %collective-permute-start.12 = (bf16[512,320]{1,0:T(8,128)(2,1)S(1)}, bf16[512,320]{1,0:T(8,128)(2,1)S(1)}, u32[]{:S(2)}, u32[]{:S(2)}) collective-permute-start(bf16[512,320]{1,0:T(8,128)(2,1)S(1)} %collective-permute-done.11.refs_0_), channel_id=1, source_target_pairs={{0,1},{1,0},{2,3},{3,2},{4,5},{5,4},{6,7},{7,6},{8,9},{9,8},{10,11... | collective-permute-start | bytes 983048 | tf_op jit(solution)/shard_map/ppermute | solution.py:22
  77.2 15.5 %collective-permute-start.10 = (bf16[512,320]{1,0:T(8,128)(2,1)S(1)}, bf16[512,320]{1,0:T(8,128)(2,1)S(1)}, u32[]{:S(2)}, u32[]{:S(2)}) collective-permute-start(bf16[512,320]{1,0:T(8,128)(2,1)S(1)} %collective-permute-done.8.refs_1_), channel_id=1, source_target_pairs={{0,2},{1,3},{2,0},{3,1},{4,6},{5,7},{6,4},{7,5},{8,10},{9,11},{10,... | collective-permute-start | bytes 983048 | tf_op jit(solution)/shard_map/ppermute | solution.py:22
  77.7 17.7 %collective-permute-start.14 = (bf16[512,320]{1,0:T(8,128)(2,1)S(1)}, bf16[512,320]{1,0:T(8,128)(2,1)S(1)}, u32[]{:S(2)}, u32[]{:S(2)}) collective-permute-start(bf16[512,320]{1,0:T(8,128)(2,1)S(1)} %collective-permute-done.13.refs_2_), channel_id=1, source_target_pairs={{0,1},{1,0},{2,3},{3,2},{4,5},{5,4},{6,7},{7,6},{8,9},{9,8},{10,11... | collective-permute-start | bytes 983048 | tf_op jit(solution)/shard_map/ppermute | solution.py:22
  78.2 2.1 %copy-start = (bf16[3,1280,512]{2,1,0:T(8,128)(2,1)S(1)}, bf16[3,1280,512]{2,1,0:T(8,128)(2,1)}, u32[]{:S(2)}) copy-start(bf16[3,1280,512]{2,1,0:T(8,128)(2,1)} %reshape.136.refs_5_) | copy-start | bytes 11796484
  80.3 4.5 %copy-start.1 = (bf16[3,1280,512]{2,1,0:T(8,128)(2,1)S(1)}, bf16[3,1280,512]{2,1,0:T(8,128)(2,1)}, u32[]{:S(2)}) copy-start(bf16[3,1280,512]{2,1,0:T(8,128)(2,1)} %reshape.136.refs_5_) | copy-start | bytes 11796484
  108.9 13.4 %collective-permute-start.19 = (bf16[512,320]{1,0:T(8,128)(2,1)S(1)}, bf16[512,320]{1,0:T(8,128)(2,1)S(1)}, u32[]{:S(2)}, u32[]{:S(2)}) collective-permute-start(bf16[512,320]{1,0:T(8,128)(2,1)S(1)} %get-tuple-element.41), channel_id=1, source_target_pairs={{0,2},{1,3},{2,0},{3,1},{4,6},{5,7},{6,4},{7,5},{8,10},{9,11},{10,... | collective-permute-start | bytes 983048 | tf_op jit(solution)/shard_map/ppermute | solution.py:22
  109.5 10.5 %copy-start.17 = (s32[256,1]{0,1:T(1,128)S(1)}, s32[256,1]{0,1:T(1,128)}, u32[]{:S(2)}) copy-start(s32[256,1]{0,1:T(1,128)} %param.15) | copy-start | bytes 3076
  118.5 12.1 %collective-permute-start.16 = (bf16[512,320]{1,0:T(8,128)(2,1)S(1)}, bf16[512,320]{1,0:T(8,128)(2,1)S(1)}, u32[]{:S(2)}, u32[]{:S(2)}) collective-permute-start(bf16[512,320]{1,0:T(8,128)(2,1)S(1)} %get-tuple-element.36), channel_id=1, source_target_pairs={{0,1},{1,0},{2,3},{3,2},{4,5},{5,4},{6,7},{7,6},{8,9},{9,8},{10,11... | collective-permute-start | bytes 983048 | tf_op jit(solution)/shard_map/ppermute | solution.py:22
  120.2 12.1 %collective-permute-start.18 = (bf16[512,320]{1,0:T(8,128)(2,1)S(1)}, bf16[512,320]{1,0:T(8,128)(2,1)S(1)}, u32[]{:S(2)}, u32[]{:S(2)}) collective-permute-start(bf16[512,320]{1,0:T(8,128)(2,1)S(1)} %get-tuple-element.39), channel_id=1, source_target_pairs={{0,2},{1,3},{2,0},{3,1},{4,6},{5,7},{6,4},{7,5},{8,10},{9,11},{10,... | collective-permute-start | bytes 983048 | tf_op jit(solution)/shard_map/ppermute | solution.py:22
  121.8 21.7 %collective-permute-start.15 = (bf16[512,320]{1,0:T(8,128)(2,1)S(1)}, bf16[512,320]{1,0:T(8,128)(2,1)S(1)}, u32[]{:S(2)}, u32[]{:S(2)}) collective-permute-start(bf16[512,320]{1,0:T(8,128)(2,1)S(1)} %get-tuple-element.34), channel_id=1, source_target_pairs={{0,1},{1,0},{2,3},{3,2},{4,5},{5,4},{6,7},{7,6},{8,9},{9,8},{10,11... | collective-permute-start | bytes 983048 | tf_op jit(solution)/shard_map/ppermute | solution.py:22
  122.5 20.9 %collective-permute-start.20 = (bf16[512,320]{1,0:T(8,128)(2,1)S(1)}, bf16[512,320]{1,0:T(8,128)(2,1)S(1)}, u32[]{:S(2)}, u32[]{:S(2)}) collective-permute-start(bf16[512,320]{1,0:T(8,128)(2,1)S(1)} %add_convert_fusion), channel_id=1, source_target_pairs={{0,1},{1,0},{2,3},{3,2},{4,5},{5,4},{6,7},{7,6},{8,9},{9,8},{10,11... | collective-permute-start | bytes 983048 | tf_op jit(solution)/shard_map/ppermute | solution.py:22
  130.7 12.9 %collective-permute-start.17 = (bf16[512,320]{1,0:T(8,128)(2,1)S(1)}, bf16[512,320]{1,0:T(8,128)(2,1)S(1)}, u32[]{:S(2)}, u32[]{:S(2)}) collective-permute-start(bf16[512,320]{1,0:T(8,128)(2,1)S(1)} %add_convert_fusion.1), channel_id=1, source_target_pairs={{0,2},{1,3},{2,0},{3,1},{4,6},{5,7},{6,4},{7,5},{8,10},{9,11},{10,... | collective-permute-start | bytes 983048 | tf_op jit(solution)/shard_map/ppermute | solution.py:22
  143.4 1.1 copy-start.8
  144.5 5.3 %copy-start.9 = (bf16[4,320,1280]{2,1,0:T(8,128)(2,1)S(1)}, bf16[4,320,1280]{2,1,0:T(8,128)(2,1)}, u32[]{:S(2)}) copy-start(bf16[4,320,1280]{2,1,0:T(8,128)(2,1)} %param.14) | copy-start | bytes 9830404
  145.3 0.9 copy-start.2
  146.2 14.5 %collective-permute-start.23 = (f32[2,1024]{1,0:T(2,128)S(1)}, f32[2,1024]{1,0:T(2,128)S(1)}, u32[]{:S(2)}, u32[]{:S(2)}) collective-permute-start(f32[2,1024]{1,0:T(2,128)S(1)} %get-tuple-element.69), channel_id=1, source_target_pairs={{0,3},{1,2},{2,1},{3,0},{4,7},{5,6},{6,5},{7,4},{8,11},{9,10},{10,... | collective-permute-start | bytes 24584 | tf_op jit(solution)/shard_map/ppermute | solution.py:22
  148.7 12.0 %collective-permute-start.22 = (f32[2,1024]{1,0:T(2,128)S(1)}, f32[2,1024]{1,0:T(2,128)S(1)}, u32[]{:S(2)}, u32[]{:S(2)}) collective-permute-start(f32[2,1024]{1,0:T(2,128)S(1)} %get-tuple-element.69), channel_id=1, source_target_pairs={{0,2},{1,3},{2,0},{3,1},{4,6},{5,7},{6,4},{7,5},{8,10},{9,11},{10,... | collective-permute-start | bytes 24584 | tf_op jit(solution)/shard_map/ppermute | solution.py:22
  149.2 11.5 %collective-permute-start.21 = (f32[2,1024]{1,0:T(2,128)S(1)}, f32[2,1024]{1,0:T(2,128)S(1)}, u32[]{:S(2)}, u32[]{:S(2)}) collective-permute-start(f32[2,1024]{1,0:T(2,128)S(1)} %get-tuple-element.69), channel_id=1, source_target_pairs={{0,1},{1,0},{2,3},{3,2},{4,5},{5,4},{6,7},{7,6},{8,9},{9,8},{10,11... | collective-permute-start | bytes 24584 | tf_op jit(solution)/shard_map/ppermute | solution.py:22
  162.9 1.1 copy-start.3
  164.1 1.0 copy-start.5
  165.1 1.0 copy-start.6
  168.1 14.2 %copy-start.4 = (bf16[1024,320]{1,0:T(8,128)(2,1)S(1)}, bf16[1024,320]{1,0:T(8,128)(2,1)}, u32[]{:S(2)}) copy-start(bf16[1024,320]{1,0:T(8,128)(2,1)} %copy-done.2) | copy-start | bytes 1966084
  168.1 5.7 %collective-permute-start.24 = (bf16[256,320]{1,0:T(8,128)(2,1)S(1)}, bf16[256,320]{1,0:T(8,128)(2,1)S(1)}, u32[]{:S(2)}, u32[]{:S(2)}) collective-permute-start(bf16[256,320]{1,0:T(8,128)(2,1)S(1)} %get-tuple-element.43), channel_id=1, source_target_pairs={{0,1},{1,0},{2,3},{3,2},{4,5},{5,4},{6,7},{7,6},{8,9},{9,8},{10,11... | collective-permute-start | bytes 491528 | tf_op jit(solution)/shard_map/ppermute | solution.py:22
  169.6 6.9 %collective-permute-start.25 = (bf16[256,320]{1,0:T(8,128)(2,1)S(1)}, bf16[256,320]{1,0:T(8,128)(2,1)S(1)}, u32[]{:S(2)}, u32[]{:S(2)}) collective-permute-start(bf16[256,320]{1,0:T(8,128)(2,1)S(1)} %get-tuple-element.44), channel_id=1, source_target_pairs={{0,2},{1,3},{2,0},{3,1},{4,6},{5,7},{6,4},{7,5},{8,10},{9,11},{10,... | collective-permute-start | bytes 491528 | tf_op jit(solution)/shard_map/ppermute | solution.py:22
  171.2 6.6 %collective-permute-start.26 = (bf16[256,320]{1,0:T(8,128)(2,1)S(1)}, bf16[256,320]{1,0:T(8,128)(2,1)S(1)}, u32[]{:S(2)}, u32[]{:S(2)}) collective-permute-start(bf16[256,320]{1,0:T(8,128)(2,1)S(1)} %get-tuple-element.45), channel_id=1, source_target_pairs={{0,3},{1,2},{2,1},{3,0},{4,7},{5,6},{6,5},{7,4},{8,11},{9,10},{10,... | collective-permute-start | bytes 491528 | tf_op jit(solution)/shard_map/ppermute | solution.py:22
  178.9 15.9 %all-to-all-start = ((bf16[8,64,320]{2,1,0:T(8,128)(2,1)}), bf16[8,64,320]{2,1,0:T(8,128)(2,1)S(1)}, u32[]{:S(2)}, u32[]{:S(2)}) async-start(bf16[8,64,320]{2,1,0:T(8,128)(2,1)} %bitcast.13), calls=%async_computation | async-start | bytes 786432 | tf_op jit(solution)/shard_map/all_to_all | solution.py:374

commit v2 on v0

v2 whole, which is shorter than its diff:
```python
import functools
import math

import jax
import jax.numpy as jnp
from jax import lax
from jax.experimental import pallas as pl
from jax.experimental.pallas import tpu as pltpu
from jax.sharding import PartitionSpec as P

HD = 80
HEAD_ROWS = 96
PAD = 128
FAR = 2.0**100
EPS = 1e-06
BLOCK = 256
BF = jnp.bfloat16
F32 = jnp.float32
VM = pl.BlockSpec(memory_space=pltpu.VMEM)
SM = pl.BlockSpec(memory_space=pltpu.SMEM)


def hop(x, axis, distance):
    return lax.ppermute(x, axis, [(i, i ^ distance) for i in range(lax.axis_size(axis))])


def call(body, name, args, smem, outs, scratch, flops, transcendentals=0):
    shapes = [jax.ShapeDtypeStruct(s, d) for s, d in outs]
    size = lambda s: math.prod(s.shape) * s.dtype.itemsize
    return pl.pallas_call(
        body,
        in_specs=[SM if i < smem else VM for i in range(len(args))],
        out_specs=[VM for _ in outs],
        out_shape=shapes,
        scratch_shapes=scratch,
        compiler_params=pltpu.CompilerParams(vmem_limit_bytes=20 << 20),
        cost_estimate=pl.CostEstimate(
            flops=flops,
            bytes_accessed=sum(size(a) for a in args) + sum(size(s) for s in shapes),
            transcendentals=transcendentals,
        ),
        name=name,
    )(*args)


def project_body(n_parts, kinds, col, scale, *refs):
    order = refs[0]
    parts = refs[1 : 1 + n_parts]
    gain, w, ids = refs[1 + n_parts : 4 + n_parts]
    outs = refs[4 + n_parts : 4 + n_parts + len(kinds)]
    normed = refs[-1]
    width, rows = parts[0].shape
    heads = w.shape[1] // HD
    values = [p[...].astype(F32) for p in parts]
    center = sum(jnp.sum(v, axis=0, keepdims=True) for v in values) * (1.0 / normed.shape[0])
    values = [v - center for v in values]
    spread = sum(jnp.sum(v * v, axis=0, keepdims=True) for v in values) * (
        1.0 / normed.shape[0]
    )
    inv = lax.rsqrt(spread + EPS)
    for k, v in enumerate(values):
        at = pl.ds(pl.multiple_of(order[k] * width, 16), width)
        normed[at, :] = (v * inv * gain[at, :]).astype(BF)
    line = lax.broadcasted_iota(jnp.int32, (HEAD_ROWS - HD, rows), 0)
    bits = (jnp.broadcast_to(ids[0:1, col : col + rows], line.shape) >> (line >> 1)) & 1
    hit = bits == (line & 1)
    for kind, out in zip(kinds, outs):
        acc = jnp.dot(w[kind], normed[...], preferred_element_type=F32)
        if kind == 0:
            acc = acc * scale
            extra = jnp.where(hit, 0.0, -FAR)
        elif kind == 1:
            extra = jnp.where(hit, 1.0, 0.0)
        else:
            extra = jnp.where(line == 0, 1.0, 0.0)
        for h in range(heads):
            piece = acc[h * HD : (h + 1) * HD, :]
            if kind == 1:
                tall = jnp.concatenate(
                    [piece, extra, jnp.zeros((PAD - HEAD_ROWS, rows), F32)], axis=0
                )
                out[:, h * PAD : (h + 1) * PAD] = tall.T.astype(BF)
            else:
                lo = h * HEAD_ROWS
                out[lo : lo + HD, :] = piece.astype(BF)
                out[lo + HD : lo + HEAD_ROWS, :] = extra.astype(BF)


def project(order, parts, gain, w, ids, kinds, col):
    width, rows = parts[0].shape
    full = width * len(parts)
    heads = w.shape[1] // HD
    shape = lambda kind: (
        (rows, heads * PAD) if kind == 1 else (heads * HEAD_ROWS, rows),
        BF,
    )
    return call(
        functools.partial(
            project_body, len(parts), kinds, col, HD**-0.5 * math.log2(math.e)
        ),
        "project",
        [order, *parts, gain, w, ids],
        1,
        [shape(kind) for kind in kinds],
        [pltpu.VMEM((full, rows), BF)],
        2 * rows * full * heads * HD * len(kinds),
    )


def visit(q, kr, vr, lo, size, acc, top, cols):
    heads = q.shape[0] // HEAD_ROWS
    scores = [
        jnp.dot(
            kr[lo : lo + size, h * PAD : h * PAD + HEAD_ROWS],
            q[h * HEAD_ROWS : (h + 1) * HEAD_ROWS, :],
            preferred_element_type=F32,
        )
        for h in range(heads)
    ]
    for h, s in enumerate(scores):
        at = slice(h * HEAD_ROWS, (h + 1) * HEAD_ROWS)
        old = top[h : h + 1, cols]
        new = jnp.maximum(old, jnp.max(s, axis=0, keepdims=True))
        p = jnp.exp2(s - new).astype(BF)
        acc[at, cols] = acc[at, cols] * jnp.exp2(old - new) + jnp.dot(
            vr[at, lo : lo + size], p, preferred_element_type=F32
        )
        top[h : h + 1, cols] = new


def near_body(block, flags, q0, q1, k0, k1, v0, v1, acc, top):
    acc[...] = jnp.zeros_like(acc)
    top[...] = jnp.full_like(top, -1e20)
    sweep(block, flags, 0, (q0, q1), (k0, k1), (v0, v1), acc, top, 0)


def sweep(block, flags, first_col, qs, ks, vs, acc, top, first_q):
    per = block // BLOCK
    q_index = first_q
    col = 0
    for q in qs:
        for qc in range(0, q.shape[1], block):
            chunk = first_col
            for kr, vr in zip(ks, vs):
                for lo in range(0, kr.shape[0], BLOCK):
                    wanted = flags[q_index, chunk]
                    for extra in range(1, per):
                        wanted = wanted + flags[q_index + extra, chunk]

                    @pl.when(wanted > 0)
                    def _(q=q, qc=qc, kr=kr, vr=vr, lo=lo, col=col):
                        visit(
                            q[:, qc : qc + block], kr, vr, lo, BLOCK, acc, top,
                            slice(col, col + block),
                        )

                    chunk += 1
            q_index += per
            col += block


def near(flags, qs, ks, vs):
    wide, rows = qs[0].shape
    heads = wide // HEAD_ROWS
    return call(
        functools.partial(near_body, min(512, rows)),
        "near",
        [flags, *qs, *ks, *vs],
        1,
        [((wide, 2 * rows), F32), ((8, 2 * rows), F32)],
        [],
        16 * rows * rows * wide,
        4 * rows * rows * heads,
    )


def middle_body(flags, q0, q1, k, v, acc_in, top_in, acc, top):
    acc[...] = acc_in[...]
    top[...] = top_in[...]
    sweep(BLOCK, flags, 0, (q0, q1), (k,), (v,), acc, top, 0)


def middle(flags, qs, k, v, acc, top):
    wide, rows = qs[0].shape
    heads = wide // HEAD_ROWS
    return call(
        middle_body,
        "middle",
        [flags, *qs, k, v, acc, top],
        1,
        [(acc.shape, F32), (top.shape, F32)],
        [],
        8 * rows * rows * wide,
        2 * rows * rows * heads,
    )


def last_body(n_out, index, flags, order, q, k, v, acc_in, top_in, w, *refs):
    outs = refs[:n_out]
    acc, top, ctx = refs[n_out:]
    rows = q.shape[1]
    heads = q.shape[0] // HEAD_ROWS
    here = slice(index * rows, (index + 1) * rows)
    acc[...] = acc_in[:, here]
    top[...] = top_in[:, here]
    sweep(BLOCK, flags, k.shape[0] // BLOCK, (q,), (k,), (v,), acc, top, index * rows // BLOCK)
    for h in range(heads):
        lo = h * HEAD_ROWS
        ctx[h * HD : (h + 1) * HD, :] = (
            acc[lo : lo + HD, :] / acc[lo + HD : lo + HD + 1, :]
        ).astype(BF)
    width = outs[0].shape[0]
    for j in reversed(range(n_out)):
        at = pl.ds(pl.multiple_of(order[j] * width, 16), width)
        outs[j][...] = jnp.dot(w[at, :], ctx[...], preferred_element_type=F32).astype(BF)


def last(flags, order, q, k, v, acc, top, w, n_out, index):
    wide, rows = q.shape
    heads = wide // HEAD_ROWS
    full = w.shape[0]
    return call(
        functools.partial(last_body, n_out, index),
        "last",
        [flags, order, q, k, v, acc, top, w],
        2,
        [((full // n_out, rows), BF) for _ in range(n_out)],
        [
            pltpu.VMEM((wide, rows), F32),
            pltpu.VMEM((8, rows), F32),
            pltpu.VMEM((heads * HD, rows), BF),
        ],
        4 * rows * rows * wide + 2 * rows * heads * HD * full,
        rows * rows * heads,
    )


def hidden_body(n_half, *refs):
    hidden, stats = refs[-2:]
    inputs = refs[:-2]
    each = len(inputs) // n_half
    stats[...] = jnp.zeros_like(stats)
    for i in range(n_half):
        group = inputs[i * each : (i + 1) * each]
        rows = group[0].shape[1]
        at = slice(i * rows, (i + 1) * rows)
        total = group[0][...].astype(F32)
        for g in group[1:]:
            total = total + g[...].astype(F32)
        rounded = total.astype(BF)
        hidden[:, at] = rounded
        values = rounded.astype(F32)
        center = jnp.mean(values, axis=0, keepdims=True)
        stats[0:1, at] = center
        stats[1:2, at] = jnp.mean((values - center) ** 2, axis=0, keepdims=True)


def hidden_sum(groups):
    width, rows = groups[0][0].shape
    count = rows * len(groups)
    return call(
        functools.partial(hidden_body, len(groups)),
        "hidden",
        [x for g in groups for x in g],
        0,
        [((width, count), BF), ((8, count), F32)],
        [],
        10 * width * count,
    )


def merge_body(n_stats, n_out, order, hidden, *refs):
    stats = refs[:n_stats]
    gain, pick, w = refs[n_stats : n_stats + 3]
    outs = refs[n_stats + 3 : n_stats + 3 + n_out]
    blocks = refs[-1]
    width, rows = hidden.shape
    means = [s[0:1, :] for s in stats]
    center = sum(means) * (1.0 / n_stats)
    spread = sum(
        s[1:2, :] + (m - center) ** 2 for s, m in zip(stats, means)
    ) * (1.0 / n_stats)
    inv = lax.rsqrt(spread + EPS)
    scaled = ((hidden[...].astype(F32) - center) * inv * gain[...]).astype(BF)
    size = pick.shape[0]
    quarter = size // 4
    for lo in range(0, rows, size):
        picked = lax.dot_general(
            pick[...],
            scaled[:, lo : lo + size],
            (((1,), (1,)), ((), ())),
            preferred_element_type=F32,
        ).astype(BF)
        for j in range(4):
            blocks[lo // 4 : lo // 4 + quarter, j * width : (j + 1) * width] = picked[
                j * quarter : (j + 1) * quarter, :
            ]
    terms = jnp.dot(blocks[...], w[...], preferred_element_type=F32)
    if n_out == 1:
        outs[0][...] = terms.astype(BF)
        return
    for me in range(n_out):

        @pl.when(order[0] == me)
        def _(me=me):
            for k in range(n_out):
                lo = (me ^ k) * width
                outs[k][...] = terms[:, lo : lo + width].astype(BF)


def merge(order, hidden, stats, gain, pick, w, n_out):
    width, rows = hidden.shape
    full = w.shape[1]
    return call(
        functools.partial(merge_body, len(stats), n_out),
        "merge",
        [order, hidden, *stats, gain, pick, w],
        1,
        [((rows // 4, full // n_out), BF) for _ in range(n_out)],
        [pltpu.VMEM((rows // 4, 4 * width), BF)],
        2 * rows * width * full + 2 * rows * pick.shape[0] * width,
    )


def place_body(n_in, *refs):
    merged = sum(r[...].astype(F32) for r in refs[:n_in]).astype(BF)
    dispatch, out = refs[n_in:]
    out[...] = jnp.dot(dispatch[...], merged, preferred_element_type=F32).astype(BF)


def place(terms, dispatch):
    return call(
        functools.partial(place_body, len(terms)),
        "place",
        [*terms, dispatch],
        0,
        [((dispatch.shape[0], terms[0].shape[1]), BF)],
        [],
        2 * math.prod(dispatch.shape) * terms[0].shape[1],
    )[0]


def spread_square(halves):
    low, high = halves
    a0 = hop(low, "tp", 1)
    b1 = hop(high, "tp", 2)
    a1 = hop(high, "tp", 1)
    b0 = hop(low, "tp", 2)
    c = hop(a0, "tp", 2)
    d = hop(b1, "tp", 1)
    return [(low, a0, b0, c), (high, a1, b1, d)]


def shards(tokens, segment, ln_gain, w_qkv, w_out, merge_gain, w_merge, owner):
    row_count, local_width = tokens.shape
    tp_count = lax.axis_size("tp")
    grp_count = lax.axis_size("grp")
    full_width = local_width * tp_count
    half = row_count // 2
    square = tp_count == 4
    me = lax.axis_index("tp")
    partner = grp_count // 2
    n_out = 4 if square else 1

    tall = tokens.T
    halves = [tall[:, :half], tall[:, half:]]
    far_segment = hop(segment, "grp", partner)
    far_halves = [hop(t, "grp", partner) for t in halves]
    if square:
        own_parts = spread_square(halves)
        far_parts = spread_square(far_halves)
        order = jnp.stack([me ^ k for k in range(4)]).astype(jnp.int32)
    else:
        own_parts = [(lax.all_gather(t, "tp", axis=0, tiled=True),) for t in halves]
        far_parts = [(lax.all_gather(t, "tp", axis=0, tiled=True),) for t in far_halves]
        order = jnp.zeros((1,), jnp.int32)

    gain = ln_gain[:, None]
    w_in = jnp.swapaxes(w_qkv, 1, 2)
    w_back = w_out.T
    gain_part = lax.dynamic_slice_in_dim(merge_gain, me * local_width, local_width, 0)[:, None]
    w_blocks = w_merge.reshape(4 * local_width, full_width)

    low_ids, high_ids = segment[::BLOCK], segment[BLOCK - 1 :: BLOCK]
    meets = lambda ids: (
        (ids[::BLOCK][None, :] <= high_ids[:, None])
        & (ids[BLOCK - 1 :: BLOCK][None, :] >= low_ids[:, None])
    ).astype(jnp.int32)
    near_flags = meets(segment)
    far_flags = meets(far_segment)

    picked = jnp.arange(half, dtype=jnp.int32)
    pick = (
        (picked % (half // 4) * 4 + picked // (half // 4))[:, None] == picked[None, :]
    ).astype(BF)

    merged_count = row_count // 4
    cap_slots = max(2, merged_count // grp_count * 2)
    targets = owner[:, 0]
    onehot = (targets[:, None] == jnp.arange(grp_count, dtype=jnp.int32)[None, :]).astype(F32)
    lower_mask = (
        jnp.arange(merged_count)[:, None] > jnp.arange(merged_count)[None, :]
    ).astype(F32)
    earlier = jnp.dot(lower_mask, onehot, precision=lax.Precision.HIGHEST)
    slot_index = jnp.sum(earlier * onehot, axis=1).astype(jnp.int32)
    slot_place = targets * cap_slots + slot_index
    dispatch = (
        jnp.arange(grp_count * cap_slots, dtype=jnp.int32)[:, None] == slot_place[None, :]
    ).astype(BF)

    ids = segment[None, :]
    far_ids = far_segment[None, :]
    own = [
        project(order, p, gain, w_in, ids, (0, 1, 2), i * half) for i, p in enumerate(own_parts)
    ]
    qs, ks, vs = zip(*own)
    far = [
        project(order, p, gain, w_in, far_ids, (1, 2), i * half)
        for i, p in enumerate(far_parts)
    ]
    acc, top = near(near_flags, qs, ks, vs)
    acc, top = middle(far_flags, qs, far[0][0], far[0][1], acc, top)
    terms = [
        last(far_flags, order, qs[i], far[1][0], far[1][1], acc, top, w_back, n_out, i)
        for i in range(2)
    ]

    if square:
        groups = []
        for i, (side_hop, next_hop) in enumerate(((1, 2), (2, 1))):
            corner = hop(terms[i][3], "tp", side_hop)
            side = hop(terms[i][side_hop], "tp", side_hop)
            passed = (terms[i][next_hop].astype(F32) + corner.astype(F32)).astype(BF)
            onward = hop(passed, "tp", next_hop)
            groups.append((halves[i], terms[i][0], side, onward))
    else:
        groups = [
            (h, lax.psum_scatter(t[0], "tp", scatter_dimension=0, tiled=True))
            for h, t in zip(halves, terms)
        ]
    hidden, stats = hidden_sum(groups)
    if square:
        all_stats = [stats] + [hop(stats, "tp", k) for k in (1, 2, 3)]
    else:
        gathered = lax.all_gather(stats, "tp")
        all_stats = [gathered[k] for k in range(tp_count)]
    merge_terms = merge(order, hidden, all_stats, gain_part, pick, w_blocks, n_out)
    if square:
        received = [merge_terms[0]] + [hop(merge_terms[k], "tp", k) for k in (1, 2, 3)]
    else:
        received = [lax.psum_scatter(merge_terms[0], "tp", scatter_dimension=1, tiled=True)]
    outgoing = place(received, dispatch).reshape(grp_count, cap_slots, local_width)
    routed = lax.all_to_all(outgoing, "grp", split_axis=0, concat_axis=0, tiled=True)
    return (hidden.T, routed[None])


def solution(mesh):
    return jax.shard_map(
        shards,
        mesh=mesh,
        in_specs=(
            P("grp", "tp"),
            P("grp"),
            P(),
            P(None, None, "tp"),
            P("tp", None),
            P(),
            P(None, "tp", None),
            P("grp", None),
        ),
        out_specs=(P("grp", "tp"), P("grp", None, None, "tp")),
        check_vma=False,
    )
```

time: 320 us -> 146 us (0.46)
  waiting for transfers between devices: 206 us -> 51 us
  matrix products: 31.1 us -> 0.19 us
  Pallas kernels: 0 us -> 30.9 us
  starting transfers between devices: 3.08 us -> 32.1 us
  other arithmetic: 18.6 us -> 1.37 us
  local copies, waits for them, and re-layouts: 27.8 us -> 12 us
  between operations: 13.9 us -> 0.85 us
    all_gather x2 -> x0, waiting for transfers between devices: 83.2 us -> none  [the longest x1 44.3 us: shards(): gathered = lax.all_gather(tokens, 'tp', axis=1, tiled=True)]
    reduce_scatter x1 -> x0, waiting for transfers between devices: 39.7 us -> none  [shards(): lax.psum_scatter(out_terms.astype(jnp.bfloat16), 'tp', scatter_dimension=...]
    dot_general x20 -> x0, matrix products: 30.9 us -> none  [the longest x8 10.3 us: one_block(): jnp.dot(query_rows[:, low_col:low_col + HD], key_rows[:, low_col:low_col...]
    pallas_call x0 -> x11, Pallas kernels: none -> 30.9 us  [call(): pl.pallas_call(body, in_specs=[SM if i < smem else VM for i in range(len(...]
    ppermute x2 -> x27, starting transfers between devices: 2.92 us -> 32.1 us  [hop(): lax.ppermute(x, axis, [(i, i ^ distance) for i in range(lax.axis_size(axi...]
    unnamed x5 -> x0, waiting for transfers between devices: 26.1 us -> none
    reduce_sum x12 -> x0, other arithmetic: 11.8 us -> none  [the longest x8 5.66 us: one_block(): sums_total = jnp.sum(raw_weights, axis=1, keepdims=True)]
    while x11 -> x0, local copies, waits for them, and re-layouts: 9.18 us -> none  [the longest x3 9.17 us: shards(): lax.map(one_block, jnp.arange(block_count, dtype=jnp.int32))]
  transfers between devices with their start and end apart: 6 -> 27, of which waited for: 5 -> 14; matrix products, arithmetic and copies ran while one was open for 2% -> 5% of each run, Pallas kernels for 0% -> 14%
where the time goes in v2:
time: 146 us; the launch traced here: 145 us
  waiting for transfers between devices  51 us (35%)
  starting transfers between devices  32.1 us (22%)
  Pallas kernels  30.9 us (21%)
  blocking collectives  16.4 us (11%)
  local copies, waits for them, and re-layouts  12 us (8%)
    ppermute x27, waiting for transfers between devices, hop(): lax.ppermute(x, axis, [(i, i ^ distance) for i in range(lax.axis_size(axi...  51 us
    ppermute x27, starting transfers between devices, hop(): lax.ppermute(x, axis, [(i, i ^ distance) for i in range(lax.axis_size(axi...  32.1 us
    pallas_call x11, Pallas kernels, call(): pl.pallas_call(body, in_specs=[SM if i < smem else VM for i in range(len(...  30.9 us
    all_to_all x1, blocking collectives, shards(): lax.all_to_all(outgoing, 'grp', split_axis=0, concat_axis=0, tiled=True)  16.4 us
    unnamed x18, local copies, waits for them, and re-layouts  5.53 us
  transfers between devices with their start and end apart: 27, of which 14 were waited for; matrix products, arithmetic and copies ran while one was open for 5% of the time, Pallas kernels for 14%

profile of v2, /device:TPU:0, one launch (start us, length us, event | category | flops | bytes accessed | tf_op | source)
XLA Modules:
  0.0 144.8 jit_solution(8095226828740235052)
XLA Ops:
  0.7 2.1 %fusion.13 = (bf16[320,512]{1,0:T(8,128)(2,1)}, bf16[320,512]{1,0:T(8,128)(2,1)}) fusion(bf16[320,1024]{1,0:T(8,128)(2,1)} %bitcast.28), kind=kLoop, calls=%fused_computation.28 | loop fusion | bytes 1310720 | tf_op jit(solution)/shard_map/slice | solution.py:366
  2.8 3.0 %collective-permute-start.9 = (bf16[320,512]{1,0:T(8,128)(2,1)}, bf16[320,512]{1,0:T(8,128)(2,1)}, u32[]{:S(2)}, u32[]{:S(2)}) collective-permute-start(bf16[320,512]{1,0:T(8,128)(2,1)} %get-tuple-element.58.refs_1_.refs_4_), channel_id=1, source_target_pairs={{0,2},{1,3},{2,0},{3,1},{4,6},{5,7},{6,4},{7,5},{8,10},{9,11},{10,... | collective-permute-start | bytes 983048 | tf_op jit(solution)/shard_map/ppermute | solution.py:24
  5.7 2.6 %collective-permute-start.11 = (bf16[320,512]{1,0:T(8,128)(2,1)}, bf16[320,512]{1,0:T(8,128)(2,1)}, u32[]{:S(2)}, u32[]{:S(2)}) collective-permute-start(bf16[320,512]{1,0:T(8,128)(2,1)} %get-tuple-element.59.refs_1_.refs_0_), channel_id=1, source_target_pairs={{0,16},{4,20},{8,24},{12,28},{16,0},{20,4},{24,8},{28,12},{1,17},{... | collective-permute-start | bytes 983048 | tf_op jit(solution)/shard_map/ppermute | solution.py:24
  8.3 0.3 collective-permute-start
  8.6 1.5 %collective-permute-start.8 = (bf16[320,512]{1,0:T(8,128)(2,1)}, bf16[320,512]{1,0:T(8,128)(2,1)}, u32[]{:S(2)}, u32[]{:S(2)}) collective-permute-start(bf16[320,512]{1,0:T(8,128)(2,1)} %get-tuple-element.58.refs_1_.refs_4_), channel_id=1, source_target_pairs={{0,1},{1,0},{2,3},{3,2},{4,5},{5,4},{6,7},{7,6},{8,9},{9,8},{10,11... | collective-permute-start | bytes 983048 | tf_op jit(solution)/shard_map/ppermute | solution.py:24
  10.1 0.5 collective-permute-start.1
  10.7 12.6 %collective-permute-done = s32[1024]{0:T(1024)S(1)} collective-permute-done((s32[1024]{0:T(1024)}, s32[1024]{0:T(1024)S(1)}, u32[]{:S(2)}, u32[]{:S(2)}) %collective-permute-start) | collective-permute-done | bytes 4128 | tf_op jit(solution)/shard_map/ppermute | solution.py:24
  23.3 0.8 slice.22
  24.0 0.8 slice.24
  24.8 1.8 %broadcast_in_dim.16.refs_5_ = f32[1280,1]{1,0:T(8,128)} reshape(f32[1280]{0:T(1024)} %param.10) | data formatting | bytes 10240 | tf_op jit(solution)/shard_map/broadcast_in_dim | solution.py:378
  26.6 1.5 %copy.15 = bf16[320,1280]{0,1:T(8,128)(2,1)S(1)} copy(bf16[320,1280]{1,0:T(8,128)(2,1)} %param.12) | data formatting | bytes 1638400 | tf_op args[4]
  28.1 1.6 %collective-permute-start.10 = (bf16[320,512]{1,0:T(8,128)(2,1)}, bf16[320,512]{1,0:T(8,128)(2,1)}, u32[]{:S(2)}, u32[]{:S(2)}) collective-permute-start(bf16[320,512]{1,0:T(8,128)(2,1)} %collective-permute-done.9.refs_3_), channel_id=1, source_target_pairs={{0,1},{1,0},{2,3},{3,2},{4,5},{5,4},{6,7},{7,6},{8,9},{9,8},{10,11... | collective-permute-start | bytes 983048 | tf_op jit(solution)/shard_map/ppermute | solution.py:24
  29.7 0.5 collective-permute-start.12
  30.5 0.5 collective-permute-start.2
  31.0 1.6 %collective-permute-start.3 = (bf16[320,512]{1,0:T(8,128)(2,1)}, bf16[320,512]{1,0:T(8,128)(2,1)S(1)}, u32[]{:S(2)}, u32[]{:S(2)}) collective-permute-start(bf16[320,512]{1,0:T(8,128)(2,1)} %collective-permute-done.1.refs_2_), channel_id=1, source_target_pairs={{0,2},{1,3},{2,0},{3,1},{4,6},{5,7},{6,4},{7,5},{8,10},{9,11},{10,... | collective-permute-start | bytes 983048 | tf_op jit(solution)/shard_map/ppermute | solution.py:24
  32.5 7.6 %collective-permute-done.4.refs_1_ = bf16[320,512]{1,0:T(8,128)(2,1)} collective-permute-done((bf16[320,512]{1,0:T(8,128)(2,1)}, bf16[320,512]{1,0:T(8,128)(2,1)}, u32[]{:S(2)}, u32[]{:S(2)}) %collective-permute-start.4) | collective-permute-done | bytes 327712 | tf_op jit(solution)/shard_map/ppermute | solution.py:24
  40.1 0.5 collective-permute-start.6
  40.7 1.5 %collective-permute-start.13 = (bf16[320,512]{1,0:T(8,128)(2,1)}, bf16[320,512]{1,0:T(8,128)(2,1)S(1)}, u32[]{:S(2)}, u32[]{:S(2)}) collective-permute-start(bf16[320,512]{1,0:T(8,128)(2,1)} %collective-permute-done.11.refs_1_), channel_id=1, source_target_pairs={{0,2},{1,3},{2,0},{3,1},{4,6},{5,7},{6,4},{7,5},{8,10},{9,11},{10,... | collective-permute-start | bytes 983048 | tf_op jit(solution)/shard_map/ppermute | solution.py:24
  42.2 1.9 %collective-permute-done.12.refs_2_ = bf16[320,512]{1,0:T(8,128)(2,1)} collective-permute-done((bf16[320,512]{1,0:T(8,128)(2,1)}, bf16[320,512]{1,0:T(8,128)(2,1)}, u32[]{:S(2)}, u32[]{:S(2)}) %collective-permute-start.12) | collective-permute-done | bytes 327712 | tf_op jit(solution)/shard_map/ppermute | solution.py:24
  44.1 0.5 collective-permute-start.14
  44.6 1.1 copy-done.1
  45.7 3.8 %project.6 = (bf16[384,512]{1,0:T(8,128)(2,1)S(1)}, bf16[512,512]{1,0:T(8,128)(2,1)S(1)}, bf16[384,512]{1,0:T(8,128)(2,1)S(1)}) custom-call(s32[4]{0:T(128)S(1)} %pad_add_fusion.refs_0_.order, bf16[320,512]{1,0:T(8,128)(2,1)} %get-tuple-element.58.refs_1_.refs_4_, bf16[320,512]{1,0:T(8,128)(2,1)} %collective-permute-done.8.refs_2_, ...), custom_call_target="tpu_custom_call" | custom-call | flops 1258291200 | bytes 5088272 | tf_op jit(solution)/shard_map/project/pallas_call | solution.py:30
  49.5 1.6 %collective-permute-start.5 = (bf16[320,512]{1,0:T(8,128)(2,1)}, bf16[320,512]{1,0:T(8,128)(2,1)S(1)}, u32[]{:S(2)}, u32[]{:S(2)}) collective-permute-start(bf16[320,512]{1,0:T(8,128)(2,1)} %collective-permute-done.4.refs_1_), channel_id=1, source_target_pairs={{0,1},{1,0},{2,3},{3,2},{4,5},{5,4},{6,7},{7,6},{8,9},{9,8},{10,11... | collective-permute-start | bytes 983048 | tf_op jit(solution)/shard_map/ppermute | solution.py:24
  51.1 4.3 %collective-permute-done.6.refs_3_ = bf16[320,512]{1,0:T(8,128)(2,1)S(1)} collective-permute-done((bf16[320,512]{1,0:T(8,128)(2,1)}, bf16[320,512]{1,0:T(8,128)(2,1)S(1)}, u32[]{:S(2)}, u32[]{:S(2)}) %collective-permute-start.6) | collective-permute-done | bytes 327712 | tf_op jit(solution)/shard_map/ppermute | solution.py:24
  55.4 1.5 %collective-permute-start.7 = (bf16[320,512]{1,0:T(8,128)(2,1)S(1)}, bf16[320,512]{1,0:T(8,128)(2,1)S(1)}, u32[]{:S(2)}, u32[]{:S(2)}) collective-permute-start(bf16[320,512]{1,0:T(8,128)(2,1)S(1)} %collective-permute-done.6.refs_3_), channel_id=1, source_target_pairs={{0,1},{1,0},{2,3},{3,2},{4,5},{5,4},{6,7},{7,6},{8,9},{9,8},{10,11... | collective-permute-start | bytes 983048 | tf_op jit(solution)/shard_map/ppermute | solution.py:24
  56.9 3.6 %project.4 = (bf16[384,512]{1,0:T(8,128)(2,1)S(1)}, bf16[512,512]{1,0:T(8,128)(2,1)S(1)}, bf16[384,512]{1,0:T(8,128)(2,1)S(1)}) custom-call(s32[4]{0:T(128)S(1)} %pad_add_fusion.refs_0_.order, bf16[320,512]{1,0:T(8,128)(2,1)} %get-tuple-element.59.refs_1_.refs_0_, bf16[320,512]{1,0:T(8,128)(2,1)} %collective-permute-done.1.refs_2_, ...), custom_call_target="tpu_custom_call" | custom-call | flops 1258291200 | bytes 5088272 | tf_op jit(solution)/shard_map/project/pallas_call | solution.py:30
  60.5 5.6 %near.1 = (f32[384,1024]{1,0:T(8,128)S(1)}, f32[8,1024]{1,0:T(8,128)S(1)}) custom-call(s32[4,4]{1,0:T(4,128)S(1)} %get-tuple-element.60.flags, bf16[384,512]{1,0:T(8,128)(2,1)S(1)} %get-tuple-element.30.q0.q, bf16[384,512]{1,0:T(8,128)(2,1)S(1)} %get-tuple-element.33.q1.q, bf16[512,512]{1,0:T(8,128)(2,1)S(1)} %get-tuple-element.36.k0, ...), custom_call_target="tpu_custom_call" | custom-call | flops 1610612736 | bytes 4227136 | tf_op jit(solution)/shard_map/near/pallas_call | solution.py:30
  66.1 0.8 collective-permute-done.14.refs_4_
  66.9 3.1 %project.7 = (bf16[512,512]{1,0:T(8,128)(2,1)S(1)}, bf16[384,512]{1,0:T(8,128)(2,1)S(1)}) custom-call(s32[4]{0:T(128)S(1)} %pad_add_fusion.refs_0_.order, bf16[320,512]{1,0:T(8,128)(2,1)} %collective-permute-done.11.refs_1_, bf16[320,512]{1,0:T(8,128)(2,1)} %collective-permute-done.12.refs_2_, bf16[320,512]{1,0:T(8,128)(2,1)S(1)} %collective-permute-done.13.refs_3_, ...), custom_call_target="tpu_custom_call" | custom-call | flops 838860800 | bytes 4695056 | tf_op jit(solution)/shard_map/project/pallas_call | solution.py:30
  70.0 2.8 %middle.1 = (f32[384,1024]{1,0:T(8,128)S(1)}, f32[8,1024]{1,0:T(8,128)S(1)}) custom-call(s32[4,4]{1,0:T(4,128)S(1)} %get-tuple-element.61.flags, bf16[384,512]{1,0:T(8,128)(2,1)S(1)} %get-tuple-element.30.q0.q, bf16[384,512]{1,0:T(8,128)(2,1)S(1)} %get-tuple-element.33.q1.q, bf16[512,512]{1,0:T(8,128)(2,1)S(1)} %get-tuple-element.34.k, ...), custom_call_target="tpu_custom_call" | custom-call | flops 805306368 | bytes 4915264 | tf_op jit(solution)/shard_map/middle/pallas_call | solution.py:30
  72.8 3.0 %project.5 = (bf16[512,512]{1,0:T(8,128)(2,1)S(1)}, bf16[384,512]{1,0:T(8,128)(2,1)S(1)}) custom-call(s32[4]{0:T(128)S(1)} %pad_add_fusion.refs_0_.order, bf16[320,512]{1,0:T(8,128)(2,1)} %collective-permute-done.4.refs_1_, bf16[320,512]{1,0:T(8,128)(2,1)S(1)} %collective-permute-done.5.refs_2_, bf16[320,512]{1,0:T(8,128)(2,1)S(1)} %collective-permute-done.6.refs_3_, ...), custom_call_target="tpu_custom_call" | custom-call | flops 838860800 | bytes 4695056 | tf_op jit(solution)/shard_map/project/pallas_call | solution.py:30
  75.9 1.5 %last.3 = (bf16[320,512]{1,0:T(8,128)(2,1)S(1)}, bf16[320,512]{1,0:T(8,128)(2,1)S(1)}, bf16[320,512]{1,0:T(8,128)(2,1)S(1)}, bf16[320,512]{1,0:T(8,128)(2,1)S(1)}) custom-call(s32[4,4]{1,0:T(4,128)S(1)} %get-tuple-element.61.flags, s32[4]{0:T(128)S(1)} %pad_add_fusion.refs_0_.order, bf16[384,512]{1,0:T(8,128)(2,1)S(1)} %get-tuple-element.33.q1.q, ...), custom_call_target="tpu_custom_call" | custom-call | flops 822083584 | bytes 5046352 | tf_op jit(solution)/shard_map/last/pallas_call | solution.py:30
  77.4 0.5 collective-permute-start.19
  78.0 1.7 %last.2 = (bf16[320,512]{1,0:T(8,128)(2,1)S(1)}, bf16[320,512]{1,0:T(8,128)(2,1)S(1)}, bf16[320,512]{1,0:T(8,128)(2,1)S(1)}, bf16[320,512]{1,0:T(8,128)(2,1)S(1)}) custom-call(s32[4,4]{1,0:T(4,128)S(1)} %get-tuple-element.61.flags, s32[4]{0:T(128)S(1)} %pad_add_fusion.refs_0_.order, bf16[384,512]{1,0:T(8,128)(2,1)S(1)} %get-tuple-element.30.q0.q, ...), custom_call_target="tpu_custom_call" | custom-call | flops 822083584 | bytes 5046352 | tf_op jit(solution)/shard_map/last/pallas_call | solution.py:30
  79.7 1.6 %collective-permute-start.16 = (bf16[320,512]{1,0:T(8,128)(2,1)S(1)}, bf16[320,512]{1,0:T(8,128)(2,1)S(1)}, u32[]{:S(2)}, u32[]{:S(2)}) collective-permute-start(bf16[320,512]{1,0:T(8,128)(2,1)S(1)} %get-tuple-element.47), channel_id=1, source_target_pairs={{0,1},{1,0},{2,3},{3,2},{4,5},{5,4},{6,7},{7,6},{8,9},{9,8},{10,11... | collective-permute-start | bytes 983048 | tf_op jit(solution)/shard_map/ppermute | solution.py:24
  81.3 0.2 fusion
  81.5 1.6 %collective-permute-start.18 = (bf16[320,512]{1,0:T(8,128)(2,1)S(1)}, bf16[320,512]{1,0:T(8,128)(2,1)S(1)}, u32[]{:S(2)}, u32[]{:S(2)}) collective-permute-start(bf16[320,512]{1,0:T(8,128)(2,1)S(1)} %get-tuple-element.49), channel_id=1, source_target_pairs={{0,2},{1,3},{2,0},{3,1},{4,6},{5,7},{6,4},{7,5},{8,10},{9,11},{10,... | collective-permute-start | bytes 983048 | tf_op jit(solution)/shard_map/ppermute | solution.py:24
  83.0 0.5 collective-permute-start.15
  83.6 4.5 %collective-permute-done.19 = bf16[320,512]{1,0:T(8,128)(2,1)S(1)} collective-permute-done((bf16[320,512]{1,0:T(8,128)(2,1)S(1)}, bf16[320,512]{1,0:T(8,128)(2,1)S(1)}, u32[]{:S(2)}, u32[]{:S(2)}) %collective-permute-start.19) | collective-permute-done | bytes 327712 | tf_op jit(solution)/shard_map/ppermute | solution.py:24
  88.2 1.6 %collective-permute-start.20 = (bf16[320,512]{1,0:T(8,128)(2,1)S(1)}, bf16[320,512]{1,0:T(8,128)(2,1)S(1)}, u32[]{:S(2)}, u32[]{:S(2)}) collective-permute-start(bf16[320,512]{1,0:T(8,128)(2,1)S(1)} %add_convert_fusion), channel_id=1, source_target_pairs={{0,1},{1,0},{2,3},{3,2},{4,5},{5,4},{6,7},{7,6},{8,9},{9,8},{10,11... | collective-permute-start | bytes 983048 | tf_op jit(solution)/shard_map/ppermute | solution.py:24
  89.8 0.6 collective-permute-done.16
  90.4 1.6 %collective-permute-start.17 = (bf16[320,512]{1,0:T(8,128)(2,1)S(1)}, bf16[320,512]{1,0:T(8,128)(2,1)S(1)}, u32[]{:S(2)}, u32[]{:S(2)}) collective-permute-start(bf16[320,512]{1,0:T(8,128)(2,1)S(1)} %add_convert_fusion.1), channel_id=1, source_target_pairs={{0,2},{1,3},{2,0},{3,1},{4,6},{5,7},{6,4},{7,5},{8,10},{9,11},{10,... | collective-permute-start | bytes 983048 | tf_op jit(solution)/shard_map/ppermute | solution.py:24
  92.0 1.0 fusion.1.refs_5_
  93.0 2.1 %collective-permute-done.18.refs_6_ = bf16[320,512]{1,0:T(8,128)(2,1)S(1)} collective-permute-done((bf16[320,512]{1,0:T(8,128)(2,1)S(1)}, bf16[320,512]{1,0:T(8,128)(2,1)S(1)}, u32[]{:S(2)}, u32[]{:S(2)}) %collective-permute-start.18) | collective-permute-done | bytes 327712 | tf_op jit(solution)/shard_map/ppermute | solution.py:24
  95.1 2.2 %collective-permute-done.15.refs_2_ = bf16[320,512]{1,0:T(8,128)(2,1)S(1)} collective-permute-done((bf16[320,512]{1,0:T(8,128)(2,1)S(1)}, bf16[320,512]{1,0:T(8,128)(2,1)S(1)}, u32[]{:S(2)}, u32[]{:S(2)}) %collective-permute-start.15) | collective-permute-done | bytes 327712 | tf_op jit(solution)/shard_map/ppermute | solution.py:24
  97.4 5.9 %collective-permute-done.20.refs_7_ = bf16[320,512]{1,0:T(8,128)(2,1)S(1)} collective-permute-done((bf16[320,512]{1,0:T(8,128)(2,1)S(1)}, bf16[320,512]{1,0:T(8,128)(2,1)S(1)}, u32[]{:S(2)}, u32[]{:S(2)}) %collective-permute-start.20) | collective-permute-done | bytes 327712 | tf_op jit(solution)/shard_map/ppermute | solution.py:24
  103.3 2.7 %hidden.1 = (bf16[320,1024]{1,0:T(8,128)(2,1)}, f32[8,1024]{1,0:T(8,128)S(1)}) custom-call(bf16[320,512]{1,0:T(8,128)(2,1)} %get-tuple-element.59.refs_1_.refs_0_, bf16[320,512]{1,0:T(8,128)(2,1)S(1)} %get-tuple-element.44.refs_1_, bf16[320,512]{1,0:T(8,128)(2,1)S(1)} %collective-permute-done.15.refs_2_, ...), custom_call_target="tpu_custom_call" | custom-call | flops 3276800 | bytes 3309568 | tf_op jit(solution)/shard_map/hidden/pallas_call | solution.py:30
  106.0 1.5 %collective-permute-start.21 = (f32[8,1024]{1,0:T(8,128)S(1)}, f32[8,1024]{1,0:T(8,128)S(1)}, u32[]{:S(2)}, u32[]{:S(2)}) collective-permute-start(f32[8,1024]{1,0:T(8,128)S(1)} %get-tuple-element.53.refs_0_), channel_id=1, source_target_pairs={{0,1},{1,0},{2,3},{3,2},{4,5},{5,4},{6,7},{7,6},{8,9},{9,8},{10,11... | collective-permute-start | bytes 98312 | tf_op jit(solution)/shard_map/ppermute | solution.py:24
  107.5 1.5 %collective-permute-start.22 = (f32[8,1024]{1,0:T(8,128)S(1)}, f32[8,1024]{1,0:T(8,128)S(1)}, u32[]{:S(2)}, u32[]{:S(2)}) collective-permute-start(f32[8,1024]{1,0:T(8,128)S(1)} %get-tuple-element.53.refs_0_), channel_id=1, source_target_pairs={{0,2},{1,3},{2,0},{3,1},{4,6},{5,7},{6,4},{7,5},{8,10},{9,11},{10,... | collective-permute-start | bytes 98312 | tf_op jit(solution)/shard_map/ppermute | solution.py:24
  109.0 0.5 collective-permute-start.23
  109.5 0.8 dynamic_slice.3
  110.3 1.3 collective-permute-done.22.refs_2_
  111.6 2.2 %collective-permute-done.23.refs_3_ = f32[8,1024]{1,0:T(8,128)S(1)} collective-permute-done((f32[8,1024]{1,0:T(8,128)S(1)}, f32[8,1024]{1,0:T(8,128)S(1)}, u32[]{:S(2)}, u32[]{:S(2)}) %collective-permute-start.23) | collective-permute-done | bytes 32800 | tf_op jit(solution)/shard_map/ppermute | solution.py:24
  113.8 1.0 copy-done.4
  114.8 1.1 copy-done.5
  115.9 2.7 %merge.1 = (bf16[256,320]{1,0:T(8,128)(2,1)S(1)}, bf16[256,320]{1,0:T(8,128)(2,1)S(1)}, bf16[256,320]{1,0:T(8,128)(2,1)S(1)}, bf16[256,320]{1,0:T(8,128)(2,1)S(1)}) custom-call(s32[4]{0:T(128)S(1)} %pad_add_fusion.refs_0_.order, bf16[320,1024]{1,0:T(8,128)(2,1)S(1)} %copy-done.5, f32[8,1024]{1,0:T(8,128)S(1)} %get-tuple-element.53.refs_0_, ...), custom_call_target="tpu_custom_call" | custom-call | flops 1174405120 | bytes 5244176 | tf_op jit(solution)/shard_map/merge/pallas_call | solution.py:30
  118.6 0.6 collective-permute-start.24
  119.2 0.5 collective-permute-start.25
  119.7 2.5 %collective-permute-start.26 = (bf16[256,320]{1,0:T(8,128)(2,1)S(1)}, bf16[256,320]{1,0:T(8,128)(2,1)S(1)}, u32[]{:S(2)}, u32[]{:S(2)}) collective-permute-start(bf16[256,320]{1,0:T(8,128)(2,1)S(1)} %get-tuple-element.57), channel_id=1, source_target_pairs={{0,3},{1,2},{2,1},{3,0},{4,7},{5,6},{6,5},{7,4},{8,11},{9,10},{10,... | collective-permute-start | bytes 491528 | tf_op jit(solution)/shard_map/ppermute | solution.py:24
  122.2 2.7 %collective-permute-done.24.refs_1_ = bf16[256,320]{1,0:T(8,128)(2,1)S(1)} collective-permute-done((bf16[256,320]{1,0:T(8,128)(2,1)S(1)}, bf16[256,320]{1,0:T(8,128)(2,1)S(1)}, u32[]{:S(2)}, u32[]{:S(2)}) %collective-permute-start.24) | collective-permute-done | bytes 163872 | tf_op jit(solution)/shard_map/ppermute | solution.py:24
  124.9 2.4 %collective-permute-done.25.refs_2_ = bf16[256,320]{1,0:T(8,128)(2,1)S(1)} collective-permute-done((bf16[256,320]{1,0:T(8,128)(2,1)S(1)}, bf16[256,320]{1,0:T(8,128)(2,1)S(1)}, u32[]{:S(2)}, u32[]{:S(2)}) %collective-permute-start.25) | collective-permute-done | bytes 163872 | tf_op jit(solution)/shard_map/ppermute | solution.py:24
  127.3 0.4 place.1
  127.6 16.4 %all_to_all.5 = bf16[8,64,320]{2,1,0:T(8,128)(2,1)S(1)} all-to-all(bf16[8,64,320]{2,1,0:T(8,128)(2,1)S(1)} %bitcast.21), channel_id=1, replica_groups=mesh['grp'=8,'tp'=4] {'grp'}, dimensions={0} | all-to-all | bytes 655360 | tf_op jit(solution)/shard_map/all_to_all | solution.py:453
  144.0 0.7 copy.18
  (37 shorter events, 0.7 us)
Async XLA Ops:
  0.6 44.0 %copy-start.6 = (s32[1024]{0:T(1024)S(1)}, s32[1024]{0:T(1024)}, u32[]{:S(2)}) copy-start(s32[1024]{0:T(1024)} %param.9) | copy-start | bytes 12292
  0.6 44.0 %copy-start = (bf16[3,1280,320]{1,2,0:T(8,128)(2,1)S(1)}, bf16[3,1280,320]{1,2,0:T(8,128)(2,1)}, u32[]{:S(2)}) copy-start(bf16[3,1280,320]{1,2,0:T(8,128)(2,1)} %param.11) | copy-start | bytes 7372804
  2.8 25.4 %collective-permute-start.9 = (bf16[320,512]{1,0:T(8,128)(2,1)}, bf16[320,512]{1,0:T(8,128)(2,1)}, u32[]{:S(2)}, u32[]{:S(2)}) collective-permute-start(bf16[320,512]{1,0:T(8,128)(2,1)} %get-tuple-element.58.refs_1_.refs_4_), channel_id=1, source_target_pairs={{0,2},{1,3},{2,0},{3,1},{4,6},{5,7},{6,4},{7,5},{8,10},{9,11},{10,... | collective-permute-start | bytes 983048 | tf_op jit(solution)/shard_map/ppermute | solution.py:24
  5.7 24.0 %collective-permute-start.11 = (bf16[320,512]{1,0:T(8,128)(2,1)}, bf16[320,512]{1,0:T(8,128)(2,1)}, u32[]{:S(2)}, u32[]{:S(2)}) collective-permute-start(bf16[320,512]{1,0:T(8,128)(2,1)} %get-tuple-element.59.refs_1_.refs_0_), channel_id=1, source_target_pairs={{0,16},{4,20},{8,24},{12,28},{16,0},{20,4},{24,8},{28,12},{1,17},{... | collective-permute-start | bytes 983048 | tf_op jit(solution)/shard_map/ppermute | solution.py:24
  8.3 14.9 %collective-permute-start = (s32[1024]{0:T(1024)}, s32[1024]{0:T(1024)S(1)}, u32[]{:S(2)}, u32[]{:S(2)}) collective-permute-start(s32[1024]{0:T(1024)} %param.9), channel_id=1, source_target_pairs={{0,16},{4,20},{8,24},{12,28},{16,0},{20,4},{24,8},{28,12},{1,17},{... | collective-permute-start | bytes 12296 | tf_op jit(solution)/shard_map/ppermute | solution.py:24
  8.6 21.8 %collective-permute-start.8 = (bf16[320,512]{1,0:T(8,128)(2,1)}, bf16[320,512]{1,0:T(8,128)(2,1)}, u32[]{:S(2)}, u32[]{:S(2)}) collective-permute-start(bf16[320,512]{1,0:T(8,128)(2,1)} %get-tuple-element.58.refs_1_.refs_4_), channel_id=1, source_target_pairs={{0,1},{1,0},{2,3},{3,2},{4,5},{5,4},{6,7},{7,6},{8,9},{9,8},{10,11... | collective-permute-start | bytes 983048 | tf_op jit(solution)/shard_map/ppermute | solution.py:24
  10.1 20.8 %collective-permute-start.1 = (bf16[320,512]{1,0:T(8,128)(2,1)}, bf16[320,512]{1,0:T(8,128)(2,1)}, u32[]{:S(2)}, u32[]{:S(2)}) collective-permute-start(bf16[320,512]{1,0:T(8,128)(2,1)} %get-tuple-element.59.refs_1_.refs_0_), channel_id=1, source_target_pairs={{0,1},{1,0},{2,3},{3,2},{4,5},{5,4},{6,7},{7,6},{8,9},{9,8},{10,11... | collective-permute-start | bytes 983048 | tf_op jit(solution)/shard_map/ppermute | solution.py:24
  23.3 16.8 %collective-permute-start.4 = (bf16[320,512]{1,0:T(8,128)(2,1)}, bf16[320,512]{1,0:T(8,128)(2,1)}, u32[]{:S(2)}, u32[]{:S(2)}) collective-permute-start(bf16[320,512]{1,0:T(8,128)(2,1)} %get-tuple-element.58.refs_1_.refs_4_), channel_id=1, source_target_pairs={{0,16},{4,20},{8,24},{12,28},{16,0},{20,4},{24,8},{28,12},{1,17},{... | collective-permute-start | bytes 983048 | tf_op jit(solution)/shard_map/ppermute | solution.py:24
  28.1 12.5 %collective-permute-start.10 = (bf16[320,512]{1,0:T(8,128)(2,1)}, bf16[320,512]{1,0:T(8,128)(2,1)}, u32[]{:S(2)}, u32[]{:S(2)}) collective-permute-start(bf16[320,512]{1,0:T(8,128)(2,1)} %collective-permute-done.9.refs_3_), channel_id=1, source_target_pairs={{0,1},{1,0},{2,3},{3,2},{4,5},{5,4},{6,7},{7,6},{8,9},{9,8},{10,11... | collective-permute-start | bytes 983048 | tf_op jit(solution)/shard_map/ppermute | solution.py:24
  29.7 14.4 %collective-permute-start.12 = (bf16[320,512]{1,0:T(8,128)(2,1)}, bf16[320,512]{1,0:T(8,128)(2,1)}, u32[]{:S(2)}, u32[]{:S(2)}) collective-permute-start(bf16[320,512]{1,0:T(8,128)(2,1)} %collective-permute-done.11.refs_1_), channel_id=1, source_target_pairs={{0,1},{1,0},{2,3},{3,2},{4,5},{5,4},{6,7},{7,6},{8,9},{9,8},{10,11... | collective-permute-start | bytes 983048 | tf_op jit(solution)/shard_map/ppermute | solution.py:24
  30.5 19.1 %collective-permute-start.2 = (bf16[320,512]{1,0:T(8,128)(2,1)}, bf16[320,512]{1,0:T(8,128)(2,1)S(1)}, u32[]{:S(2)}, u32[]{:S(2)}) collective-permute-start(bf16[320,512]{1,0:T(8,128)(2,1)} %get-tuple-element.59.refs_1_.refs_0_), channel_id=1, source_target_pairs={{0,2},{1,3},{2,0},{3,1},{4,6},{5,7},{6,4},{7,5},{8,10},{9,11},{10,... | collective-permute-start | bytes 983048 | tf_op jit(solution)/shard_map/ppermute | solution.py:24
  31.0 25.9 %collective-permute-start.3 = (bf16[320,512]{1,0:T(8,128)(2,1)}, bf16[320,512]{1,0:T(8,128)(2,1)S(1)}, u32[]{:S(2)}, u32[]{:S(2)}) collective-permute-start(bf16[320,512]{1,0:T(8,128)(2,1)} %collective-permute-done.1.refs_2_), channel_id=1, source_target_pairs={{0,2},{1,3},{2,0},{3,1},{4,6},{5,7},{6,4},{7,5},{8,10},{9,11},{10,... | collective-permute-start | bytes 983048 | tf_op jit(solution)/shard_map/ppermute | solution.py:24
  40.1 15.3 %collective-permute-start.6 = (bf16[320,512]{1,0:T(8,128)(2,1)}, bf16[320,512]{1,0:T(8,128)(2,1)S(1)}, u32[]{:S(2)}, u32[]{:S(2)}) collective-permute-start(bf16[320,512]{1,0:T(8,128)(2,1)} %collective-permute-done.4.refs_1_), channel_id=1, source_target_pairs={{0,2},{1,3},{2,0},{3,1},{4,6},{5,7},{6,4},{7,5},{8,10},{9,11},{10,... | collective-permute-start | bytes 983048 | tf_op jit(solution)/shard_map/ppermute | solution.py:24
  40.7 25.4 %collective-permute-start.13 = (bf16[320,512]{1,0:T(8,128)(2,1)}, bf16[320,512]{1,0:T(8,128)(2,1)S(1)}, u32[]{:S(2)}, u32[]{:S(2)}) collective-permute-start(bf16[320,512]{1,0:T(8,128)(2,1)} %collective-permute-done.11.refs_1_), channel_id=1, source_target_pairs={{0,2},{1,3},{2,0},{3,1},{4,6},{5,7},{6,4},{7,5},{8,10},{9,11},{10,... | collective-permute-start | bytes 983048 | tf_op jit(solution)/shard_map/ppermute | solution.py:24
  44.1 22.7 %collective-permute-start.14 = (bf16[320,512]{1,0:T(8,128)(2,1)}, bf16[320,512]{1,0:T(8,128)(2,1)S(1)}, u32[]{:S(2)}, u32[]{:S(2)}) collective-permute-start(bf16[320,512]{1,0:T(8,128)(2,1)} %collective-permute-done.12.refs_2_), channel_id=1, source_target_pairs={{0,2},{1,3},{2,0},{3,1},{4,6},{5,7},{6,4},{7,5},{8,10},{9,11},{10,... | collective-permute-start | bytes 983048 | tf_op jit(solution)/shard_map/ppermute | solution.py:24
  44.6 1.1 copy-start.1
  45.7 11.2 %copy-start.2 = (f32[1280,1]{1,0:T(8,128)S(1)}, f32[1280,1]{1,0:T(8,128)}, u32[]{:S(2)}) copy-start(f32[1280,1]{1,0:T(8,128)} %broadcast_in_dim.16.refs_5_) | copy-start | bytes 15364
  49.5 23.3 %collective-permute-start.5 = (bf16[320,512]{1,0:T(8,128)(2,1)}, bf16[320,512]{1,0:T(8,128)(2,1)S(1)}, u32[]{:S(2)}, u32[]{:S(2)}) collective-permute-start(bf16[320,512]{1,0:T(8,128)(2,1)} %collective-permute-done.4.refs_1_), channel_id=1, source_target_pairs={{0,1},{1,0},{2,3},{3,2},{4,5},{5,4},{6,7},{7,6},{8,9},{9,8},{10,11... | collective-permute-start | bytes 983048 | tf_op jit(solution)/shard_map/ppermute | solution.py:24
  55.4 17.4 %collective-permute-start.7 = (bf16[320,512]{1,0:T(8,128)(2,1)S(1)}, bf16[320,512]{1,0:T(8,128)(2,1)S(1)}, u32[]{:S(2)}, u32[]{:S(2)}) collective-permute-start(bf16[320,512]{1,0:T(8,128)(2,1)S(1)} %collective-permute-done.6.refs_3_), channel_id=1, source_target_pairs={{0,1},{1,0},{2,3},{3,2},{4,5},{5,4},{6,7},{7,6},{8,9},{9,8},{10,11... | collective-permute-start | bytes 983048 | tf_op jit(solution)/shard_map/ppermute | solution.py:24
  77.4 3.9 %copy-start.7 = (s32[256,1]{0,1:T(1,128)S(1)}, s32[256,1]{0,1:T(1,128)}, u32[]{:S(2)}) copy-start(s32[256,1]{0,1:T(1,128)} %param.15) | copy-start | bytes 3076
  77.4 10.7 %collective-permute-start.19 = (bf16[320,512]{1,0:T(8,128)(2,1)S(1)}, bf16[320,512]{1,0:T(8,128)(2,1)S(1)}, u32[]{:S(2)}, u32[]{:S(2)}) collective-permute-start(bf16[320,512]{1,0:T(8,128)(2,1)S(1)} %get-tuple-element.51), channel_id=1, source_target_pairs={{0,2},{1,3},{2,0},{3,1},{4,6},{5,7},{6,4},{7,5},{8,10},{9,11},{10,... | collective-permute-start | bytes 983048 | tf_op jit(solution)/shard_map/ppermute | solution.py:24
  79.7 10.7 %collective-permute-start.16 = (bf16[320,512]{1,0:T(8,128)(2,1)S(1)}, bf16[320,512]{1,0:T(8,128)(2,1)S(1)}, u32[]{:S(2)}, u32[]{:S(2)}) collective-permute-start(bf16[320,512]{1,0:T(8,128)(2,1)S(1)} %get-tuple-element.47), channel_id=1, source_target_pairs={{0,1},{1,0},{2,3},{3,2},{4,5},{5,4},{6,7},{7,6},{8,9},{9,8},{10,11... | collective-permute-start | bytes 983048 | tf_op jit(solution)/shard_map/ppermute | solution.py:24
  81.5 13.7 %collective-permute-start.18 = (bf16[320,512]{1,0:T(8,128)(2,1)S(1)}, bf16[320,512]{1,0:T(8,128)(2,1)S(1)}, u32[]{:S(2)}, u32[]{:S(2)}) collective-permute-start(bf16[320,512]{1,0:T(8,128)(2,1)S(1)} %get-tuple-element.49), channel_id=1, source_target_pairs={{0,2},{1,3},{2,0},{3,1},{4,6},{5,7},{6,4},{7,5},{8,10},{9,11},{10,... | collective-permute-start | bytes 983048 | tf_op jit(solution)/shard_map/ppermute | solution.py:24
  83.0 14.3 %collective-permute-start.15 = (bf16[320,512]{1,0:T(8,128)(2,1)S(1)}, bf16[320,512]{1,0:T(8,128)(2,1)S(1)}, u32[]{:S(2)}, u32[]{:S(2)}) collective-permute-start(bf16[320,512]{1,0:T(8,128)(2,1)S(1)} %get-tuple-element.45), channel_id=1, source_target_pairs={{0,1},{1,0},{2,3},{3,2},{4,5},{5,4},{6,7},{7,6},{8,9},{9,8},{10,11... | collective-permute-start | bytes 983048 | tf_op jit(solution)/shard_map/ppermute | solution.py:24
  88.1 25.7 %copy-start.3 = (bf16[4,320,1280]{2,1,0:T(8,128)(2,1)S(1)}, bf16[4,320,1280]{2,1,0:T(8,128)(2,1)}, u32[]{:S(2)}) copy-start(bf16[4,320,1280]{2,1,0:T(8,128)(2,1)} %param.14) | copy-start | bytes 9830404
  88.2 15.1 %collective-permute-start.20 = (bf16[320,512]{1,0:T(8,128)(2,1)S(1)}, bf16[320,512]{1,0:T(8,128)(2,1)S(1)}, u32[]{:S(2)}, u32[]{:S(2)}) collective-permute-start(bf16[320,512]{1,0:T(8,128)(2,1)S(1)} %add_convert_fusion), channel_id=1, source_target_pairs={{0,1},{1,0},{2,3},{3,2},{4,5},{5,4},{6,7},{7,6},{8,9},{9,8},{10,11... | collective-permute-start | bytes 983048 | tf_op jit(solution)/shard_map/ppermute | solution.py:24
  90.4 12.9 %collective-permute-start.17 = (bf16[320,512]{1,0:T(8,128)(2,1)S(1)}, bf16[320,512]{1,0:T(8,128)(2,1)S(1)}, u32[]{:S(2)}, u32[]{:S(2)}) collective-permute-start(bf16[320,512]{1,0:T(8,128)(2,1)S(1)} %add_convert_fusion.1), channel_id=1, source_target_pairs={{0,2},{1,3},{2,0},{3,1},{4,6},{5,7},{6,4},{7,5},{8,10},{9,11},{10,... | collective-permute-start | bytes 983048 | tf_op jit(solution)/shard_map/ppermute | solution.py:24
  106.0 4.4 %collective-permute-start.21 = (f32[8,1024]{1,0:T(8,128)S(1)}, f32[8,1024]{1,0:T(8,128)S(1)}, u32[]{:S(2)}, u32[]{:S(2)}) collective-permute-start(f32[8,1024]{1,0:T(8,128)S(1)} %get-tuple-element.53.refs_0_), channel_id=1, source_target_pairs={{0,1},{1,0},{2,3},{3,2},{4,5},{5,4},{6,7},{7,6},{8,9},{9,8},{10,11... | collective-permute-start | bytes 98312 | tf_op jit(solution)/shard_map/ppermute | solution.py:24
  107.5 4.2 %collective-permute-start.22 = (f32[8,1024]{1,0:T(8,128)S(1)}, f32[8,1024]{1,0:T(8,128)S(1)}, u32[]{:S(2)}, u32[]{:S(2)}) collective-permute-start(f32[8,1024]{1,0:T(8,128)S(1)} %get-tuple-element.53.refs_0_), channel_id=1, source_target_pairs={{0,2},{1,3},{2,0},{3,1},{4,6},{5,7},{6,4},{7,5},{8,10},{9,11},{10,... | collective-permute-start | bytes 98312 | tf_op jit(solution)/shard_map/ppermute | solution.py:24
  109.0 4.8 %collective-permute-start.23 = (f32[8,1024]{1,0:T(8,128)S(1)}, f32[8,1024]{1,0:T(8,128)S(1)}, u32[]{:S(2)}, u32[]{:S(2)}) collective-permute-start(f32[8,1024]{1,0:T(8,128)S(1)} %get-tuple-element.53.refs_0_), channel_id=1, source_target_pairs={{0,3},{1,2},{2,1},{3,0},{4,7},{5,6},{6,5},{7,4},{8,11},{9,10},{10,... | collective-permute-start | bytes 98312 | tf_op jit(solution)/shard_map/ppermute | solution.py:24
  113.8 1.0 copy-start.4
  114.8 1.1 copy-start.5
  118.6 6.3 %collective-permute-start.24 = (bf16[256,320]{1,0:T(8,128)(2,1)S(1)}, bf16[256,320]{1,0:T(8,128)(2,1)S(1)}, u32[]{:S(2)}, u32[]{:S(2)}) collective-permute-start(bf16[256,320]{1,0:T(8,128)(2,1)S(1)} %get-tuple-element.55), channel_id=1, source_target_pairs={{0,1},{1,0},{2,3},{3,2},{4,5},{5,4},{6,7},{7,6},{8,9},{9,8},{10,11... | collective-permute-start | bytes 491528 | tf_op jit(solution)/shard_map/ppermute | solution.py:24
  119.2 8.0 %collective-permute-start.25 = (bf16[256,320]{1,0:T(8,128)(2,1)S(1)}, bf16[256,320]{1,0:T(8,128)(2,1)S(1)}, u32[]{:S(2)}, u32[]{:S(2)}) collective-permute-start(bf16[256,320]{1,0:T(8,128)(2,1)S(1)} %get-tuple-element.56), channel_id=1, source_target_pairs={{0,2},{1,3},{2,0},{3,1},{4,6},{5,7},{6,4},{7,5},{8,10},{9,11},{10,... | collective-permute-start | bytes 491528 | tf_op jit(solution)/shard_map/ppermute | solution.py:24
  119.7 7.6 %collective-permute-start.26 = (bf16[256,320]{1,0:T(8,128)(2,1)S(1)}, bf16[256,320]{1,0:T(8,128)(2,1)S(1)}, u32[]{:S(2)}, u32[]{:S(2)}) collective-permute-start(bf16[256,320]{1,0:T(8,128)(2,1)S(1)} %get-tuple-element.57), channel_id=1, source_target_pairs={{0,3},{1,2},{2,1},{3,0},{4,7},{5,6},{6,5},{7,4},{8,11},{9,10},{10,... | collective-permute-start | bytes 491528 | tf_op jit(solution)/shard_map/ppermute | solution.py:24

commit v3 on v2

v3 whole, which is shorter than its diff:
```python
import functools
import math

import jax
import jax.numpy as jnp
from jax import lax
from jax.experimental import pallas as pl
from jax.experimental.pallas import tpu as pltpu
from jax.sharding import PartitionSpec as P

HD = 80
HEAD_ROWS = 96
PAD = 128
FAR = 2.0**100
EPS = 1e-06
BLOCK = 256
BF = jnp.bfloat16
F32 = jnp.float32
VM = pl.BlockSpec(memory_space=pltpu.VMEM)
SM = pl.BlockSpec(memory_space=pltpu.SMEM)
HB = pl.BlockSpec(memory_space=pltpu.HBM)


def hop(x, axis, distance):
    return lax.ppermute(x, axis, [(i, i ^ distance) for i in range(lax.axis_size(axis))])


def nearby(count):
    if count == 1:
        return [0]
    me = lax.axis_index("tp")
    return [me ^ k for k in range(count)]


def call(body, name, args, smem, outs, scratch, loose=()):
    def place(i):
        if i < smem:
            return SM
        return HB if i in loose else VM

    return pl.pallas_call(
        body,
        in_specs=[place(i) for i in range(len(args))],
        out_specs=[VM for _ in outs],
        out_shape=[jax.ShapeDtypeStruct(s, d) for s, d in outs],
        scratch_shapes=scratch,
        compiler_params=pltpu.CompilerParams(vmem_limit_bytes=16 << 20),
        cost_estimate=pl.CostEstimate(flops=0, bytes_accessed=0, transcendentals=0),
        name=name,
    )(*args)


def prepare_body(w, gain, merge_gain, owner, w_back, gain_wide, merge_wide, dispatch):
    full = w.shape[1]
    for lo in range(0, full, PAD):
        at = slice(lo, lo + PAD)
        w_back[at, :] = w[:, at].astype(F32).T.astype(BF)
        gain_wide[at, :] = jnp.broadcast_to(gain[:, at], (PAD, PAD)).T
        merge_wide[at, :] = jnp.broadcast_to(merge_gain[:, at], (PAD, PAD)).T
    slots, count = dispatch.shape
    groups = lax.axis_size("grp")
    named = owner[...]
    onehot = jnp.broadcast_to(named, (groups, count)) == lax.broadcasted_iota(
        jnp.int32, (groups, count), 0
    )
    before = lax.broadcasted_iota(jnp.int32, (count, count), 0) < lax.broadcasted_iota(
        jnp.int32, (count, count), 1
    )
    earlier = jnp.dot(
        jnp.where(onehot, 1.0, 0.0).astype(BF),
        jnp.where(before, 1.0, 0.0).astype(BF),
        preferred_element_type=F32,
    )
    slot = jnp.sum(jnp.where(onehot, earlier, 0.0), axis=0, keepdims=True).astype(jnp.int32)
    goal = named * (slots // groups) + slot
    dispatch[...] = jnp.where(
        lax.broadcasted_iota(jnp.int32, (slots, count), 0)
        == jnp.broadcast_to(goal, (slots, count)),
        1.0,
        0.0,
    ).astype(BF)


def prepare(w, gain, merge_gain, owner, slots):
    width, full = w.shape
    count = owner.shape[0]
    return call(
        prepare_body,
        "prepare",
        [w, gain[None, :], merge_gain[None, :], owner.reshape(1, count)],
        0,
        [((full, width), BF), ((full, PAD), F32), ((full, PAD), F32), ((slots, count), BF)],
        [],
    )


def split_body(spans, source, *refs):
    outs, sem = refs[:-1], refs[-1]
    copies = [
        pltpu.make_async_copy(source.at[:, lo:hi], out, sem.at[i])
        for i, ((lo, hi), out) in enumerate(zip(spans, outs))
    ]
    for copy in copies:
        copy.start()
    for copy in copies:
        copy.wait()


def split(x, spans):
    return call(
        functools.partial(split_body, spans),
        "split",
        [x],
        0,
        [((x.shape[0], hi - lo), x.dtype) for lo, hi in spans],
        [pltpu.SemaphoreType.DMA((len(spans),))],
        loose=(0,),
    )


def project_body(places, n_parts, kinds, scale, id_start, *refs):
    count = len(places)
    sources = refs[:count]
    gain, w, ids = refs[count : 3 + count]
    outs = refs[3 + count : 3 + count + len(kinds)]
    order = nearby(n_parts)
    normed = refs[-1]
    full, rows = normed.shape
    width = full // n_parts
    heads = w.shape[0] // (3 * HD)

    def load(part, col):
        found = []
        for source, (own, _, r_lo) in zip(sources, places):
            if own == part and r_lo <= col < r_lo + source.shape[1]:
                found.append(source[:, col - r_lo : col - r_lo + PAD].astype(F32))
        return found[0] if len(found) == 1 else jnp.concatenate(found, axis=0)

    each = heads * HD
    line = lax.broadcasted_iota(jnp.int32, (HEAD_ROWS - HD, BLOCK), 0)
    for start in range(0, rows, BLOCK):
        for lo in range(start, start + BLOCK, PAD):
            here = slice(lo, lo + PAD)
            base = load(0, lo)[0:1, :]
            moved = 0.0
            square = 0.0
            for k in range(n_parts):
                off = load(k, lo) - base
                moved = moved + jnp.sum(off, axis=0, keepdims=True)
                square = square + jnp.sum(off * off, axis=0, keepdims=True)
            moved = moved * (1.0 / full)
            spread = jnp.maximum(square * (1.0 / full) - moved * moved, 0.0)
            center = base + moved
            inv = lax.rsqrt(spread + EPS)
            for k in range(n_parts):
                at = pl.ds(pl.multiple_of(order[k] * width, 16), width)
                normed[at, here] = ((load(k, lo) - center) * inv * gain[at, :]).astype(BF)
        there = slice(start, start + BLOCK)
        near_ids = ids[0:1, id_start + start : id_start + start + BLOCK]
        bits = (jnp.broadcast_to(near_ids, line.shape) >> (line >> 1)) & 1
        hit = bits == (line & 1)
        product = jnp.dot(
            w[kinds[0] * each : (kinds[-1] + 1) * each, :],
            normed[:, there],
            preferred_element_type=F32,
        )
        for i, (kind, out) in enumerate(zip(kinds, outs)):
            acc = product[i * each : (i + 1) * each, :]
            if kind == 0:
                acc = acc * scale
                extra = jnp.where(hit, 0.0, -FAR)
            elif kind == 1:
                extra = jnp.where(hit, 1.0, 0.0)
            else:
                extra = jnp.where(line == 0, 1.0, 0.0)
            for h in range(heads):
                piece = acc[h * HD : (h + 1) * HD, :]
                if kind == 1:
                    tall = jnp.concatenate(
                        [piece, extra, jnp.zeros((PAD - HEAD_ROWS, BLOCK), F32)], axis=0
                    )
                    out[there, h * PAD : (h + 1) * PAD] = tall.T.astype(BF)
                else:
                    lo = h * HEAD_ROWS
                    out[lo : lo + HD, there] = piece.astype(BF)
                    out[lo + HD : lo + HEAD_ROWS, there] = extra.astype(BF)


def project(pieces, n_parts, rows, gain, w, ids, kinds, id_start):
    full = gain.shape[0]
    heads = w.shape[0] // (3 * HD)
    shape = lambda kind: (
        (rows, heads * PAD) if kind == 1 else (heads * HEAD_ROWS, rows),
        BF,
    )
    arrays = [x for x, *_ in pieces]
    places = tuple(tuple(p[1:]) for p in pieces)
    return call(
        functools.partial(
            project_body, places, n_parts, kinds, HD**-0.5 * math.log2(math.e), id_start
        ),
        "project",
        [*arrays, gain, w, ids],
        0,
        [shape(kind) for kind in kinds],
        [pltpu.VMEM((full, rows), BF)],
    )


def visit(q, kr, vr, lo, size, acc, top, cols):
    heads = q.shape[0] // HEAD_ROWS
    scores = [
        jnp.dot(
            kr[lo : lo + size, h * PAD : h * PAD + HEAD_ROWS],
            q[h * HEAD_ROWS : (h + 1) * HEAD_ROWS, :],
            preferred_element_type=F32,
        )
        for h in range(heads)
    ]
    for h, s in enumerate(scores):
        at = slice(h * HEAD_ROWS, (h + 1) * HEAD_ROWS)
        old = top[h : h + 1, cols]
        new = jnp.maximum(old, jnp.max(s, axis=0, keepdims=True))
        p = jnp.exp2(s - new).astype(BF)
        acc[at, cols] = acc[at, cols] * jnp.exp2(old - new) + jnp.dot(
            vr[at, lo : lo + size], p, preferred_element_type=F32
        )
        top[h : h + 1, cols] = new


def sweep(block, q_ids, k_ids, k_start, q, q_start, kr, vr, acc, top):
    for col in range(0, acc.shape[1], block):
        row = q_start + col
        for lo in range(0, kr.shape[0], BLOCK):
            meets = (k_ids[k_start + lo] <= q_ids[row + block - 1]) & (
                k_ids[k_start + lo + BLOCK - 1] >= q_ids[row]
            )

            @pl.when(meets)
            def _(col=col, row=row, lo=lo):
                visit(
                    q[:, row : row + block], kr, vr, lo, BLOCK, acc, top,
                    slice(col, col + block),
                )


def near_body(block, q_ids, q, k, v, acc, top):
    acc[...] = jnp.zeros_like(acc)
    top[...] = jnp.full_like(top, -1e20)
    sweep(block, q_ids, q_ids, 0, q, 0, k, v, acc, top)


def near(q_ids, q, k, v):
    wide, rows = q.shape
    heads = wide // HEAD_ROWS
    return call(
        functools.partial(near_body, 2 * BLOCK),
        "near",
        [q_ids, q, k, v],
        1,
        [((wide, rows), F32), ((8, rows), F32)],
        [],
    )


def middle_body(start, q_ids, k_ids, q, k, v, acc_in, top_in, acc, top):
    acc[...] = acc_in[...]
    top[...] = top_in[...]
    sweep(BLOCK, q_ids, k_ids, start, q, 0, k, v, acc, top)


def middle(q_ids, k_ids, q, k, v, acc, top, start):
    wide, rows = q.shape
    heads = wide // HEAD_ROWS
    return call(
        functools.partial(middle_body, start),
        "middle",
        [q_ids, k_ids, q, k, v, acc, top],
        2,
        [(acc.shape, F32), (top.shape, F32)],
        [],
    )


def last_body(n_out, start, k_start, q_ids, k_ids, q, k, v, acc_in, top_in, w, *refs):
    outs = refs[:n_out]
    acc, top, ctx = refs[n_out:]
    rows = acc.shape[1]
    heads = q.shape[0] // HEAD_ROWS
    acc[...] = acc_in[:, start : start + rows]
    top[...] = top_in[:, start : start + rows]
    sweep(BLOCK, q_ids, k_ids, k_start, q, start, k, v, acc, top)
    for h in range(heads):
        lo = h * HEAD_ROWS
        ctx[h * HD : (h + 1) * HD, :] = (
            acc[lo : lo + HD, :] / acc[lo + HD : lo + HD + 1, :]
        ).astype(BF)
    width = outs[0].shape[0]
    order = nearby(n_out)
    for j in reversed(range(n_out)):
        at = pl.ds(pl.multiple_of(order[j] * width, 16), width)
        outs[j][...] = jnp.dot(w[at, :], ctx[...], preferred_element_type=F32).astype(BF)


def last(q_ids, k_ids, q, k, v, acc, top, w, n_out, start, rows, k_start):
    wide = q.shape[0]
    heads = wide // HEAD_ROWS
    full = w.shape[0]
    return call(
        functools.partial(last_body, n_out, start, k_start),
        "last",
        [q_ids, k_ids, q, k, v, acc, top, w],
        2,
        [((full // n_out, rows), BF) for _ in range(n_out)],
        [
            pltpu.VMEM((wide, rows), F32),
            pltpu.VMEM((8, rows), F32),
            pltpu.VMEM((heads * HD, rows), BF),
        ],
    )


def hidden_body(n_half, tokens, *refs):
    hidden, again, stats = refs[-3:]
    inputs = refs[:-3]
    each = len(inputs) // n_half
    rows = hidden.shape[1] // n_half
    for i in range(n_half):
        for lo in range(0, rows, PAD):
            at = slice(i * rows + lo, i * rows + lo + PAD)
            total = tokens[:, at].astype(F32)
            for g in inputs[i * each : (i + 1) * each]:
                total = total + g[:, lo : lo + PAD].astype(F32)
            rounded = total.astype(BF)
            hidden[:, at] = rounded
            again[:, at] = rounded
            values = rounded.astype(F32)
            center = jnp.mean(values, axis=0, keepdims=True)
            spread = jnp.mean((values - center) ** 2, axis=0, keepdims=True)
            stats[:, at] = jnp.concatenate(
                [center, spread, jnp.zeros((6, PAD), F32)], axis=0
            )


def hidden_sum(tokens, groups):
    width, count = tokens.shape
    return call(
        functools.partial(hidden_body, len(groups)),
        "hidden",
        [tokens, *[x for g in groups for x in g]],
        0,
        [((width, count), BF), ((width, count), BF), ((8, count), F32)],
        [],
    )


def merge_body(n_stats, n_out, source, *refs):
    stats = refs[:n_stats]
    gain, w = refs[n_stats : n_stats + 2]
    outs = refs[n_stats + 2 : n_stats + 2 + n_out]
    scaled, blocks, pick = refs[-3:]
    width, rows = source.shape
    me = lax.axis_index("tp")
    own_gain = gain[pl.ds(pl.multiple_of(me * width, 16), width), :]
    row = lax.broadcasted_iota(jnp.int32, pick.shape, 0)
    col = lax.broadcasted_iota(jnp.int32, pick.shape, 1)
    fourth = pick.shape[0] // 4
    pick[...] = jnp.where(4 * (row % fourth) + row // fourth == col, 1.0, 0.0).astype(BF)
    for lo in range(0, rows, PAD):
        at = slice(lo, lo + PAD)
        means = [s[0:1, at] for s in stats]
        center = sum(means) * (1.0 / n_stats)
        spread = sum(
            s[1:2, at] + (m - center) ** 2 for s, m in zip(stats, means)
        ) * (1.0 / n_stats)
        inv = lax.rsqrt(spread + EPS)
        scaled[:, at] = ((source[:, at].astype(F32) - center) * inv * own_gain).astype(BF)
    size = pick.shape[0]
    quarter = size // 4
    for lo in range(0, rows, size):
        picked = lax.dot_general(
            pick[...],
            scaled[:, lo : lo + size],
            (((1,), (1,)), ((), ())),
            preferred_element_type=F32,
        ).astype(BF)
        for j in range(4):
            blocks[lo // 4 : lo // 4 + quarter, j * width : (j + 1) * width] = picked[
                j * quarter : (j + 1) * quarter, :
            ]
    terms = jnp.dot(blocks[...], w[...], preferred_element_type=F32)
    if n_out == 1:
        outs[0][...] = terms.astype(BF)
        return
    for case in range(n_out):

        @pl.when(me == case)
        def _(case=case):
            for k in range(n_out):
                lo = (case ^ k) * width
                outs[k][...] = terms[:, lo : lo + width].astype(BF)


def merge(hidden, stats, gain, w, n_out):
    width, rows = hidden.shape
    full = w.shape[1]
    return call(
        functools.partial(merge_body, len(stats), n_out),
        "merge",
        [hidden, *stats, gain, w],
        0,
        [((rows // 4, full // n_out), BF) for _ in range(n_out)],
        [
            pltpu.VMEM((width, rows), BF),
            pltpu.VMEM((rows // 4, 4 * width), BF),
            pltpu.VMEM((rows // 2, rows // 2), BF),
        ],
    )


def place_body(n_in, crossing, *refs):
    merged = sum(r[...].astype(F32) for r in refs[:n_in]).astype(BF)
    dispatch = refs[n_in]
    placed = jnp.dot(dispatch[...], merged, preferred_element_type=F32).astype(BF)
    if not crossing:
        refs[-1][...] = placed
        return
    whole = refs[-1]
    whole[...] = placed
    group = lax.axis_index("grp")
    for k, out in enumerate(refs[n_in + 1 : -1]):
        cap = out.shape[0] // 2
        for e in range(2):
            at = pl.ds(pl.multiple_of((group ^ (2 * k + e)) * cap, 16), cap)
            out[e * cap : (e + 1) * cap, :] = whole[at, :]


def place(terms, dispatch, n_out):
    slots = dispatch.shape[0]
    width = terms[0].shape[1]
    return call(
        functools.partial(place_body, len(terms), n_out > 1),
        "place",
        [*terms, dispatch],
        0,
        [((slots // n_out, width), BF) for _ in range(n_out)],
        [pltpu.VMEM((slots, width), BF)] if n_out > 1 else [],
    )


def settle_body(*refs):
    crossed, out = refs[-2:]
    cap = out.shape[1]
    group = lax.axis_index("grp")
    for k, block in enumerate(refs[:-2]):
        out[pl.ds(group ^ (2 * k), 1)] = block[:cap, :][None]
        out[pl.ds(group ^ (2 * k + 1), 1)] = crossed[k * cap : (k + 1) * cap, :][None]


def settle(blocks, crossed, cap):
    width = crossed.shape[1]
    return call(
        settle_body,
        "settle",
        [*blocks, crossed],
        0,
        [((2 * len(blocks), cap, width), BF)],
        [],
    )[0]


def shards(tokens, segment, ln_gain, w_qkv, w_out, merge_gain, w_merge, owner):
    row_count, local_width = tokens.shape
    tp_count = lax.axis_size("tp")
    grp_count = lax.axis_size("grp")
    full_width = local_width * tp_count
    half = row_count // 2
    square = tp_count == 4
    partner = grp_count // 2
    n_out = 4 if square else 1
    after = lambda x, *first: lax.optimization_barrier((x, *first))[0]

    tall = tokens.T
    spans = ((0, half), (half, row_count))
    far_segment = hop(segment, "grp", partner)
    merged_count = row_count // 4
    cap_slots = max(2, merged_count // grp_count * 2)
    w_back, gain, merge_wide, dispatch = prepare(
        w_out, ln_gain, merge_gain, owner, grp_count * cap_slots
    )
    w_in = jnp.swapaxes(w_qkv, 1, 2).reshape(3 * local_width, full_width)
    w_blocks = w_merge.reshape(4 * local_width, full_width)

    def keys_of(pieces, start):
        return project(pieces, n_out, half, gain, w_in, far_segment[None, :], (1, 2), start)

    def own_of(pieces):
        return project(
            pieces, n_out, row_count, gain, w_in, segment[None, :], (0, 1, 2), 0
        )

    if square:
        mid = local_width // 2
        a = hop(tall, "tp", 1)
        b = hop(tall, "tp", 2)
        h0, h1 = split(tall, spans)
        z0 = hop(h0, "grp", partner)
        c = hop(after(a, w_back)[:mid], "tp", 2)
        d = hop(b[mid:], "tp", 1)
        z1 = hop(after(h1, z0), "grp", partner)
        q, k, v = own_of(
            [(tall, 0, 0, 0), (a, 1, 0, 0), (b, 2, 0, 0), (c, 3, 0, 0), (d, 3, mid, 0)]
        )
        z0 = after(z0, c, d)
        za0 = hop(z0, "tp", 1)
        zb0 = hop(z0, "tp", 2)
        z1 = after(z1, k, za0, zb0)
        za1 = hop(z1, "tp", 1)
        zb1 = hop(z1, "tp", 2)
        ta0, tb0 = za0[:mid], zb0[mid:]
        zc0 = hop(ta0, "tp", 2)
        zd0 = hop(tb0, "tp", 1)
        acc, top = near(segment, after(q, z1, ta0, tb0), k, v)
        za1, zb1, far_segment = lax.optimization_barrier((za1, zb1, far_segment, top))[:3]
        ta1, tb1 = za1[:mid], zb1[mid:]
        zc1 = hop(ta1, "tp", 2)
        zd1 = hop(tb1, "tp", 1)
        far0 = keys_of(
            [(z0, 0, 0, 0), (za0, 1, 0, 0), (zb0, 2, 0, 0), (zc0, 3, 0, 0), (zd0, 3, mid, 0)],
            0,
        )
        acc, top = middle(segment, far_segment, q, *far0, acc, top, 0)
        far1 = keys_of(
            [(z1, 0, 0, 0), (za1, 1, 0, 0), (zb1, 2, 0, 0), (zc1, 3, 0, 0), (zd1, 3, mid, 0)],
            half,
        )
    else:
        q, k, v = own_of([(lax.all_gather(tall, "tp", axis=0, tiled=True), 0, 0, 0)])
        far_whole = lax.all_gather(hop(tall, "grp", partner), "tp", axis=0, tiled=True)
        far0, far1 = [keys_of([(far_whole[:, lo:hi], 0, 0, 0)], lo) for lo, hi in spans]
        acc, top = near(segment, q, k, v)
        acc, top = middle(segment, far_segment, q, *far0, acc, top, 0)

    crossing = grp_count == 8
    terms = [
        last(segment, far_segment, q, *far1, acc, top, w_back, n_out, start, half, half)
        for start in (0, half)
    ]

    if square:
        groups = []
        for i, (side_hop, next_hop) in enumerate(((1, 2), (2, 1))):
            corner = hop(terms[i][3], "tp", side_hop)
            side = hop(terms[i][side_hop], "tp", side_hop)
            passed = (terms[i][next_hop].astype(F32) + corner.astype(F32)).astype(BF)
            onward = hop(passed, "tp", next_hop)
            groups.append((terms[i][0], side, onward))
    else:
        groups = [
            (lax.psum_scatter(t[0], "tp", scatter_dimension=0, tiled=True),) for t in terms
        ]
    hidden_out, hidden, stats = hidden_sum(tall, groups)
    if square:
        all_stats = [stats] + [hop(stats, "tp", n) for n in (1, 2, 3)]
    else:
        gathered = lax.all_gather(stats, "tp")
        all_stats = [gathered[n] for n in range(tp_count)]
    merge_terms = merge(hidden, all_stats, merge_wide, w_blocks, n_out)
    if square:
        received = [merge_terms[0]] + [hop(merge_terms[n], "tp", n) for n in (1, 2, 3)]
    else:
        received = [lax.psum_scatter(merge_terms[0], "tp", scatter_dimension=1, tiled=True)]
    if crossing:
        blocks = place(received, dispatch, grp_count // 2)
        blocks = [blocks[0]] + [
            hop(block, "grp", 2 * n) for n, block in enumerate(blocks) if n > 0
        ]
        crossed = hop(
            jnp.concatenate([block[cap_slots:] for block in blocks], axis=0), "grp", 1
        )
        routed = settle(blocks, crossed, cap_slots)
    else:
        outgoing = place(received, dispatch, 1)[0].reshape(grp_count, cap_slots, local_width)
        routed = lax.all_to_all(outgoing, "grp", split_axis=0, concat_axis=0, tiled=True)
    return (hidden_out.T, routed[None])


def solution(mesh):
    return jax.shard_map(
        shards,
        mesh=mesh,
        in_specs=(
            P("grp", "tp"),
            P("grp"),
            P(),
            P(None, None, "tp"),
            P("tp", None),
            P(),
            P(None, "tp", None),
            P("grp", None),
        ),
        out_specs=(P("grp", "tp"), P("grp", None, None, "tp")),
        check_vma=False,
    )
```

time: 146 us -> 121 us (0.83)
  blocking collectives: 16.4 us -> 0 us
  waiting for transfers between devices: 51 us -> 42 us
  starting transfers between devices: 32.1 us -> 40.9 us
  local copies, waits for them, and re-layouts: 12 us -> 6.26 us
  Pallas kernels: 30.9 us -> 28.7 us
    all_to_all x1 -> x0, blocking collectives: 16.4 us -> none  [shards(): lax.all_to_all(outgoing, 'grp', split_axis=0, concat_axis=0, tiled=True)]
    ppermute x27 -> x31, waiting for transfers between devices: 51 us -> 42 us  [hop(): lax.ppermute(x, axis, [(i, i ^ distance) for i in range(lax.axis_size(axi...]
    ppermute x27 -> x31, starting transfers between devices: 32.1 us -> 40.9 us  [hop(): lax.ppermute(x, axis, [(i, i ^ distance) for i in range(lax.axis_size(axi...]
    slice x5 -> x10, local copies, waits for them, and re-layouts: 3.82 us -> 0.11 us  [the longest x2 0.02 us: shards(): ta1, tb1 = (za1[:mid], zb1[mid:])]
    pallas_call x11 -> x13, Pallas kernels: 30.9 us -> 28.7 us  [call(): pl.pallas_call(body, in_specs=[place(i) for i in range(len(args))], out_s...]
  transfers between devices with their start and end apart: 27 -> 31, of which waited for: 14 -> 20; matrix products, arithmetic and copies ran while one was open for 5% -> 1% of each run, Pallas kernels for 14% -> 17%
where the time goes in v3:
time: 121 us; the launch traced here: 119 us
  waiting for transfers between devices  42 us (35%)
  starting transfers between devices  40.9 us (34%)
  Pallas kernels  28.7 us (24%)
  local copies, waits for them, and re-layouts  6.26 us (5%)
    ppermute x31, waiting for transfers between devices, hop(): lax.ppermute(x, axis, [(i, i ^ distance) for i in range(lax.axis_size(axi...  42 us
    ppermute x31, starting transfers between devices, hop(): lax.ppermute(x, axis, [(i, i ^ distance) for i in range(lax.axis_size(axi...  40.9 us
    pallas_call x13, Pallas kernels, call(): pl.pallas_call(body, in_specs=[place(i) for i in range(len(args))], out_s...  28.7 us
    unnamed x18, local copies, waits for them, and re-layouts  4.74 us
  transfers between devices with their start and end apart: 31, of which 20 were waited for; matrix products, arithmetic and copies ran while one was open for 1% of the time, Pallas kernels for 17%

profile of v3, /device:TPU:0, one launch (start us, length us, event | category | flops | bytes accessed | tf_op | source)
XLA Modules:
  0.0 118.9 jit_solution(6525197719193865438)
XLA Ops:
  0.6 3.0 %collective-permute-start.2 = (bf16[320,1024]{1,0:T(8,128)(2,1)}, bf16[320,1024]{1,0:T(8,128)(2,1)S(1)}, u32[]{:S(2)}, u32[]{:S(2)}) collective-permute-start(bf16[320,1024]{1,0:T(8,128)(2,1)} %bitcast.13), channel_id=1, source_target_pairs={{0,1},{1,0},{2,3},{3,2},{4,5},{5,4},{6,7},{7,6},{8,9},{9,8},{10,11... | collective-permute-start | bytes 1966088 | tf_op jit(solution)/shard_map/ppermute | solution.py:25
  3.6 1.5 %collective-permute-start.3 = (bf16[320,1024]{1,0:T(8,128)(2,1)}, bf16[320,1024]{1,0:T(8,128)(2,1)S(1)}, u32[]{:S(2)}, u32[]{:S(2)}) collective-permute-start(bf16[320,1024]{1,0:T(8,128)(2,1)} %bitcast.14), channel_id=1, source_target_pairs={{0,2},{1,3},{2,0},{3,1},{4,6},{5,7},{6,4},{7,5},{8,10},{9,11},{10,... | collective-permute-start | bytes 1966088 | tf_op jit(solution)/shard_map/ppermute | solution.py:25
  5.2 1.1 copy-done.1
  6.4 2.7 %collective-permute-start = (bf16[320,512]{1,0:T(8,128)(2,1)S(1)}, bf16[320,512]{1,0:T(8,128)(2,1)S(1)}, u32[]{:S(2)}, u32[]{:S(2)}) collective-permute-start(bf16[320,512]{1,0:T(8,128)(2,1)S(1)} %get-tuple-element.47), channel_id=1, source_target_pairs={{0,16},{4,20},{8,24},{12,28},{16,0},{20,4},{24,8},{28,12},{1,17},{... | collective-permute-start | bytes 983048 | tf_op jit(solution)/shard_map/ppermute | solution.py:25
  9.0 0.7 broadcast_in_dim.16.gain
  9.7 0.7 broadcast_in_dim.17.merge_gain
  10.4 1.1 copy-done.5
  11.6 0.7 copy-done.8
  12.2 0.7 prepare.1
  13.0 5.6 %collective-permute-done.2.refs_1_ = bf16[320,1024]{1,0:T(8,128)(2,1)S(1)} collective-permute-done((bf16[320,1024]{1,0:T(8,128)(2,1)}, bf16[320,1024]{1,0:T(8,128)(2,1)S(1)}, u32[]{:S(2)}, u32[]{:S(2)}) %collective-permute-start.2) | collective-permute-done | bytes 655392 | tf_op jit(solution)/shard_map/ppermute | solution.py:25
  18.6 1.8 %collective-permute-start.4 = (bf16[160,1024]{1,0:T(8,128)(2,1)S(1)}, bf16[160,1024]{1,0:T(8,128)(2,1)S(1)}, u32[]{:S(2)}, u32[]{:S(2)}) collective-permute-start(bf16[160,1024]{1,0:T(8,128)(2,1)S(1)} %slice.30), channel_id=1, source_target_pairs={{0,2},{1,3},{2,0},{3,1},{4,6},{5,7},{6,4},{7,5},{8,10},{9,11},{10,... | collective-permute-start | bytes 983048 | tf_op jit(solution)/shard_map/ppermute | solution.py:25
  20.5 1.6 %collective-permute-start.5 = (bf16[160,1024]{1,0:T(8,128)(2,1)S(1)}, bf16[160,1024]{1,0:T(8,128)(2,1)S(1)}, u32[]{:S(2)}, u32[]{:S(2)}) collective-permute-start(bf16[160,1024]{1,0:T(8,128)(2,1)S(1)} %slice.40), channel_id=1, source_target_pairs={{0,1},{1,0},{2,3},{3,2},{4,5},{5,4},{6,7},{7,6},{8,9},{9,8},{10,11... | collective-permute-start | bytes 983048 | tf_op jit(solution)/shard_map/ppermute | solution.py:25
  22.0 1.2 %collective-permute-done.refs_0_ = bf16[320,512]{1,0:T(8,128)(2,1)S(1)} collective-permute-done((bf16[320,512]{1,0:T(8,128)(2,1)S(1)}, bf16[320,512]{1,0:T(8,128)(2,1)S(1)}, u32[]{:S(2)}, u32[]{:S(2)}) %collective-permute-start) | collective-permute-done | bytes 327712 | tf_op jit(solution)/shard_map/ppermute | solution.py:25
  23.2 1.4 %collective-permute-start.1 = (bf16[320,512]{1,0:T(8,128)(2,1)S(1)}, bf16[320,512]{1,0:T(8,128)(2,1)S(1)}, u32[]{:S(2)}, u32[]{:S(2)}) collective-permute-start(bf16[320,512]{1,0:T(8,128)(2,1)S(1)} %get-tuple-element.48), channel_id=1, source_target_pairs={{0,16},{4,20},{8,24},{12,28},{16,0},{20,4},{24,8},{28,12},{1,17},{... | collective-permute-start | bytes 983048 | tf_op jit(solution)/shard_map/ppermute | solution.py:25
  24.6 3.0 %collective-permute-done.4.refs_3_ = bf16[160,1024]{1,0:T(8,128)(2,1)S(1)} collective-permute-done((bf16[160,1024]{1,0:T(8,128)(2,1)S(1)}, bf16[160,1024]{1,0:T(8,128)(2,1)S(1)}, u32[]{:S(2)}, u32[]{:S(2)}) %collective-permute-start.4) | collective-permute-done | bytes 327712 | tf_op jit(solution)/shard_map/ppermute | solution.py:25
  27.6 1.3 %collective-permute-done.5.refs_4_ = bf16[160,1024]{1,0:T(8,128)(2,1)S(1)} collective-permute-done((bf16[160,1024]{1,0:T(8,128)(2,1)S(1)}, bf16[160,1024]{1,0:T(8,128)(2,1)S(1)}, u32[]{:S(2)}, u32[]{:S(2)}) %collective-permute-start.5) | collective-permute-done | bytes 327712 | tf_op jit(solution)/shard_map/ppermute | solution.py:25
  28.8 1.5 %collective-permute-start.6 = (bf16[320,512]{1,0:T(8,128)(2,1)S(1)}, bf16[320,512]{1,0:T(8,128)(2,1)S(1)}, u32[]{:S(2)}, u32[]{:S(2)}) collective-permute-start(bf16[320,512]{1,0:T(8,128)(2,1)S(1)} %collective-permute-done.refs_0_), channel_id=1, source_target_pairs={{0,1},{1,0},{2,3},{3,2},{4,5},{5,4},{6,7},{7,6},{8,9},{9,8},{10,11... | collective-permute-start | bytes 983048 | tf_op jit(solution)/shard_map/ppermute | solution.py:25
  30.3 0.5 collective-permute-start.7
  30.8 1.1 copy-done.2
  31.9 0.7 copy-done.6
  32.6 5.5 %project.3 = (bf16[384,1024]{1,0:T(8,128)(2,1)S(1)}, bf16[1024,512]{1,0:T(8,128)(2,1)S(1)}, bf16[384,1024]{1,0:T(8,128)(2,1)S(1)}) custom-call(bf16[320,1024]{1,0:T(8,128)(2,1)S(1)} %bitcast.16, bf16[320,1024]{1,0:T(8,128)(2,1)S(1)} %collective-permute-done.2.refs_1_, bf16[320,1024]{1,0:T(8,128)(2,1)S(1)} %collective-permute-done.3.refs_2_, ...), custom_call_target="tpu_custom_call" | custom-call | tf_op jit(solution)/shard_map/project/pallas_call | solution.py:41
  38.1 1.6 %collective-permute-done.1.refs_0_ = bf16[320,512]{1,0:T(8,128)(2,1)S(1)} collective-permute-done((bf16[320,512]{1,0:T(8,128)(2,1)S(1)}, bf16[320,512]{1,0:T(8,128)(2,1)S(1)}, u32[]{:S(2)}, u32[]{:S(2)}) %collective-permute-start.1) | collective-permute-done | bytes 327712 | tf_op jit(solution)/shard_map/ppermute | solution.py:25
  39.7 0.5 collective-permute-start.8
  40.3 0.6 collective-permute-start.9
  40.8 2.0 %collective-permute-start.10 = (s32[1024]{0:T(1024)S(1)}, s32[1024]{0:T(1024)S(1)}, u32[]{:S(2)}, u32[]{:S(2)}) collective-permute-start(s32[1024]{0:T(1024)S(1)} %copy-done.6), channel_id=1, source_target_pairs={{0,16},{4,20},{8,24},{12,28},{16,0},{20,4},{24,8},{28,12},{1,17},{... | collective-permute-start | bytes 12296 | tf_op jit(solution)/shard_map/ppermute | solution.py:25
  42.9 1.2 collective-permute-start.13
  44.1 1.0 collective-permute-start.14
  45.0 6.4 %near.1 = (f32[384,1024]{1,0:T(8,128)S(1)}, f32[8,1024]{1,0:T(8,128)S(1)}) custom-call(s32[1024]{0:T(1024)S(1)} %copy-done.6, bf16[384,1024]{1,0:T(8,128)(2,1)S(1)} %get-tuple-element.56.q, bf16[1024,512]{1,0:T(8,128)(2,1)S(1)} %get-tuple-element.52.k, bf16[384,1024]{1,0:T(8,128)(2,1)S(1)} %get-tuple-element.57.v), custom_call_target="tpu_custom_call" | custom-call | tf_op jit(solution)/shard_map/near/pallas_call | solution.py:41
  51.6 1.6 %collective-permute-start.11 = (bf16[160,512]{1,0:T(8,128)(2,1)S(1)}, bf16[160,512]{1,0:T(8,128)(2,1)S(1)}, u32[]{:S(2)}, u32[]{:S(2)}) collective-permute-start(bf16[160,512]{1,0:T(8,128)(2,1)S(1)} %slice.34), channel_id=1, source_target_pairs={{0,2},{1,3},{2,0},{3,1},{4,6},{5,7},{6,4},{7,5},{8,10},{9,11},{10,... | collective-permute-start | bytes 491528 | tf_op jit(solution)/shard_map/ppermute | solution.py:25
  53.2 0.6 collective-permute-start.12
  53.8 2.1 %project.5 = (bf16[512,512]{1,0:T(8,128)(2,1)S(1)}, bf16[384,512]{1,0:T(8,128)(2,1)S(1)}) custom-call(bf16[320,512]{1,0:T(8,128)(2,1)S(1)} %collective-permute-done.refs_0_, bf16[320,512]{1,0:T(8,128)(2,1)S(1)} %collective-permute-done.6.refs_1_, bf16[320,512]{1,0:T(8,128)(2,1)S(1)} %collective-permute-done.7.refs_2_, ...), custom_call_target="tpu_custom_call" | custom-call | tf_op jit(solution)/shard_map/project/pallas_call | solution.py:41
  55.9 3.0 %middle.1 = (f32[384,1024]{1,0:T(8,128)S(1)}, f32[8,1024]{1,0:T(8,128)S(1)}) custom-call(s32[1024]{0:T(1024)S(1)} %copy-done.6, s32[1024]{0:T(1024)S(1)} %collective-permute-done.10.k_ids, bf16[384,1024]{1,0:T(8,128)(2,1)S(1)} %get-tuple-element.56.q, bf16[512,512]{1,0:T(8,128)(2,1)S(1)} %get-tuple-element.64.k, bf16[384,512]{1,0:T(8,128)(2,1)S(1)} %get-tuple-element.65.v, ...), custom_call_target="tpu_custom_call" | custom-call | tf_op jit(solution)/shard_map/middle/pallas_call | solution.py:41
  58.8 2.1 %project.4 = (bf16[512,512]{1,0:T(8,128)(2,1)S(1)}, bf16[384,512]{1,0:T(8,128)(2,1)S(1)}) custom-call(bf16[320,512]{1,0:T(8,128)(2,1)S(1)} %collective-permute-done.1.refs_0_, bf16[320,512]{1,0:T(8,128)(2,1)S(1)} %collective-permute-done.8.refs_1_, bf16[320,512]{1,0:T(8,128)(2,1)S(1)} %collective-permute-done.9.refs_2_, ...), custom_call_target="tpu_custom_call" | custom-call | tf_op jit(solution)/shard_map/project/pallas_call | solution.py:41
  61.0 1.6 %last.3 = (bf16[320,512]{1,0:T(8,128)(2,1)S(1)}, bf16[320,512]{1,0:T(8,128)(2,1)S(1)}, bf16[320,512]{1,0:T(8,128)(2,1)S(1)}, bf16[320,512]{1,0:T(8,128)(2,1)S(1)}) custom-call(s32[1024]{0:T(1024)S(1)} %copy-done.6, s32[1024]{0:T(1024)S(1)} %collective-permute-done.10.k_ids, bf16[384,1024]{1,0:T(8,128)(2,1)S(1)} %get-tuple-element.56.q, ...), custom_call_target="tpu_custom_call" | custom-call | tf_op jit(solution)/shard_map/last/pallas_call | solution.py:41
  62.6 1.2 collective-permute-start.19
  63.8 1.8 %last.2 = (bf16[320,512]{1,0:T(8,128)(2,1)S(1)}, bf16[320,512]{1,0:T(8,128)(2,1)S(1)}, bf16[320,512]{1,0:T(8,128)(2,1)S(1)}, bf16[320,512]{1,0:T(8,128)(2,1)S(1)}) custom-call(s32[1024]{0:T(1024)S(1)} %copy-done.7, s32[1024]{0:T(1024)S(1)} %collective-permute-done.10.k_ids, bf16[384,1024]{1,0:T(8,128)(2,1)S(1)} %get-tuple-element.56.q, ...), custom_call_target="tpu_custom_call" | custom-call | tf_op jit(solution)/shard_map/last/pallas_call | solution.py:41
  65.6 1.0 collective-permute-start.16
  66.6 1.5 %collective-permute-start.18 = (bf16[320,512]{1,0:T(8,128)(2,1)S(1)}, bf16[320,512]{1,0:T(8,128)(2,1)S(1)}, u32[]{:S(2)}, u32[]{:S(2)}) collective-permute-start(bf16[320,512]{1,0:T(8,128)(2,1)S(1)} %get-tuple-element.74), channel_id=1, source_target_pairs={{0,2},{1,3},{2,0},{3,1},{4,6},{5,7},{6,4},{7,5},{8,10},{9,11},{10,... | collective-permute-start | bytes 983048 | tf_op jit(solution)/shard_map/ppermute | solution.py:25
  68.1 0.5 collective-permute-start.15
  68.6 4.1 %collective-permute-done.19 = bf16[320,512]{1,0:T(8,128)(2,1)S(1)} collective-permute-done((bf16[320,512]{1,0:T(8,128)(2,1)S(1)}, bf16[320,512]{1,0:T(8,128)(2,1)S(1)}, u32[]{:S(2)}, u32[]{:S(2)}) %collective-permute-start.19) | collective-permute-done | bytes 327712 | tf_op jit(solution)/shard_map/ppermute | solution.py:25
  72.8 2.1 %collective-permute-start.20 = (bf16[320,512]{1,0:T(8,128)(2,1)S(1)}, bf16[320,512]{1,0:T(8,128)(2,1)S(1)}, u32[]{:S(2)}, u32[]{:S(2)}) collective-permute-start(bf16[320,512]{1,0:T(8,128)(2,1)S(1)} %add_convert_fusion), channel_id=1, source_target_pairs={{0,1},{1,0},{2,3},{3,2},{4,5},{5,4},{6,7},{7,6},{8,9},{9,8},{10,11... | collective-permute-start | bytes 983048 | tf_op jit(solution)/shard_map/ppermute | solution.py:25
  75.0 1.3 %collective-permute-done.16 = bf16[320,512]{1,0:T(8,128)(2,1)S(1)} collective-permute-done((bf16[320,512]{1,0:T(8,128)(2,1)S(1)}, bf16[320,512]{1,0:T(8,128)(2,1)S(1)}, u32[]{:S(2)}, u32[]{:S(2)}) %collective-permute-start.16) | collective-permute-done | bytes 327712 | tf_op jit(solution)/shard_map/ppermute | solution.py:25
  76.4 1.0 collective-permute-start.17
  77.4 0.9 collective-permute-done.18.refs_4_
  78.3 2.7 %collective-permute-done.15.refs_1_ = bf16[320,512]{1,0:T(8,128)(2,1)S(1)} collective-permute-done((bf16[320,512]{1,0:T(8,128)(2,1)S(1)}, bf16[320,512]{1,0:T(8,128)(2,1)S(1)}, u32[]{:S(2)}, u32[]{:S(2)}) %collective-permute-start.15) | collective-permute-done | bytes 327712 | tf_op jit(solution)/shard_map/ppermute | solution.py:25
  81.0 3.9 %collective-permute-done.20.refs_5_ = bf16[320,512]{1,0:T(8,128)(2,1)S(1)} collective-permute-done((bf16[320,512]{1,0:T(8,128)(2,1)S(1)}, bf16[320,512]{1,0:T(8,128)(2,1)S(1)}, u32[]{:S(2)}, u32[]{:S(2)}) %collective-permute-start.20) | collective-permute-done | bytes 327712 | tf_op jit(solution)/shard_map/ppermute | solution.py:25
  84.9 1.8 %hidden.1 = (bf16[320,1024]{1,0:T(8,128)(2,1)}, bf16[320,1024]{1,0:T(8,128)(2,1)S(1)}, f32[8,1024]{1,0:T(8,128)S(1)}) custom-call(bf16[320,1024]{1,0:T(8,128)(2,1)S(1)} %bitcast.17, bf16[320,512]{1,0:T(8,128)(2,1)S(1)} %get-tuple-element.69.refs_0_, bf16[320,512]{1,0:T(8,128)(2,1)S(1)} %collective-permute-done.15.refs_1_, ...), custom_call_target="tpu_custom_call" | custom-call | tf_op jit(solution)/shard_map/hidden/pallas_call | solution.py:41
  86.7 1.0 collective-permute-start.21
  87.6 1.6 %collective-permute-start.22 = (f32[8,1024]{1,0:T(8,128)S(1)}, f32[8,1024]{1,0:T(8,128)S(1)}, u32[]{:S(2)}, u32[]{:S(2)}) collective-permute-start(f32[8,1024]{1,0:T(8,128)S(1)} %get-tuple-element.79.refs_0_), channel_id=1, source_target_pairs={{0,2},{1,3},{2,0},{3,1},{4,6},{5,7},{6,4},{7,5},{8,10},{9,11},{10,... | collective-permute-start | bytes 98312 | tf_op jit(solution)/shard_map/ppermute | solution.py:25
  89.3 0.9 collective-permute-start.23
  90.6 1.0 collective-permute-done.22.refs_2_
  91.6 3.1 %collective-permute-done.23.refs_3_ = f32[8,1024]{1,0:T(8,128)S(1)} collective-permute-done((f32[8,1024]{1,0:T(8,128)S(1)}, f32[8,1024]{1,0:T(8,128)S(1)}, u32[]{:S(2)}, u32[]{:S(2)}) %collective-permute-start.23) | collective-permute-done | bytes 32800 | tf_op jit(solution)/shard_map/ppermute | solution.py:25
  94.6 2.3 %merge.1 = (bf16[256,320]{1,0:T(8,128)(2,1)S(1)}, bf16[256,320]{1,0:T(8,128)(2,1)S(1)}, bf16[256,320]{1,0:T(8,128)(2,1)S(1)}, bf16[256,320]{1,0:T(8,128)(2,1)S(1)}) custom-call(bf16[320,1024]{1,0:T(8,128)(2,1)S(1)} %get-tuple-element.78.source, f32[8,1024]{1,0:T(8,128)S(1)} %get-tuple-element.79.refs_0_, f32[8,1024]{1,0:T(8,128)S(1)} %collective-permute-done.21.refs_1_, ...), custom_call_target="tpu_custom_call" | custom-call | tf_op jit(solution)/shard_map/merge/pallas_call | solution.py:41
  97.3 1.1 collective-permute-start.25
  98.4 2.0 %collective-permute-start.26 = (bf16[256,320]{1,0:T(8,128)(2,1)S(1)}, bf16[256,320]{1,0:T(8,128)(2,1)S(1)}, u32[]{:S(2)}, u32[]{:S(2)}) collective-permute-start(bf16[256,320]{1,0:T(8,128)(2,1)S(1)} %get-tuple-element.84), channel_id=1, source_target_pairs={{0,3},{1,2},{2,1},{3,0},{4,7},{5,6},{6,5},{7,4},{8,11},{9,10},{10,... | collective-permute-start | bytes 491528 | tf_op jit(solution)/shard_map/ppermute | solution.py:25
  100.5 2.2 %collective-permute-done.24.refs_1_ = bf16[256,320]{1,0:T(8,128)(2,1)S(1)} collective-permute-done((bf16[256,320]{1,0:T(8,128)(2,1)S(1)}, bf16[256,320]{1,0:T(8,128)(2,1)S(1)}, u32[]{:S(2)}, u32[]{:S(2)}) %collective-permute-start.24) | collective-permute-done | bytes 163872 | tf_op jit(solution)/shard_map/ppermute | solution.py:25
  103.0 2.1 %collective-permute-done.26.refs_3_ = bf16[256,320]{1,0:T(8,128)(2,1)S(1)} collective-permute-done((bf16[256,320]{1,0:T(8,128)(2,1)S(1)}, bf16[256,320]{1,0:T(8,128)(2,1)S(1)}, u32[]{:S(2)}, u32[]{:S(2)}) %collective-permute-start.26) | collective-permute-done | bytes 163872 | tf_op jit(solution)/shard_map/ppermute | solution.py:25
  105.5 2.6 %collective-permute-start.27 = (bf16[128,320]{1,0:T(8,128)(2,1)S(1)}, bf16[128,320]{1,0:T(8,128)(2,1)S(1)}, u32[]{:S(2)}, u32[]{:S(2)}) collective-permute-start(bf16[128,320]{1,0:T(8,128)(2,1)S(1)} %get-tuple-element.87), channel_id=1, source_target_pairs={{0,8},{4,12},{8,0},{12,4},{16,24},{20,28},{24,16},{28,20},{1,9},{5... | collective-permute-start | bytes 245768 | tf_op jit(solution)/shard_map/ppermute | solution.py:25
  108.1 2.0 %collective-permute-start.28 = (bf16[128,320]{1,0:T(8,128)(2,1)S(1)}, bf16[128,320]{1,0:T(8,128)(2,1)S(1)}, u32[]{:S(2)}, u32[]{:S(2)}) collective-permute-start(bf16[128,320]{1,0:T(8,128)(2,1)S(1)} %get-tuple-element.88), channel_id=1, source_target_pairs={{0,16},{4,20},{8,24},{12,28},{16,0},{20,4},{24,8},{28,12},{1,17},{... | collective-permute-start | bytes 245768 | tf_op jit(solution)/shard_map/ppermute | solution.py:25
  110.1 0.5 collective-permute-start.29
  110.7 4.0 %collective-permute-done.28.refs_2_ = bf16[128,320]{1,0:T(8,128)(2,1)S(1)} collective-permute-done((bf16[128,320]{1,0:T(8,128)(2,1)S(1)}, bf16[128,320]{1,0:T(8,128)(2,1)S(1)}, u32[]{:S(2)}, u32[]{:S(2)}) %collective-permute-start.28) | collective-permute-done | bytes 81952 | tf_op jit(solution)/shard_map/ppermute | solution.py:25
  114.7 1.9 %collective-permute-done.29.refs_3_ = bf16[128,320]{1,0:T(8,128)(2,1)S(1)} collective-permute-done((bf16[128,320]{1,0:T(8,128)(2,1)S(1)}, bf16[128,320]{1,0:T(8,128)(2,1)S(1)}, u32[]{:S(2)}, u32[]{:S(2)}) %collective-permute-start.29) | collective-permute-done | bytes 81952 | tf_op jit(solution)/shard_map/ppermute | solution.py:25
  116.7 1.4 %collective-permute-done.30.refs_4_ = bf16[256,320]{1,0:T(8,128)(2,1)S(1)} collective-permute-done((bf16[256,320]{1,0:T(8,128)(2,1)S(1)}, bf16[256,320]{1,0:T(8,128)(2,1)S(1)}, u32[]{:S(2)}, u32[]{:S(2)}) %collective-permute-start.30) | collective-permute-done | bytes 163872 | tf_op jit(solution)/shard_map/ppermute | solution.py:25
  118.1 0.8 settle.1
  (44 shorter events, 2.2 us)
Async XLA Ops:
  0.6 30.2 %copy-start = (bf16[3,1280,320]{1,2,0:T(8,128)(2,1)S(1)}, bf16[3,1280,320]{1,2,0:T(8,128)(2,1)}, u32[]{:S(2)}) copy-start(bf16[3,1280,320]{1,2,0:T(8,128)(2,1)} %param.11) | copy-start | bytes 7372804
  0.6 17.9 %collective-permute-start.2 = (bf16[320,1024]{1,0:T(8,128)(2,1)}, bf16[320,1024]{1,0:T(8,128)(2,1)S(1)}, u32[]{:S(2)}, u32[]{:S(2)}) collective-permute-start(bf16[320,1024]{1,0:T(8,128)(2,1)} %bitcast.13), channel_id=1, source_target_pairs={{0,1},{1,0},{2,3},{3,2},{4,5},{5,4},{6,7},{7,6},{8,9},{9,8},{10,11... | collective-permute-start | bytes 1966088 | tf_op jit(solution)/shard_map/ppermute | solution.py:25
  3.6 16.8 %collective-permute-start.3 = (bf16[320,1024]{1,0:T(8,128)(2,1)}, bf16[320,1024]{1,0:T(8,128)(2,1)S(1)}, u32[]{:S(2)}, u32[]{:S(2)}) collective-permute-start(bf16[320,1024]{1,0:T(8,128)(2,1)} %bitcast.14), channel_id=1, source_target_pairs={{0,2},{1,3},{2,0},{3,1},{4,6},{5,7},{6,4},{7,5},{8,10},{9,11},{10,... | collective-permute-start | bytes 1966088 | tf_op jit(solution)/shard_map/ppermute | solution.py:25
  5.2 1.1 copy-start.1
  6.4 16.9 %collective-permute-start = (bf16[320,512]{1,0:T(8,128)(2,1)S(1)}, bf16[320,512]{1,0:T(8,128)(2,1)S(1)}, u32[]{:S(2)}, u32[]{:S(2)}) collective-permute-start(bf16[320,512]{1,0:T(8,128)(2,1)S(1)} %get-tuple-element.47), channel_id=1, source_target_pairs={{0,16},{4,20},{8,24},{12,28},{16,0},{20,4},{24,8},{28,12},{1,17},{... | collective-permute-start | bytes 983048 | tf_op jit(solution)/shard_map/ppermute | solution.py:25
  10.4 1.1 copy-start.5
  11.6 0.7 copy-start.8
  18.6 9.0 %collective-permute-start.4 = (bf16[160,1024]{1,0:T(8,128)(2,1)S(1)}, bf16[160,1024]{1,0:T(8,128)(2,1)S(1)}, u32[]{:S(2)}, u32[]{:S(2)}) collective-permute-start(bf16[160,1024]{1,0:T(8,128)(2,1)S(1)} %slice.30), channel_id=1, source_target_pairs={{0,2},{1,3},{2,0},{3,1},{4,6},{5,7},{6,4},{7,5},{8,10},{9,11},{10,... | collective-permute-start | bytes 983048 | tf_op jit(solution)/shard_map/ppermute | solution.py:25
  20.5 8.4 %collective-permute-start.5 = (bf16[160,1024]{1,0:T(8,128)(2,1)S(1)}, bf16[160,1024]{1,0:T(8,128)(2,1)S(1)}, u32[]{:S(2)}, u32[]{:S(2)}) collective-permute-start(bf16[160,1024]{1,0:T(8,128)(2,1)S(1)} %slice.40), channel_id=1, source_target_pairs={{0,1},{1,0},{2,3},{3,2},{4,5},{5,4},{6,7},{7,6},{8,9},{9,8},{10,11... | collective-permute-start | bytes 983048 | tf_op jit(solution)/shard_map/ppermute | solution.py:25
  23.2 16.5 %collective-permute-start.1 = (bf16[320,512]{1,0:T(8,128)(2,1)S(1)}, bf16[320,512]{1,0:T(8,128)(2,1)S(1)}, u32[]{:S(2)}, u32[]{:S(2)}) collective-permute-start(bf16[320,512]{1,0:T(8,128)(2,1)S(1)} %get-tuple-element.48), channel_id=1, source_target_pairs={{0,16},{4,20},{8,24},{12,28},{16,0},{20,4},{24,8},{28,12},{1,17},{... | collective-permute-start | bytes 983048 | tf_op jit(solution)/shard_map/ppermute | solution.py:25
  28.8 10.9 %collective-permute-start.6 = (bf16[320,512]{1,0:T(8,128)(2,1)S(1)}, bf16[320,512]{1,0:T(8,128)(2,1)S(1)}, u32[]{:S(2)}, u32[]{:S(2)}) collective-permute-start(bf16[320,512]{1,0:T(8,128)(2,1)S(1)} %collective-permute-done.refs_0_), channel_id=1, source_target_pairs={{0,1},{1,0},{2,3},{3,2},{4,5},{5,4},{6,7},{7,6},{8,9},{9,8},{10,11... | collective-permute-start | bytes 983048 | tf_op jit(solution)/shard_map/ppermute | solution.py:25
  30.3 9.4 %collective-permute-start.7 = (bf16[320,512]{1,0:T(8,128)(2,1)S(1)}, bf16[320,512]{1,0:T(8,128)(2,1)S(1)}, u32[]{:S(2)}, u32[]{:S(2)}) collective-permute-start(bf16[320,512]{1,0:T(8,128)(2,1)S(1)} %collective-permute-done.refs_0_), channel_id=1, source_target_pairs={{0,2},{1,3},{2,0},{3,1},{4,6},{5,7},{6,4},{7,5},{8,10},{9,11},{10,... | collective-permute-start | bytes 983048 | tf_op jit(solution)/shard_map/ppermute | solution.py:25
  30.8 1.1 copy-start.2
  31.9 0.7 copy-start.6
  39.7 11.8 %collective-permute-start.8 = (bf16[320,512]{1,0:T(8,128)(2,1)S(1)}, bf16[320,512]{1,0:T(8,128)(2,1)S(1)}, u32[]{:S(2)}, u32[]{:S(2)}) collective-permute-start(bf16[320,512]{1,0:T(8,128)(2,1)S(1)} %collective-permute-done.1.refs_0_), channel_id=1, source_target_pairs={{0,1},{1,0},{2,3},{3,2},{4,5},{5,4},{6,7},{7,6},{8,9},{9,8},{10,11... | collective-permute-start | bytes 983048 | tf_op jit(solution)/shard_map/ppermute | solution.py:25
  40.3 11.3 %collective-permute-start.9 = (bf16[320,512]{1,0:T(8,128)(2,1)S(1)}, bf16[320,512]{1,0:T(8,128)(2,1)S(1)}, u32[]{:S(2)}, u32[]{:S(2)}) collective-permute-start(bf16[320,512]{1,0:T(8,128)(2,1)S(1)} %collective-permute-done.1.refs_0_), channel_id=1, source_target_pairs={{0,2},{1,3},{2,0},{3,1},{4,6},{5,7},{6,4},{7,5},{8,10},{9,11},{10,... | collective-permute-start | bytes 983048 | tf_op jit(solution)/shard_map/ppermute | solution.py:25
  40.8 10.7 %collective-permute-start.10 = (s32[1024]{0:T(1024)S(1)}, s32[1024]{0:T(1024)S(1)}, u32[]{:S(2)}, u32[]{:S(2)}) collective-permute-start(s32[1024]{0:T(1024)S(1)} %copy-done.6), channel_id=1, source_target_pairs={{0,16},{4,20},{8,24},{12,28},{16,0},{20,4},{24,8},{28,12},{1,17},{... | collective-permute-start | bytes 12296 | tf_op jit(solution)/shard_map/ppermute | solution.py:25
  42.9 10.9 %collective-permute-start.13 = (bf16[160,512]{1,0:T(8,128)(2,1)S(1)}, bf16[160,512]{1,0:T(8,128)(2,1)S(1)}, u32[]{:S(2)}, u32[]{:S(2)}) collective-permute-start(bf16[160,512]{1,0:T(8,128)(2,1)S(1)} %slice.41), channel_id=1, source_target_pairs={{0,2},{1,3},{2,0},{3,1},{4,6},{5,7},{6,4},{7,5},{8,10},{9,11},{10,... | collective-permute-start | bytes 491528 | tf_op jit(solution)/shard_map/ppermute | solution.py:25
  44.1 9.7 %collective-permute-start.14 = (bf16[160,512]{1,0:T(8,128)(2,1)S(1)}, bf16[160,512]{1,0:T(8,128)(2,1)S(1)}, u32[]{:S(2)}, u32[]{:S(2)}) collective-permute-start(bf16[160,512]{1,0:T(8,128)(2,1)S(1)} %slice.42), channel_id=1, source_target_pairs={{0,1},{1,0},{2,3},{3,2},{4,5},{5,4},{6,7},{7,6},{8,9},{9,8},{10,11... | collective-permute-start | bytes 491528 | tf_op jit(solution)/shard_map/ppermute | solution.py:25
  51.6 7.3 %collective-permute-start.11 = (bf16[160,512]{1,0:T(8,128)(2,1)S(1)}, bf16[160,512]{1,0:T(8,128)(2,1)S(1)}, u32[]{:S(2)}, u32[]{:S(2)}) collective-permute-start(bf16[160,512]{1,0:T(8,128)(2,1)S(1)} %slice.34), channel_id=1, source_target_pairs={{0,2},{1,3},{2,0},{3,1},{4,6},{5,7},{6,4},{7,5},{8,10},{9,11},{10,... | collective-permute-start | bytes 491528 | tf_op jit(solution)/shard_map/ppermute | solution.py:25
  53.2 5.7 %collective-permute-start.12 = (bf16[160,512]{1,0:T(8,128)(2,1)S(1)}, bf16[160,512]{1,0:T(8,128)(2,1)S(1)}, u32[]{:S(2)}, u32[]{:S(2)}) collective-permute-start(bf16[160,512]{1,0:T(8,128)(2,1)S(1)} %slice.35), channel_id=1, source_target_pairs={{0,1},{1,0},{2,3},{3,2},{4,5},{5,4},{6,7},{7,6},{8,9},{9,8},{10,11... | collective-permute-start | bytes 491528 | tf_op jit(solution)/shard_map/ppermute | solution.py:25
  61.0 2.8 %copy-start.7 = (s32[1024]{0:T(1024)S(1)}, s32[1024]{0:T(1024)}, u32[]{:S(2)}) copy-start(s32[1024]{0:T(1024)} %q_ids.7) | copy-start | bytes 12292
  62.6 22.3 %copy-start.3 = (bf16[1024,320]{0,1:T(8,128)(2,1)S(1)}, bf16[1024,320]{0,1:T(8,128)(2,1)}, u32[]{:S(2)}) copy-start(bf16[1024,320]{0,1:T(8,128)(2,1)} %param.8) | copy-start | bytes 1966084
  62.6 10.1 %collective-permute-start.19 = (bf16[320,512]{1,0:T(8,128)(2,1)S(1)}, bf16[320,512]{1,0:T(8,128)(2,1)S(1)}, u32[]{:S(2)}, u32[]{:S(2)}) collective-permute-start(bf16[320,512]{1,0:T(8,128)(2,1)S(1)} %get-tuple-element.76), channel_id=1, source_target_pairs={{0,2},{1,3},{2,0},{3,1},{4,6},{5,7},{6,4},{7,5},{8,10},{9,11},{10,... | collective-permute-start | bytes 983048 | tf_op jit(solution)/shard_map/ppermute | solution.py:25
  65.6 29.0 %copy-start.4 = (bf16[4,320,1280]{2,1,0:T(8,128)(2,1)S(1)}, bf16[4,320,1280]{2,1,0:T(8,128)(2,1)}, u32[]{:S(2)}) copy-start(bf16[4,320,1280]{2,1,0:T(8,128)(2,1)} %param.14) | copy-start | bytes 9830404
  65.6 10.7 %collective-permute-start.16 = (bf16[320,512]{1,0:T(8,128)(2,1)S(1)}, bf16[320,512]{1,0:T(8,128)(2,1)S(1)}, u32[]{:S(2)}, u32[]{:S(2)}) collective-permute-start(bf16[320,512]{1,0:T(8,128)(2,1)S(1)} %get-tuple-element.72), channel_id=1, source_target_pairs={{0,1},{1,0},{2,3},{3,2},{4,5},{5,4},{6,7},{7,6},{8,9},{9,8},{10,11... | collective-permute-start | bytes 983048 | tf_op jit(solution)/shard_map/ppermute | solution.py:25
  66.6 11.8 %collective-permute-start.18 = (bf16[320,512]{1,0:T(8,128)(2,1)S(1)}, bf16[320,512]{1,0:T(8,128)(2,1)S(1)}, u32[]{:S(2)}, u32[]{:S(2)}) collective-permute-start(bf16[320,512]{1,0:T(8,128)(2,1)S(1)} %get-tuple-element.74), channel_id=1, source_target_pairs={{0,2},{1,3},{2,0},{3,1},{4,6},{5,7},{6,4},{7,5},{8,10},{9,11},{10,... | collective-permute-start | bytes 983048 | tf_op jit(solution)/shard_map/ppermute | solution.py:25
  68.1 12.9 %collective-permute-start.15 = (bf16[320,512]{1,0:T(8,128)(2,1)S(1)}, bf16[320,512]{1,0:T(8,128)(2,1)S(1)}, u32[]{:S(2)}, u32[]{:S(2)}) collective-permute-start(bf16[320,512]{1,0:T(8,128)(2,1)S(1)} %get-tuple-element.70), channel_id=1, source_target_pairs={{0,1},{1,0},{2,3},{3,2},{4,5},{5,4},{6,7},{7,6},{8,9},{9,8},{10,11... | collective-permute-start | bytes 983048 | tf_op jit(solution)/shard_map/ppermute | solution.py:25
  72.8 12.1 %collective-permute-start.20 = (bf16[320,512]{1,0:T(8,128)(2,1)S(1)}, bf16[320,512]{1,0:T(8,128)(2,1)S(1)}, u32[]{:S(2)}, u32[]{:S(2)}) collective-permute-start(bf16[320,512]{1,0:T(8,128)(2,1)S(1)} %add_convert_fusion), channel_id=1, source_target_pairs={{0,1},{1,0},{2,3},{3,2},{4,5},{5,4},{6,7},{7,6},{8,9},{9,8},{10,11... | collective-permute-start | bytes 983048 | tf_op jit(solution)/shard_map/ppermute | solution.py:25
  76.4 8.5 %collective-permute-start.17 = (bf16[320,512]{1,0:T(8,128)(2,1)S(1)}, bf16[320,512]{1,0:T(8,128)(2,1)S(1)}, u32[]{:S(2)}, u32[]{:S(2)}) collective-permute-start(bf16[320,512]{1,0:T(8,128)(2,1)S(1)} %add_convert_fusion.1), channel_id=1, source_target_pairs={{0,2},{1,3},{2,0},{3,1},{4,6},{5,7},{6,4},{7,5},{8,10},{9,11},{10,... | collective-permute-start | bytes 983048 | tf_op jit(solution)/shard_map/ppermute | solution.py:25
  86.7 3.9 %collective-permute-start.21 = (f32[8,1024]{1,0:T(8,128)S(1)}, f32[8,1024]{1,0:T(8,128)S(1)}, u32[]{:S(2)}, u32[]{:S(2)}) collective-permute-start(f32[8,1024]{1,0:T(8,128)S(1)} %get-tuple-element.79.refs_0_), channel_id=1, source_target_pairs={{0,1},{1,0},{2,3},{3,2},{4,5},{5,4},{6,7},{7,6},{8,9},{9,8},{10,11... | collective-permute-start | bytes 98312 | tf_op jit(solution)/shard_map/ppermute | solution.py:25
  87.6 3.9 %collective-permute-start.22 = (f32[8,1024]{1,0:T(8,128)S(1)}, f32[8,1024]{1,0:T(8,128)S(1)}, u32[]{:S(2)}, u32[]{:S(2)}) collective-permute-start(f32[8,1024]{1,0:T(8,128)S(1)} %get-tuple-element.79.refs_0_), channel_id=1, source_target_pairs={{0,2},{1,3},{2,0},{3,1},{4,6},{5,7},{6,4},{7,5},{8,10},{9,11},{10,... | collective-permute-start | bytes 98312 | tf_op jit(solution)/shard_map/ppermute | solution.py:25
  89.3 5.3 %collective-permute-start.23 = (f32[8,1024]{1,0:T(8,128)S(1)}, f32[8,1024]{1,0:T(8,128)S(1)}, u32[]{:S(2)}, u32[]{:S(2)}) collective-permute-start(f32[8,1024]{1,0:T(8,128)S(1)} %get-tuple-element.79.refs_0_), channel_id=1, source_target_pairs={{0,3},{1,2},{2,1},{3,0},{4,7},{5,6},{6,5},{7,4},{8,11},{9,10},{10,... | collective-permute-start | bytes 98312 | tf_op jit(solution)/shard_map/ppermute | solution.py:25
  96.9 5.7 %collective-permute-start.24 = (bf16[256,320]{1,0:T(8,128)(2,1)S(1)}, bf16[256,320]{1,0:T(8,128)(2,1)S(1)}, u32[]{:S(2)}, u32[]{:S(2)}) collective-permute-start(bf16[256,320]{1,0:T(8,128)(2,1)S(1)} %get-tuple-element.82), channel_id=1, source_target_pairs={{0,1},{1,0},{2,3},{3,2},{4,5},{5,4},{6,7},{7,6},{8,9},{9,8},{10,11... | collective-permute-start | bytes 491528 | tf_op jit(solution)/shard_map/ppermute | solution.py:25
  97.3 5.7 %collective-permute-start.25 = (bf16[256,320]{1,0:T(8,128)(2,1)S(1)}, bf16[256,320]{1,0:T(8,128)(2,1)S(1)}, u32[]{:S(2)}, u32[]{:S(2)}) collective-permute-start(bf16[256,320]{1,0:T(8,128)(2,1)S(1)} %get-tuple-element.83), channel_id=1, source_target_pairs={{0,2},{1,3},{2,0},{3,1},{4,6},{5,7},{6,4},{7,5},{8,10},{9,11},{10,... | collective-permute-start | bytes 491528 | tf_op jit(solution)/shard_map/ppermute | solution.py:25
  98.4 6.6 %collective-permute-start.26 = (bf16[256,320]{1,0:T(8,128)(2,1)S(1)}, bf16[256,320]{1,0:T(8,128)(2,1)S(1)}, u32[]{:S(2)}, u32[]{:S(2)}) collective-permute-start(bf16[256,320]{1,0:T(8,128)(2,1)S(1)} %get-tuple-element.84), channel_id=1, source_target_pairs={{0,3},{1,2},{2,1},{3,0},{4,7},{5,6},{6,5},{7,4},{8,11},{9,10},{10,... | collective-permute-start | bytes 491528 | tf_op jit(solution)/shard_map/ppermute | solution.py:25
  105.5 5.2 %collective-permute-start.27 = (bf16[128,320]{1,0:T(8,128)(2,1)S(1)}, bf16[128,320]{1,0:T(8,128)(2,1)S(1)}, u32[]{:S(2)}, u32[]{:S(2)}) collective-permute-start(bf16[128,320]{1,0:T(8,128)(2,1)S(1)} %get-tuple-element.87), channel_id=1, source_target_pairs={{0,8},{4,12},{8,0},{12,4},{16,24},{20,28},{24,16},{28,20},{1,9},{5... | collective-permute-start | bytes 245768 | tf_op jit(solution)/shard_map/ppermute | solution.py:25
  108.1 6.6 %collective-permute-start.28 = (bf16[128,320]{1,0:T(8,128)(2,1)S(1)}, bf16[128,320]{1,0:T(8,128)(2,1)S(1)}, u32[]{:S(2)}, u32[]{:S(2)}) collective-permute-start(bf16[128,320]{1,0:T(8,128)(2,1)S(1)} %get-tuple-element.88), channel_id=1, source_target_pairs={{0,16},{4,20},{8,24},{12,28},{16,0},{20,4},{24,8},{28,12},{1,17},{... | collective-permute-start | bytes 245768 | tf_op jit(solution)/shard_map/ppermute | solution.py:25
  110.1 6.5 %collective-permute-start.29 = (bf16[128,320]{1,0:T(8,128)(2,1)S(1)}, bf16[128,320]{1,0:T(8,128)(2,1)S(1)}, u32[]{:S(2)}, u32[]{:S(2)}) collective-permute-start(bf16[128,320]{1,0:T(8,128)(2,1)S(1)} %get-tuple-element.89), channel_id=1, source_target_pairs={{0,24},{4,28},{8,16},{12,20},{16,8},{20,12},{24,0},{28,4},{1,25},{... | collective-permute-start | bytes 245768 | tf_op jit(solution)/shard_map/ppermute | solution.py:25
  116.6 1.5 %collective-permute-start.30 = (bf16[256,320]{1,0:T(8,128)(2,1)S(1)}, bf16[256,320]{1,0:T(8,128)(2,1)S(1)}, u32[]{:S(2)}, u32[]{:S(2)}) collective-permute-start(bf16[256,320]{1,0:T(8,128)(2,1)S(1)} %pad_maximum_fusion), channel_id=1, source_target_pairs={{0,4},{4,0},{8,12},{12,8},{16,20},{20,16},{24,28},{28,24},{1,5},{5... | collective-permute-start | bytes 491528 | tf_op jit(solution)/shard_map/ppermute | solution.py:25

commit v4 on v3

--- a/solution.py
+++ b/solution.py
@@ -50,16 +50,25 @@
     )(*args)
 
 
-def prepare_body(w, gain, merge_gain, owner, w_back, gain_wide, merge_wide, dispatch):
+def prepare_body(
+    crossing, w, w_merge, gain, merge_gain, owner, ids, *outs
+):
+    w_back, w_tall, gain_wide, merge_wide, dispatch, ids_row = outs
+    ids_row[...] = ids[...]
     full = w.shape[1]
     for lo in range(0, full, PAD):
         at = slice(lo, lo + PAD)
         w_back[at, :] = w[:, at].astype(F32).T.astype(BF)
         gain_wide[at, :] = jnp.broadcast_to(gain[:, at], (PAD, PAD)).T
         merge_wide[at, :] = jnp.broadcast_to(merge_gain[:, at], (PAD, PAD)).T
+        for low in range(0, w_merge.shape[0], 4 * PAD):
+            high = min(low + 4 * PAD, w_merge.shape[0])
+            w_tall[at, low:high] = w_merge[low:high, at].astype(F32).T.astype(BF)
     slots, count = dispatch.shape
     groups = lax.axis_size("grp")
     named = owner[...]
+    if crossing:
+        named = named ^ lax.axis_index("grp")
     onehot = jnp.broadcast_to(named, (groups, count)) == lax.broadcasted_iota(
         jnp.int32, (groups, count), 0
     )
@@ -81,15 +90,22 @@
     ).astype(BF)
 
 
-def prepare(w, gain, merge_gain, owner, slots):
+def prepare(w, w_merge, gain, merge_gain, owner, ids, slots, crossing):
     width, full = w.shape
     count = owner.shape[0]
     return call(
-        prepare_body,
+        functools.partial(prepare_body, crossing),
         "prepare",
-        [w, gain[None, :], merge_gain[None, :], owner.reshape(1, count)],
-        0,
-        [((full, width), BF), ((full, PAD), F32), ((full, PAD), F32), ((slots, count), BF)],
+        [w, w_merge, gain[None, :], merge_gain[None, :], owner.reshape(1, count), ids],
+        0,
+        [
+            ((full, width), BF),
+            (w_merge.shape[::-1], BF),
+            ((full, PAD), F32),
+            ((full, PAD), F32),
+            ((slots, count), BF),
+            (ids.shape, jnp.int32),
+        ],
         [],
     )
 
@@ -244,83 +260,116 @@
                 )
 
 
-def near_body(block, q_ids, q, k, v, acc, top):
-    acc[...] = jnp.zeros_like(acc)
-    top[...] = jnp.full_like(top, -1e20)
-    sweep(block, q_ids, q_ids, 0, q, 0, k, v, acc, top)
+def near_body(block, q_ids, q, k, v, *refs):
+    for i in range(0, len(refs), 2):
+        acc, top = refs[i : i + 2]
+        acc[...] = jnp.zeros_like(acc)
+        top[...] = jnp.full_like(top, -1e20)
+        sweep(block, q_ids, q_ids, 0, q, i // 2 * acc.shape[1], k, v, acc, top)
 
 
 def near(q_ids, q, k, v):
     wide, rows = q.shape
-    heads = wide // HEAD_ROWS
-    return call(
+    a0, t0, a1, t1 = call(
         functools.partial(near_body, 2 * BLOCK),
         "near",
         [q_ids, q, k, v],
         1,
-        [((wide, rows), F32), ((8, rows), F32)],
+        [((wide, rows // 2), F32), ((8, rows // 2), F32)] * 2,
         [],
     )
-
-
-def middle_body(start, q_ids, k_ids, q, k, v, acc_in, top_in, acc, top):
-    acc[...] = acc_in[...]
-    top[...] = top_in[...]
-    sweep(BLOCK, q_ids, k_ids, start, q, 0, k, v, acc, top)
-
-
-def middle(q_ids, k_ids, q, k, v, acc, top, start):
-    wide, rows = q.shape
-    heads = wide // HEAD_ROWS
-    return call(
-        functools.partial(middle_body, start),
+    return [(a0, t0), (a1, t1)]
+
+
+def middle_body(k_start, q_ids, k_ids, q, k, v, *refs):
+    count = len(refs) // 4
+    for i in range(count):
+        acc_in, top_in = refs[2 * i : 2 * i + 2]
+        acc, top = refs[2 * (count + i) : 2 * (count + i) + 2]
+        acc[...] = acc_in[...]
+        top[...] = top_in[...]
+        sweep(BLOCK, q_ids, k_ids, k_start, q, i * acc.shape[1], k, v, acc, top)
+
+
+def middle(q_ids, k_ids, q, k, v, states, k_start):
+    flat = [x for state in states for x in state]
+    found = call(
+        functools.partial(middle_body, k_start),
         "middle",
-        [q_ids, k_ids, q, k, v, acc, top],
+        [q_ids, k_ids, q, k, v, *flat],
         2,
-        [(acc.shape, F32), (top.shape, F32)],
+        [(x.shape, F32) for x in flat],
         [],
     )
-
-
-def last_body(n_out, start, k_start, q_ids, k_ids, q, k, v, acc_in, top_in, w, *refs):
-    outs = refs[:n_out]
-    acc, top, ctx = refs[n_out:]
+    return [tuple(found[2 * i : 2 * i + 2]) for i in range(len(states))]
+
+
+def multiply(w, index, width, ctx):
+    at = pl.ds(pl.multiple_of(index * width, 16), width)
+    return jnp.dot(w[at, :], ctx, preferred_element_type=F32).astype(BF)
+
+
+def last_body(count, n_out, k_start, q_ids, k_ids, q, k, v, w, *refs):
+    states = refs[: 2 * count]
+    ctx = refs[2 * count]
+    outs = refs[2 * count + 1 : 3 * count + 1]
+    acc, top = refs[3 * count + 1 :]
     rows = acc.shape[1]
     heads = q.shape[0] // HEAD_ROWS
-    acc[...] = acc_in[:, start : start + rows]
-    top[...] = top_in[:, start : start + rows]
-    sweep(BLOCK, q_ids, k_ids, k_start, q, start, k, v, acc, top)
-    for h in range(heads):
-        lo = h * HEAD_ROWS
-        ctx[h * HD : (h + 1) * HD, :] = (
-            acc[lo : lo + HD, :] / acc[lo + HD : lo + HD + 1, :]
-        ).astype(BF)
-    width = outs[0].shape[0]
     order = nearby(n_out)
-    for j in reversed(range(n_out)):
-        at = pl.ds(pl.multiple_of(order[j] * width, 16), width)
-        outs[j][...] = jnp.dot(w[at, :], ctx[...], preferred_element_type=F32).astype(BF)
-
-
-def last(q_ids, k_ids, q, k, v, acc, top, w, n_out, start, rows, k_start):
-    wide = q.shape[0]
-    heads = wide // HEAD_ROWS
-    full = w.shape[0]
-    return call(
-        functools.partial(last_body, n_out, start, k_start),
+    for i in range(count):
+        at = slice(i * rows, (i + 1) * rows)
+        acc[...] = states[2 * i][...]
+        top[...] = states[2 * i + 1][...]
+        sweep(BLOCK, q_ids, k_ids, k_start, q, i * rows, k, v, acc, top)
+        for h in range(heads):
+            lo = h * HEAD_ROWS
+            ctx[h * HD : (h + 1) * HD, at] = (
+                acc[lo : lo + HD, :] / acc[lo + HD : lo + HD + 1, :]
+            ).astype(BF)
+        outs[i][...] = multiply(w, order[-1], outs[i].shape[0], ctx[:, at])
+
+
+def last(q_ids, k_ids, q, k, v, states, w, n_out, k_start):
+    wide, rows = q.shape
+    count = len(states)
+    part = rows // count
+    return call(
+        functools.partial(last_body, count, n_out, k_start),
         "last",
-        [q_ids, k_ids, q, k, v, acc, top, w],
+        [q_ids, k_ids, q, k, v, w, *[x for state in states for x in state]],
         2,
-        [((full // n_out, rows), BF) for _ in range(n_out)],
+        [((w.shape[1], rows), BF)] + [((w.shape[0] // n_out, part), BF) for _ in states],
+        [pltpu.VMEM((wide, part), F32), pltpu.VMEM((8, part), F32)],
+    )
+
+
+def rest_body(n_out, ctx, w, *outs):
+    order = nearby(n_out)
+    count = len(outs) // (n_out - 1)
+    rows = ctx.shape[1] // count
+    for j in range(n_out - 1):
+        found = multiply(w, order[j], outs[0].shape[0], ctx[...])
+        for i in range(count):
+            outs[j * count + i][...] = found[:, i * rows : (i + 1) * rows]
+
+
+def rest(ctx, w, n_out, count):
+    found = call(
+        functools.partial(rest_body, n_out),
+        "rest",
+        [ctx, w],
+        0,
         [
-            pltpu.VMEM((wide, rows), F32),
-            pltpu.VMEM((8, rows), F32),
-            pltpu.VMEM((heads * HD, rows), BF),
+            ((w.shape[0] // n_out, ctx.shape[1] // count), BF)
+            for _ in range((n_out - 1) * count)
         ],
-    )
-
-
-def hidden_body(n_half, tokens, *refs):
+        [],
+    )
+    return [[found[j * count + i] for j in range(n_out - 1)] for i in range(count)]
+
+
+def hidden_body(n_half, *refs):
     hidden, again, stats = refs[-3:]
     inputs = refs[:-3]
     each = len(inputs) // n_half
@@ -328,7 +377,7 @@
     for i in range(n_half):
         for lo in range(0, rows, PAD):
             at = slice(i * rows + lo, i * rows + lo + PAD)
-            total = tokens[:, at].astype(F32)
+            total = 0.0
             for g in inputs[i * each : (i + 1) * each]:
                 total = total + g[:, lo : lo + PAD].astype(F32)
             rounded = total.astype(BF)
@@ -342,12 +391,13 @@
             )
 
 
-def hidden_sum(tokens, groups):
-    width, count = tokens.shape
+def hidden_sum(groups):
+    width, rows = groups[0][0].shape
+    count = rows * len(groups)
     return call(
         functools.partial(hidden_body, len(groups)),
         "hidden",
-        [tokens, *[x for g in groups for x in g]],
+        [x for g in groups for x in g],
         0,
         [((width, count), BF), ((width, count), BF), ((8, count), F32)],
         [],
@@ -388,28 +438,24 @@
             blocks[lo // 4 : lo // 4 + quarter, j * width : (j + 1) * width] = picked[
                 j * quarter : (j + 1) * quarter, :
             ]
-    terms = jnp.dot(blocks[...], w[...], preferred_element_type=F32)
-    if n_out == 1:
-        outs[0][...] = terms.astype(BF)
-        return
-    for case in range(n_out):
-
-        @pl.when(me == case)
-        def _(case=case):
-            for k in range(n_out):
-                lo = (case ^ k) * width
-                outs[k][...] = terms[:, lo : lo + width].astype(BF)
+    order = nearby(n_out)
+    for j in range(n_out):
+        tall = outs[j].shape[0]
+        at = pl.ds(pl.multiple_of(order[j] * tall, 16), tall)
+        outs[j][...] = lax.dot_general(
+            w[at, :], blocks[...], (((1,), (1,)), ((), ())), preferred_element_type=F32
+        ).astype(BF)
 
 
 def merge(hidden, stats, gain, w, n_out):
     width, rows = hidden.shape
-    full = w.shape[1]
+    full = w.shape[0]
     return call(
         functools.partial(merge_body, len(stats), n_out),
         "merge",
         [hidden, *stats, gain, w],
         0,
-        [((rows // 4, full // n_out), BF) for _ in range(n_out)],
+        [((full // n_out, rows // 4), BF) for _ in range(n_out)],
         [
             pltpu.VMEM((width, rows), BF),
             pltpu.VMEM((rows // 4, 4 * width), BF),
@@ -418,34 +464,40 @@
     )
 
 
-def place_body(n_in, crossing, *refs):
+def place_body(n_in, *refs):
     merged = sum(r[...].astype(F32) for r in refs[:n_in]).astype(BF)
     dispatch = refs[n_in]
-    placed = jnp.dot(dispatch[...], merged, preferred_element_type=F32).astype(BF)
-    if not crossing:
-        refs[-1][...] = placed
+    outs = refs[n_in + 1 :]
+    dims = (((1,), (1,)), ((), ()))
+    if len(outs) == 1:
+        outs[0][...] = lax.dot_general(
+            dispatch[...], merged, dims, preferred_element_type=F32
+        ).astype(BF)
         return
-    whole = refs[-1]
-    whole[...] = placed
-    group = lax.axis_index("grp")
-    for k, out in enumerate(refs[n_in + 1 : -1]):
-        cap = out.shape[0] // 2
-        for e in range(2):
-            at = pl.ds(pl.multiple_of((group ^ (2 * k + e)) * cap, 16), cap)
-            out[e * cap : (e + 1) * cap, :] = whole[at, :]
+    placed = lax.dot_general(merged, dispatch[...], dims, preferred_element_type=F32)
+    for k, out in enumerate(outs):
+        size = out.shape[1]
+        out[...] = placed[:, k * size : (k + 1) * size].astype(BF)
 
 
 def place(terms, dispatch, n_out):
     slots = dispatch.shape[0]
-    width = terms[0].shape[1]
-    return call(
-        functools.partial(place_body, len(terms), n_out > 1),
+    width = terms[0].shape[0]
+    return call(
+        functools.partial(place_body, len(terms)),
         "place",
         [*terms, dispatch],
         0,
-        [((slots // n_out, width), BF) for _ in range(n_out)],
-        [pltpu.VMEM((slots, width), BF)] if n_out > 1 else [],
-    )
+        [((width, slots // n_out) if n_out > 1 else (slots, width), BF) for _ in range(n_out)],
+        [],
+    )
+
+
+def gather_body(*refs):
+    out = refs[-1]
+    cap = out.shape[1] // (len(refs) - 1)
+    for k, block in enumerate(refs[:-1]):
+        out[:, k * cap : (k + 1) * cap] = block[:, cap:]
 
 
 def settle_body(*refs):
@@ -453,16 +505,22 @@
     cap = out.shape[1]
     group = lax.axis_index("grp")
     for k, block in enumerate(refs[:-2]):
-        out[pl.ds(group ^ (2 * k), 1)] = block[:cap, :][None]
-        out[pl.ds(group ^ (2 * k + 1), 1)] = crossed[k * cap : (k + 1) * cap, :][None]
-
-
-def settle(blocks, crossed, cap):
-    width = crossed.shape[1]
+        out[pl.ds(group ^ (2 * k), 1)] = block[...].astype(F32).T[:cap, :].astype(BF)[None]
+    for k in range(0, len(refs) - 2, 2):
+        pair = crossed[:, k * cap : (k + 2) * cap].astype(F32).T.astype(BF)
+        out[pl.ds(group ^ (2 * k + 1), 1)] = pair[:cap, :][None]
+        out[pl.ds(group ^ (2 * k + 3), 1)] = pair[cap:, :][None]
+
+
+def settle(blocks, cap):
+    width = blocks[0].shape[0]
+    others = call(
+        gather_body, "gather", list(blocks), 0, [((width, len(blocks) * cap), BF)], []
+    )[0]
     return call(
         settle_body,
         "settle",
-        [*blocks, crossed],
+        [*blocks, hop(others, "grp", 1)],
         0,
         [((2 * len(blocks), cap, width), BF)],
         [],
@@ -482,34 +540,47 @@
 
     tall = tokens.T
     spans = ((0, half), (half, row_count))
-    far_segment = hop(segment, "grp", partner)
+    h0, h1 = split(tall, spans)
     merged_count = row_count // 4
     cap_slots = max(2, merged_count // grp_count * 2)
-    w_back, gain, merge_wide, dispatch = prepare(
-        w_out, ln_gain, merge_gain, owner, grp_count * cap_slots
+    crossing = grp_count == 8
+    w_back, w_tall, gain, merge_wide, dispatch, ids_row = prepare(
+        w_out,
+        w_merge.reshape(4 * local_width, full_width),
+        ln_gain,
+        merge_gain,
+        owner,
+        segment[None, :],
+        grp_count * cap_slots,
+        crossing,
     )
     w_in = jnp.swapaxes(w_qkv, 1, 2).reshape(3 * local_width, full_width)
-    w_blocks = w_merge.reshape(4 * local_width, full_width)
 
     def keys_of(pieces, start):
         return project(pieces, n_out, half, gain, w_in, far_segment[None, :], (1, 2), start)
 
     def own_of(pieces):
         return project(
-            pieces, n_out, row_count, gain, w_in, segment[None, :], (0, 1, 2), 0
+            pieces, n_out, row_count, gain, w_in, ids_row, (0, 1, 2), 0
         )
 
     if square:
         mid = local_width // 2
         a = hop(tall, "tp", 1)
         b = hop(tall, "tp", 2)
-        h0, h1 = split(tall, spans)
         z0 = hop(h0, "grp", partner)
         c = hop(after(a, w_back)[:mid], "tp", 2)
         d = hop(b[mid:], "tp", 1)
         z1 = hop(after(h1, z0), "grp", partner)
         q, k, v = own_of(
-            [(tall, 0, 0, 0), (a, 1, 0, 0), (b, 2, 0, 0), (c, 3, 0, 0), (d, 3, mid, 0)]
+            [
+                (h0, 0, 0, 0),
+                (h1, 0, 0, half),
+                (a, 1, 0, 0),
+                (b, 2, 0, 0),
+                (c, 3, 0, 0),
+                (d, 3, mid, 0),
+            ]
         )
         z0 = after(z0, c, d)
         za0 = hop(z0, "tp", 1)
@@ -520,8 +591,9 @@
         ta0, tb0 = za0[:mid], zb0[mid:]
         zc0 = hop(ta0, "tp", 2)
         zd0 = hop(tb0, "tp", 1)
-        acc, top = near(segment, after(q, z1, ta0, tb0), k, v)
-        za1, zb1, far_segment = lax.optimization_barrier((za1, zb1, far_segment, top))[:3]
+        states = near(segment, after(q, z1, ta0, tb0), k, v)
+        far_segment = hop(segment, "grp", partner)
+        za1, zb1, far_segment = after((za1, zb1, far_segment), states[0][1])
         ta1, tb1 = za1[:mid], zb1[mid:]
         zc1 = hop(ta1, "tp", 2)
         zd1 = hop(tb1, "tp", 1)
@@ -529,56 +601,53 @@
             [(z0, 0, 0, 0), (za0, 1, 0, 0), (zb0, 2, 0, 0), (zc0, 3, 0, 0), (zd0, 3, mid, 0)],
             0,
         )
-        acc, top = middle(segment, far_segment, q, *far0, acc, top, 0)
         far1 = keys_of(
             [(z1, 0, 0, 0), (za1, 1, 0, 0), (zb1, 2, 0, 0), (zc1, 3, 0, 0), (zd1, 3, mid, 0)],
             half,
         )
     else:
+        far_segment = hop(segment, "grp", partner)
         q, k, v = own_of([(lax.all_gather(tall, "tp", axis=0, tiled=True), 0, 0, 0)])
         far_whole = lax.all_gather(hop(tall, "grp", partner), "tp", axis=0, tiled=True)
         far0, far1 = [keys_of([(far_whole[:, lo:hi], 0, 0, 0)], lo) for lo, hi in spans]
-        acc, top = near(segment, q, k, v)
-        acc, top = middle(segment, far_segment, q, *far0, acc, top, 0)
-
-    crossing = grp_count == 8
-    terms = [
-        last(segment, far_segment, q, *far1, acc, top, w_back, n_out, start, half, half)
-        for start in (0, half)
-    ]
-
+        states = near(segment, q, k, v)
+
+    states = middle(segment, far_segment, q, *far0, states, 0)
+    ctx, *corners = last(segment, far_segment, q, *far1, states, w_back, n_out, half)
+
+    halves = [h0, h1]
     if square:
+        hops = ((1, 2), (2, 1))
+        corners = [hop(t, "tp", side_hop) for t, (side_hop, _) in zip(corners, hops)]
         groups = []
-        for i, (side_hop, next_hop) in enumerate(((1, 2), (2, 1))):
-            corner = hop(terms[i][3], "tp", side_hop)
-            side = hop(terms[i][side_hop], "tp", side_hop)
-            passed = (terms[i][next_hop].astype(F32) + corner.astype(F32)).astype(BF)
+        for i, terms in enumerate(rest(ctx, w_back, n_out, 2)):
+            side_hop, next_hop = hops[i]
+            side = hop(terms[side_hop], "tp", side_hop)
+            passed = (terms[next_hop].astype(F32) + corners[i].astype(F32)).astype(BF)
             onward = hop(passed, "tp", next_hop)
-            groups.append((terms[i][0], side, onward))
+            groups.append((halves[i], terms[0], side, onward))
     else:
         groups = [
-            (lax.psum_scatter(t[0], "tp", scatter_dimension=0, tiled=True),) for t in terms
+            (h, lax.psum_scatter(t, "tp", scatter_dimension=0, tiled=True))
+            for h, t in zip(halves, corners)
         ]
-    hidden_out, hidden, stats = hidden_sum(tall, groups)
+    hidden_out, hidden, stats = hidden_sum(groups)
     if square:
         all_stats = [stats] + [hop(stats, "tp", n) for n in (1, 2, 3)]
     else:
         gathered = lax.all_gather(stats, "tp")
         all_stats = [gathered[n] for n in range(tp_count)]
-    merge_terms = merge(hidden, all_stats, merge_wide, w_blocks, n_out)
+    merge_terms = merge(hidden, all_stats, merge_wide, w_tall, n_out)
     if square:
-        received = [merge_terms[0]] + [hop(merge_terms[n], "tp", n) for n in (1, 2, 3)]
+        received = [hop(merge_terms[n], "tp", n) for n in (3, 1, 2)] + [merge_terms[0]]
     else:
-        received = [lax.psum_scatter(merge_terms[0], "tp", scatter_dimension=1, tiled=True)]
+        received = [lax.psum_scatter(merge_terms[0], "tp", scatter_dimension=0, tiled=True)]
     if crossing:
         blocks = place(received, dispatch, grp_count // 2)
         blocks = [blocks[0]] + [
             hop(block, "grp", 2 * n) for n, block in enumerate(blocks) if n > 0
         ]
-        crossed = hop(
-            jnp.concatenate([block[cap_slots:] for block in blocks], axis=0), "grp", 1
-        )
-        routed = settle(blocks, crossed, cap_slots)
+        routed = settle(blocks, cap_slots)
     else:
         outgoing = place(received, dispatch, 1)[0].reshape(grp_count, cap_slots, local_width)
         routed = lax.all_to_all(outgoing, "grp", split_axis=0, concat_axis=0, tiled=True)

time: 121 us -> 117 us (0.967); the launches traced: 119 us -> 117 us
  waiting for transfers between devices: 42 us -> 40.5 us
    ppermute x31, waiting for transfers between devices: 42 us -> 40.5 us  [hop(): lax.ppermute(x, axis, [(i, i ^ distance) for i in range(lax.axis_size(axi...]
    unnamed x18 -> x14, local copies, waits for them, and re-layouts: 4.74 us -> 5.56 us
    pallas_call x13 -> x14, Pallas kernels: 28.7 us -> 28.6 us  [call(): pl.pallas_call(body, in_specs=[place(i) for i in range(len(args))], out_s...]
  transfers between devices with their start and end apart: 31 -> 31, of which waited for: 20 -> 18; matrix products, arithmetic and copies ran while one was open for 1% -> 1% of each run, Pallas kernels for 17% -> 17%
where the time goes in v4:
time: 117 us
  waiting for transfers between devices  40.5 us (35%)
  starting transfers between devices  39.7 us (34%)
  Pallas kernels  28.6 us (24%)
  local copies, waits for them, and re-layouts  7.06 us (6%)
    ppermute x31, waiting for transfers between devices, hop(): lax.ppermute(x, axis, [(i, i ^ distance) for i in range(lax.axis_size(axi...  40.5 us
    ppermute x31, starting transfers between devices, hop(): lax.ppermute(x, axis, [(i, i ^ distance) for i in range(lax.axis_size(axi...  39.7 us
    pallas_call x14, Pallas kernels, call(): pl.pallas_call(body, in_specs=[place(i) for i in range(len(args))], out_s...  28.6 us
    unnamed x14, local copies, waits for them, and re-layouts  5.56 us
  transfers between devices with their start and end apart: 31, of which 18 were waited for; matrix products, arithmetic and copies ran while one was open for 1% of the time, Pallas kernels for 17%

profile of v4, /device:TPU:0, one launch (start us, length us, event | category | flops | bytes accessed | tf_op | source)
XLA Modules:
  0.0 116.9 jit_solution(3272422553345008757)
XLA Ops:
  0.6 3.0 %collective-permute-start.2 = (bf16[320,1024]{1,0:T(8,128)(2,1)}, bf16[320,1024]{1,0:T(8,128)(2,1)S(1)}, u32[]{:S(2)}, u32[]{:S(2)}) collective-permute-start(bf16[320,1024]{1,0:T(8,128)(2,1)} %bitcast.14), channel_id=1, source_target_pairs={{0,1},{1,0},{2,3},{3,2},{4,5},{5,4},{6,7},{7,6},{8,9},{9,8},{10,11... | collective-permute-start | bytes 1966088 | tf_op jit(solution)/shard_map/ppermute | solution.py:25
  3.6 1.5 %collective-permute-start.3 = (bf16[320,1024]{1,0:T(8,128)(2,1)}, bf16[320,1024]{1,0:T(8,128)(2,1)S(1)}, u32[]{:S(2)}, u32[]{:S(2)}) collective-permute-start(bf16[320,1024]{1,0:T(8,128)(2,1)} %bitcast.15), channel_id=1, source_target_pairs={{0,2},{1,3},{2,0},{3,1},{4,6},{5,7},{6,4},{7,5},{8,10},{9,11},{10,... | collective-permute-start | bytes 1966088 | tf_op jit(solution)/shard_map/ppermute | solution.py:25
  5.2 1.1 copy-done.3
  6.4 2.7 %collective-permute-start = (bf16[320,512]{1,0:T(8,128)(2,1)S(1)}, bf16[320,512]{1,0:T(8,128)(2,1)S(1)}, u32[]{:S(2)}, u32[]{:S(2)}) collective-permute-start(bf16[320,512]{1,0:T(8,128)(2,1)S(1)} %get-tuple-element.53.refs_0_), channel_id=1, source_target_pairs={{0,16},{4,20},{8,24},{12,28},{16,0},{20,4},{24,8},{28,12},{1,17},{... | collective-permute-start | bytes 983048 | tf_op jit(solution)/shard_map/ppermute | solution.py:25
  9.0 0.7 broadcast_in_dim.16.gain
  9.7 0.7 broadcast_in_dim.17.merge_gain
  10.4 1.9 %copy-done.1 = bf16[4,320,1280]{2,1,0:T(8,128)(2,1)S(1)} copy-done((bf16[4,320,1280]{2,1,0:T(8,128)(2,1)S(1)}, bf16[4,320,1280]{2,1,0:T(8,128)(2,1)}, u32[]{:S(2)}) %copy-start.1) | copy-done | bytes 3276824
  12.3 1.1 copy-done.2
  13.5 0.7 copy-done.4
  14.2 0.7 copy-done.6
  14.9 1.6 %prepare.1 = (bf16[1280,320]{1,0:T(8,128)(2,1)S(1)}, bf16[1280,1280]{1,0:T(8,128)(2,1)S(1)}, f32[1280,128]{1,0:T(8,128)S(1)}, f32[1280,128]{1,0:T(8,128)S(1)}, b...) custom-call(bf16[320,1280]{1,0:T(8,128)(2,1)S(1)} %copy-done.2, bf16[1280,1280]{1,0:T(8,128)(2,1)S(1)} %bitcast.13, ...), custom_call_target="tpu_custom_call" | custom-call | tf_op jit(solution)/shard_map/prepare/pallas_call | solution.py:41
  16.5 2.1 %collective-permute-done.2.refs_2_ = bf16[320,1024]{1,0:T(8,128)(2,1)S(1)} collective-permute-done((bf16[320,1024]{1,0:T(8,128)(2,1)}, bf16[320,1024]{1,0:T(8,128)(2,1)S(1)}, u32[]{:S(2)}, u32[]{:S(2)}) %collective-permute-start.2) | collective-permute-done | bytes 655392 | tf_op jit(solution)/shard_map/ppermute | solution.py:25
  18.6 1.8 %collective-permute-start.4 = (bf16[160,1024]{1,0:T(8,128)(2,1)S(1)}, bf16[160,1024]{1,0:T(8,128)(2,1)S(1)}, u32[]{:S(2)}, u32[]{:S(2)}) collective-permute-start(bf16[160,1024]{1,0:T(8,128)(2,1)S(1)} %slice.18), channel_id=1, source_target_pairs={{0,2},{1,3},{2,0},{3,1},{4,6},{5,7},{6,4},{7,5},{8,10},{9,11},{10,... | collective-permute-start | bytes 983048 | tf_op jit(solution)/shard_map/ppermute | solution.py:25
  20.5 1.6 %collective-permute-start.5 = (bf16[160,1024]{1,0:T(8,128)(2,1)S(1)}, bf16[160,1024]{1,0:T(8,128)(2,1)S(1)}, u32[]{:S(2)}, u32[]{:S(2)}) collective-permute-start(bf16[160,1024]{1,0:T(8,128)(2,1)S(1)} %slice.24), channel_id=1, source_target_pairs={{0,1},{1,0},{2,3},{3,2},{4,5},{5,4},{6,7},{7,6},{8,9},{9,8},{10,11... | collective-permute-start | bytes 983048 | tf_op jit(solution)/shard_map/ppermute | solution.py:25
  22.0 1.2 %collective-permute-done.refs_0_ = bf16[320,512]{1,0:T(8,128)(2,1)S(1)} collective-permute-done((bf16[320,512]{1,0:T(8,128)(2,1)S(1)}, bf16[320,512]{1,0:T(8,128)(2,1)S(1)}, u32[]{:S(2)}, u32[]{:S(2)}) %collective-permute-start) | collective-permute-done | bytes 327712 | tf_op jit(solution)/shard_map/ppermute | solution.py:25
  23.2 1.4 %collective-permute-start.1 = (bf16[320,512]{1,0:T(8,128)(2,1)S(1)}, bf16[320,512]{1,0:T(8,128)(2,1)S(1)}, u32[]{:S(2)}, u32[]{:S(2)}) collective-permute-start(bf16[320,512]{1,0:T(8,128)(2,1)S(1)} %get-tuple-element.55.refs_1_.refs_4_), channel_id=1, source_target_pairs={{0,16},{4,20},{8,24},{12,28},{16,0},{20,4},{24,8},{28,12},{1,17},{... | collective-permute-start | bytes 983048 | tf_op jit(solution)/shard_map/ppermute | solution.py:25
  24.6 2.9 %collective-permute-done.4.refs_4_ = bf16[160,1024]{1,0:T(8,128)(2,1)S(1)} collective-permute-done((bf16[160,1024]{1,0:T(8,128)(2,1)S(1)}, bf16[160,1024]{1,0:T(8,128)(2,1)S(1)}, u32[]{:S(2)}, u32[]{:S(2)}) %collective-permute-start.4) | collective-permute-done | bytes 327712 | tf_op jit(solution)/shard_map/ppermute | solution.py:25
  27.6 1.3 %collective-permute-done.5.refs_5_ = bf16[160,1024]{1,0:T(8,128)(2,1)S(1)} collective-permute-done((bf16[160,1024]{1,0:T(8,128)(2,1)S(1)}, bf16[160,1024]{1,0:T(8,128)(2,1)S(1)}, u32[]{:S(2)}, u32[]{:S(2)}) %collective-permute-start.5) | collective-permute-done | bytes 327712 | tf_op jit(solution)/shard_map/ppermute | solution.py:25
  28.8 1.5 %collective-permute-start.6 = (bf16[320,512]{1,0:T(8,128)(2,1)S(1)}, bf16[320,512]{1,0:T(8,128)(2,1)S(1)}, u32[]{:S(2)}, u32[]{:S(2)}) collective-permute-start(bf16[320,512]{1,0:T(8,128)(2,1)S(1)} %collective-permute-done.refs_0_), channel_id=1, source_target_pairs={{0,1},{1,0},{2,3},{3,2},{4,5},{5,4},{6,7},{7,6},{8,9},{9,8},{10,11... | collective-permute-start | bytes 983048 | tf_op jit(solution)/shard_map/ppermute | solution.py:25
  30.3 0.5 collective-permute-start.7
  30.8 5.5 %project.3 = (bf16[384,1024]{1,0:T(8,128)(2,1)S(1)}, bf16[1024,512]{1,0:T(8,128)(2,1)S(1)}, bf16[384,1024]{1,0:T(8,128)(2,1)S(1)}) custom-call(bf16[320,512]{1,0:T(8,128)(2,1)S(1)} %get-tuple-element.53.refs_0_, bf16[320,512]{1,0:T(8,128)(2,1)S(1)} %get-tuple-element.55.refs_1_.refs_4_, bf16[320,1024]{1,0:T(8,128)(2,1)S(1)} %collective-permute-done.2.refs_2_, ...), custom_call_target="tpu_custom_call" | custom-call | tf_op jit(solution)/shard_map/project/pallas_call | solution.py:41
  36.4 3.3 %collective-permute-done.1.refs_0_ = bf16[320,512]{1,0:T(8,128)(2,1)S(1)} collective-permute-done((bf16[320,512]{1,0:T(8,128)(2,1)S(1)}, bf16[320,512]{1,0:T(8,128)(2,1)S(1)}, u32[]{:S(2)}, u32[]{:S(2)}) %collective-permute-start.1) | collective-permute-done | bytes 327712 | tf_op jit(solution)/shard_map/ppermute | solution.py:25
  39.7 0.5 collective-permute-start.8
  40.3 0.6 collective-permute-start.9
  40.8 0.8 collective-permute-start.10
  41.6 1.0 collective-permute-start.13
  42.7 1.6 %collective-permute-start.14 = (bf16[160,512]{1,0:T(8,128)(2,1)S(1)}, bf16[160,512]{1,0:T(8,128)(2,1)S(1)}, u32[]{:S(2)}, u32[]{:S(2)}) collective-permute-start(bf16[160,512]{1,0:T(8,128)(2,1)S(1)} %slice.26), channel_id=1, source_target_pairs={{0,1},{1,0},{2,3},{3,2},{4,5},{5,4},{6,7},{7,6},{8,9},{9,8},{10,11... | collective-permute-start | bytes 491528 | tf_op jit(solution)/shard_map/ppermute | solution.py:25
  44.3 6.4 %near.1 = (f32[384,512]{1,0:T(8,128)S(1)}, f32[8,512]{1,0:T(8,128)S(1)}, f32[384,512]{1,0:T(8,128)S(1)}, f32[8,512]{1,0:T(8,128)S(1)}) custom-call(s32[1024]{0:T(1024)S(1)} %copy-done.4, bf16[384,1024]{1,0:T(8,128)(2,1)S(1)} %get-tuple-element.64.q, bf16[1024,512]{1,0:T(8,128)(2,1)S(1)} %get-tuple-element.60.k, bf16[384,1024]{1,0:T(8,128)(2,1)S(1)} %get-tuple-element.65.v), custom_call_target="tpu_custom_call" | custom-call | tf_op jit(solution)/shard_map/near/pallas_call | solution.py:41
  50.7 0.6 collective-permute-start.11
  51.3 1.2 %collective-permute-start.12 = (bf16[160,512]{1,0:T(8,128)(2,1)S(1)}, bf16[160,512]{1,0:T(8,128)(2,1)S(1)}, u32[]{:S(2)}, u32[]{:S(2)}) collective-permute-start(bf16[160,512]{1,0:T(8,128)(2,1)S(1)} %slice.23), channel_id=1, source_target_pairs={{0,1},{1,0},{2,3},{3,2},{4,5},{5,4},{6,7},{7,6},{8,9},{9,8},{10,11... | collective-permute-start | bytes 491528 | tf_op jit(solution)/shard_map/ppermute | solution.py:25
  52.9 2.1 %project.5 = (bf16[512,512]{1,0:T(8,128)(2,1)S(1)}, bf16[384,512]{1,0:T(8,128)(2,1)S(1)}) custom-call(bf16[320,512]{1,0:T(8,128)(2,1)S(1)} %collective-permute-done.refs_0_, bf16[320,512]{1,0:T(8,128)(2,1)S(1)} %collective-permute-done.6.refs_1_, bf16[320,512]{1,0:T(8,128)(2,1)S(1)} %collective-permute-done.7.refs_2_, ...), custom_call_target="tpu_custom_call" | custom-call | tf_op jit(solution)/shard_map/project/pallas_call | solution.py:41
  55.0 2.9 %middle.1 = (f32[384,512]{1,0:T(8,128)S(1)}, f32[8,512]{1,0:T(8,128)S(1)}, f32[384,512]{1,0:T(8,128)S(1)}, f32[8,512]{1,0:T(8,128)S(1)}) custom-call(s32[1024]{0:T(1024)S(1)} %copy-done.5, s32[1024]{0:T(1024)S(1)} %collective-permute-done.10.k_ids, bf16[384,1024]{1,0:T(8,128)(2,1)S(1)} %get-tuple-element.64.q, bf16[512,512]{1,0:T(8,128)(2,1)S(1)} %get-tuple-element.72.k, ...), custom_call_target="tpu_custom_call" | custom-call | tf_op jit(solution)/shard_map/middle/pallas_call | solution.py:41
  58.0 2.1 %project.4 = (bf16[512,512]{1,0:T(8,128)(2,1)S(1)}, bf16[384,512]{1,0:T(8,128)(2,1)S(1)}) custom-call(bf16[320,512]{1,0:T(8,128)(2,1)S(1)} %collective-permute-done.1.refs_0_, bf16[320,512]{1,0:T(8,128)(2,1)S(1)} %collective-permute-done.8.refs_1_, bf16[320,512]{1,0:T(8,128)(2,1)S(1)} %collective-permute-done.9.refs_2_, ...), custom_call_target="tpu_custom_call" | custom-call | tf_op jit(solution)/shard_map/project/pallas_call | solution.py:41
  60.1 1.7 %last.1 = (bf16[320,1024]{1,0:T(8,128)(2,1)S(1)}, bf16[320,512]{1,0:T(8,128)(2,1)S(1)}, bf16[320,512]{1,0:T(8,128)(2,1)S(1)}) custom-call(s32[1024]{0:T(1024)S(1)} %copy-done.5, s32[1024]{0:T(1024)S(1)} %collective-permute-done.10.k_ids, bf16[384,1024]{1,0:T(8,128)(2,1)S(1)} %get-tuple-element.64.q, bf16[512,512]{1,0:T(8,128)(2,1)S(1)} %get-tuple-element.70.k, ...), custom_call_target="tpu_custom_call" | custom-call | tf_op jit(solution)/shard_map/last/pallas_call | solution.py:41
  61.8 1.3 %collective-permute-start.19 = (bf16[320,512]{1,0:T(8,128)(2,1)S(1)}, bf16[320,512]{1,0:T(8,128)(2,1)S(1)}, u32[]{:S(2)}, u32[]{:S(2)}) collective-permute-start(bf16[320,512]{1,0:T(8,128)(2,1)S(1)} %get-tuple-element.89), channel_id=1, source_target_pairs={{0,2},{1,3},{2,0},{3,1},{4,6},{5,7},{6,4},{7,5},{8,10},{9,11},{10,... | collective-permute-start | bytes 983048 | tf_op jit(solution)/shard_map/ppermute | solution.py:25
  63.1 0.8 collective-permute-start.16
  63.9 1.2 %rest.1 = (bf16[320,512]{1,0:T(8,128)(2,1)S(1)}, bf16[320,512]{1,0:T(8,128)(2,1)S(1)}, bf16[320,512]{1,0:T(8,128)(2,1)S(1)}, bf16[320,512]{1,0:T(8,128)(2,1)S(1)...) custom-call(bf16[320,1024]{1,0:T(8,128)(2,1)S(1)} %get-tuple-element.81.ctx, ...), custom_call_target="tpu_custom_call" | custom-call | tf_op jit(solution)/shard_map/rest/pallas_call | solution.py:41
  65.1 1.3 %collective-permute-start.15 = (bf16[320,512]{1,0:T(8,128)(2,1)S(1)}, bf16[320,512]{1,0:T(8,128)(2,1)S(1)}, u32[]{:S(2)}, u32[]{:S(2)}) collective-permute-start(bf16[320,512]{1,0:T(8,128)(2,1)S(1)} %get-tuple-element.83), channel_id=1, source_target_pairs={{0,1},{1,0},{2,3},{3,2},{4,5},{5,4},{6,7},{7,6},{8,9},{9,8},{10,11... | collective-permute-start | bytes 983048 | tf_op jit(solution)/shard_map/ppermute | solution.py:25
  66.4 0.8 collective-permute-start.18
  67.2 5.3 %collective-permute-done.19 = bf16[320,512]{1,0:T(8,128)(2,1)S(1)} collective-permute-done((bf16[320,512]{1,0:T(8,128)(2,1)S(1)}, bf16[320,512]{1,0:T(8,128)(2,1)S(1)}, u32[]{:S(2)}, u32[]{:S(2)}) %collective-permute-start.19) | collective-permute-done | bytes 327712 | tf_op jit(solution)/shard_map/ppermute | solution.py:25
  72.6 1.6 %collective-permute-start.20 = (bf16[320,512]{1,0:T(8,128)(2,1)S(1)}, bf16[320,512]{1,0:T(8,128)(2,1)S(1)}, u32[]{:S(2)}, u32[]{:S(2)}) collective-permute-start(bf16[320,512]{1,0:T(8,128)(2,1)S(1)} %add_convert_fusion), channel_id=1, source_target_pairs={{0,1},{1,0},{2,3},{3,2},{4,5},{5,4},{6,7},{7,6},{8,9},{9,8},{10,11... | collective-permute-start | bytes 983048 | tf_op jit(solution)/shard_map/ppermute | solution.py:25
  74.3 0.5 collective-permute-start.17
  74.8 3.8 %collective-permute-done.15.refs_2_ = bf16[320,512]{1,0:T(8,128)(2,1)S(1)} collective-permute-done((bf16[320,512]{1,0:T(8,128)(2,1)S(1)}, bf16[320,512]{1,0:T(8,128)(2,1)S(1)}, u32[]{:S(2)}, u32[]{:S(2)}) %collective-permute-start.15) | collective-permute-done | bytes 327712 | tf_op jit(solution)/shard_map/ppermute | solution.py:25
  78.6 3.9 %collective-permute-done.20.refs_7_ = bf16[320,512]{1,0:T(8,128)(2,1)S(1)} collective-permute-done((bf16[320,512]{1,0:T(8,128)(2,1)S(1)}, bf16[320,512]{1,0:T(8,128)(2,1)S(1)}, u32[]{:S(2)}, u32[]{:S(2)}) %collective-permute-start.20) | collective-permute-done | bytes 327712 | tf_op jit(solution)/shard_map/ppermute | solution.py:25
  82.5 1.7 %hidden.1 = (bf16[320,1024]{1,0:T(8,128)(2,1)}, bf16[320,1024]{1,0:T(8,128)(2,1)S(1)}, f32[8,1024]{1,0:T(8,128)S(1)}) custom-call(bf16[320,512]{1,0:T(8,128)(2,1)S(1)} %get-tuple-element.53.refs_0_, bf16[320,512]{1,0:T(8,128)(2,1)S(1)} %get-tuple-element.82.refs_1_, bf16[320,512]{1,0:T(8,128)(2,1)S(1)} %collective-permute-done.15.refs_2_, ...), custom_call_target="tpu_custom_call" | custom-call | tf_op jit(solution)/shard_map/hidden/pallas_call | solution.py:41
  84.2 1.5 %collective-permute-start.21 = (f32[8,1024]{1,0:T(8,128)S(1)}, f32[8,1024]{1,0:T(8,128)S(1)}, u32[]{:S(2)}, u32[]{:S(2)}) collective-permute-start(f32[8,1024]{1,0:T(8,128)S(1)} %get-tuple-element.92.refs_0_), channel_id=1, source_target_pairs={{0,1},{1,0},{2,3},{3,2},{4,5},{5,4},{6,7},{7,6},{8,9},{9,8},{10,11... | collective-permute-start | bytes 98312 | tf_op jit(solution)/shard_map/ppermute | solution.py:25
  85.7 1.3 %collective-permute-start.22 = (f32[8,1024]{1,0:T(8,128)S(1)}, f32[8,1024]{1,0:T(8,128)S(1)}, u32[]{:S(2)}, u32[]{:S(2)}) collective-permute-start(f32[8,1024]{1,0:T(8,128)S(1)} %get-tuple-element.92.refs_0_), channel_id=1, source_target_pairs={{0,2},{1,3},{2,0},{3,1},{4,6},{5,7},{6,4},{7,5},{8,10},{9,11},{10,... | collective-permute-start | bytes 98312 | tf_op jit(solution)/shard_map/ppermute | solution.py:25
  87.0 0.7 collective-permute-start.23
  88.1 1.5 %collective-permute-done.22.refs_2_ = f32[8,1024]{1,0:T(8,128)S(1)} collective-permute-done((f32[8,1024]{1,0:T(8,128)S(1)}, f32[8,1024]{1,0:T(8,128)S(1)}, u32[]{:S(2)}, u32[]{:S(2)}) %collective-permute-start.22) | collective-permute-done | bytes 32800 | tf_op jit(solution)/shard_map/ppermute | solution.py:25
  89.6 2.7 %collective-permute-done.23.refs_3_ = f32[8,1024]{1,0:T(8,128)S(1)} collective-permute-done((f32[8,1024]{1,0:T(8,128)S(1)}, f32[8,1024]{1,0:T(8,128)S(1)}, u32[]{:S(2)}, u32[]{:S(2)}) %collective-permute-start.23) | collective-permute-done | bytes 32800 | tf_op jit(solution)/shard_map/ppermute | solution.py:25
  92.3 1.8 %merge.1 = (bf16[320,256]{1,0:T(8,128)(2,1)S(1)}, bf16[320,256]{1,0:T(8,128)(2,1)S(1)}, bf16[320,256]{1,0:T(8,128)(2,1)S(1)}, bf16[320,256]{1,0:T(8,128)(2,1)S(1)}) custom-call(bf16[320,1024]{1,0:T(8,128)(2,1)S(1)} %get-tuple-element.91.source, f32[8,1024]{1,0:T(8,128)S(1)} %get-tuple-element.92.refs_0_, f32[8,1024]{1,0:T(8,128)S(1)} %collective-permute-done.21.refs_1_, ...), custom_call_target="tpu_custom_call" | custom-call | tf_op jit(solution)/shard_map/merge/pallas_call | solution.py:41
  94.1 0.9 collective-permute-start.24
  95.0 1.3 %collective-permute-start.25 = (bf16[320,256]{1,0:T(8,128)(2,1)S(1)}, bf16[320,256]{1,0:T(8,128)(2,1)S(1)}, u32[]{:S(2)}, u32[]{:S(2)}) collective-permute-start(bf16[320,256]{1,0:T(8,128)(2,1)S(1)} %get-tuple-element.96), channel_id=1, source_target_pairs={{0,1},{1,0},{2,3},{3,2},{4,5},{5,4},{6,7},{7,6},{8,9},{9,8},{10,11... | collective-permute-start | bytes 491528 | tf_op jit(solution)/shard_map/ppermute | solution.py:25
  96.4 1.3 %collective-permute-start.26 = (bf16[320,256]{1,0:T(8,128)(2,1)S(1)}, bf16[320,256]{1,0:T(8,128)(2,1)S(1)}, u32[]{:S(2)}, u32[]{:S(2)}) collective-permute-start(bf16[320,256]{1,0:T(8,128)(2,1)S(1)} %get-tuple-element.97), channel_id=1, source_target_pairs={{0,2},{1,3},{2,0},{3,1},{4,6},{5,7},{6,4},{7,5},{8,10},{9,11},{10,... | collective-permute-start | bytes 491528 | tf_op jit(solution)/shard_map/ppermute | solution.py:25
  97.7 2.8 %collective-permute-done.24.refs_0_ = bf16[320,256]{1,0:T(8,128)(2,1)S(1)} collective-permute-done((bf16[320,256]{1,0:T(8,128)(2,1)S(1)}, bf16[320,256]{1,0:T(8,128)(2,1)S(1)}, u32[]{:S(2)}, u32[]{:S(2)}) %collective-permute-start.24) | collective-permute-done | bytes 163872 | tf_op jit(solution)/shard_map/ppermute | solution.py:25
  100.5 1.0 collective-permute-done.25.refs_1_
  101.4 0.7 collective-permute-done.26.refs_2_
  102.5 3.6 %collective-permute-start.27 = (bf16[320,128]{1,0:T(8,128)(2,1)S(1)}, bf16[320,128]{1,0:T(8,128)(2,1)S(1)}, u32[]{:S(2)}, u32[]{:S(2)}) collective-permute-start(bf16[320,128]{1,0:T(8,128)(2,1)S(1)} %get-tuple-element.101), channel_id=1, source_target_pairs={{0,8},{4,12},{8,0},{12,4},{16,24},{20,28},{24,16},{28,20},{1,9},{5... | collective-permute-start | bytes 245768 | tf_op jit(solution)/shard_map/ppermute | solution.py:25
  106.1 2.0 %collective-permute-start.28 = (bf16[320,128]{1,0:T(8,128)(2,1)S(1)}, bf16[320,128]{1,0:T(8,128)(2,1)S(1)}, u32[]{:S(2)}, u32[]{:S(2)}) collective-permute-start(bf16[320,128]{1,0:T(8,128)(2,1)S(1)} %get-tuple-element.102), channel_id=1, source_target_pairs={{0,16},{4,20},{8,24},{12,28},{16,0},{20,4},{24,8},{28,12},{1,17},{... | collective-permute-start | bytes 245768 | tf_op jit(solution)/shard_map/ppermute | solution.py:25
  108.1 0.5 collective-permute-start.29
  108.5 3.3 %collective-permute-done.28.refs_2_ = bf16[320,128]{1,0:T(8,128)(2,1)S(1)} collective-permute-done((bf16[320,128]{1,0:T(8,128)(2,1)S(1)}, bf16[320,128]{1,0:T(8,128)(2,1)S(1)}, u32[]{:S(2)}, u32[]{:S(2)}) %collective-permute-start.28) | collective-permute-done | bytes 81952 | tf_op jit(solution)/shard_map/ppermute | solution.py:25
  111.8 2.5 %collective-permute-done.29.refs_3_ = bf16[320,128]{1,0:T(8,128)(2,1)S(1)} collective-permute-done((bf16[320,128]{1,0:T(8,128)(2,1)S(1)}, bf16[320,128]{1,0:T(8,128)(2,1)S(1)}, u32[]{:S(2)}, u32[]{:S(2)}) %collective-permute-start.29) | collective-permute-done | bytes 81952 | tf_op jit(solution)/shard_map/ppermute | solution.py:25
  114.5 1.4 %collective-permute-done.30.refs_4_ = bf16[320,256]{1,0:T(8,128)(2,1)S(1)} collective-permute-done((bf16[320,256]{1,0:T(8,128)(2,1)S(1)}, bf16[320,256]{1,0:T(8,128)(2,1)S(1)}, u32[]{:S(2)}, u32[]{:S(2)}) %collective-permute-start.30) | collective-permute-done | bytes 163872 | tf_op jit(solution)/shard_map/ppermute | solution.py:25
  115.9 1.0 settle.1
  (36 shorter events, 1.7 us)
Async XLA Ops:
  0.6 30.2 %copy-start = (bf16[3,1280,320]{1,2,0:T(8,128)(2,1)S(1)}, bf16[3,1280,320]{1,2,0:T(8,128)(2,1)}, u32[]{:S(2)}) copy-start(bf16[3,1280,320]{1,2,0:T(8,128)(2,1)} %param.11) | copy-start | bytes 7372804
  0.6 17.9 %collective-permute-start.2 = (bf16[320,1024]{1,0:T(8,128)(2,1)}, bf16[320,1024]{1,0:T(8,128)(2,1)S(1)}, u32[]{:S(2)}, u32[]{:S(2)}) collective-permute-start(bf16[320,1024]{1,0:T(8,128)(2,1)} %bitcast.14), channel_id=1, source_target_pairs={{0,1},{1,0},{2,3},{3,2},{4,5},{5,4},{6,7},{7,6},{8,9},{9,8},{10,11... | collective-permute-start | bytes 1966088 | tf_op jit(solution)/shard_map/ppermute | solution.py:25
  3.6 16.8 %collective-permute-start.3 = (bf16[320,1024]{1,0:T(8,128)(2,1)}, bf16[320,1024]{1,0:T(8,128)(2,1)S(1)}, u32[]{:S(2)}, u32[]{:S(2)}) collective-permute-start(bf16[320,1024]{1,0:T(8,128)(2,1)} %bitcast.15), channel_id=1, source_target_pairs={{0,2},{1,3},{2,0},{3,1},{4,6},{5,7},{6,4},{7,5},{8,10},{9,11},{10,... | collective-permute-start | bytes 1966088 | tf_op jit(solution)/shard_map/ppermute | solution.py:25
  5.2 1.1 copy-start.3
  6.4 16.9 %collective-permute-start = (bf16[320,512]{1,0:T(8,128)(2,1)S(1)}, bf16[320,512]{1,0:T(8,128)(2,1)S(1)}, u32[]{:S(2)}, u32[]{:S(2)}) collective-permute-start(bf16[320,512]{1,0:T(8,128)(2,1)S(1)} %get-tuple-element.53.refs_0_), channel_id=1, source_target_pairs={{0,16},{4,20},{8,24},{12,28},{16,0},{20,4},{24,8},{28,12},{1,17},{... | collective-permute-start | bytes 983048 | tf_op jit(solution)/shard_map/ppermute | solution.py:25
  10.4 1.9 %copy-start.1 = (bf16[4,320,1280]{2,1,0:T(8,128)(2,1)S(1)}, bf16[4,320,1280]{2,1,0:T(8,128)(2,1)}, u32[]{:S(2)}) copy-start(bf16[4,320,1280]{2,1,0:T(8,128)(2,1)} %param.14) | copy-start | bytes 9830404
  12.3 1.1 copy-start.2
  13.5 0.7 copy-start.4
  14.2 0.7 copy-start.6
  18.6 9.0 %collective-permute-start.4 = (bf16[160,1024]{1,0:T(8,128)(2,1)S(1)}, bf16[160,1024]{1,0:T(8,128)(2,1)S(1)}, u32[]{:S(2)}, u32[]{:S(2)}) collective-permute-start(bf16[160,1024]{1,0:T(8,128)(2,1)S(1)} %slice.18), channel_id=1, source_target_pairs={{0,2},{1,3},{2,0},{3,1},{4,6},{5,7},{6,4},{7,5},{8,10},{9,11},{10,... | collective-permute-start | bytes 983048 | tf_op jit(solution)/shard_map/ppermute | solution.py:25
  20.5 8.4 %collective-permute-start.5 = (bf16[160,1024]{1,0:T(8,128)(2,1)S(1)}, bf16[160,1024]{1,0:T(8,128)(2,1)S(1)}, u32[]{:S(2)}, u32[]{:S(2)}) collective-permute-start(bf16[160,1024]{1,0:T(8,128)(2,1)S(1)} %slice.24), channel_id=1, source_target_pairs={{0,1},{1,0},{2,3},{3,2},{4,5},{5,4},{6,7},{7,6},{8,9},{9,8},{10,11... | collective-permute-start | bytes 983048 | tf_op jit(solution)/shard_map/ppermute | solution.py:25
  23.2 16.5 %collective-permute-start.1 = (bf16[320,512]{1,0:T(8,128)(2,1)S(1)}, bf16[320,512]{1,0:T(8,128)(2,1)S(1)}, u32[]{:S(2)}, u32[]{:S(2)}) collective-permute-start(bf16[320,512]{1,0:T(8,128)(2,1)S(1)} %get-tuple-element.55.refs_1_.refs_4_), channel_id=1, source_target_pairs={{0,16},{4,20},{8,24},{12,28},{16,0},{20,4},{24,8},{28,12},{1,17},{... | collective-permute-start | bytes 983048 | tf_op jit(solution)/shard_map/ppermute | solution.py:25
  28.8 10.9 %collective-permute-start.6 = (bf16[320,512]{1,0:T(8,128)(2,1)S(1)}, bf16[320,512]{1,0:T(8,128)(2,1)S(1)}, u32[]{:S(2)}, u32[]{:S(2)}) collective-permute-start(bf16[320,512]{1,0:T(8,128)(2,1)S(1)} %collective-permute-done.refs_0_), channel_id=1, source_target_pairs={{0,1},{1,0},{2,3},{3,2},{4,5},{5,4},{6,7},{7,6},{8,9},{9,8},{10,11... | collective-permute-start | bytes 983048 | tf_op jit(solution)/shard_map/ppermute | solution.py:25
  30.3 9.4 %collective-permute-start.7 = (bf16[320,512]{1,0:T(8,128)(2,1)S(1)}, bf16[320,512]{1,0:T(8,128)(2,1)S(1)}, u32[]{:S(2)}, u32[]{:S(2)}) collective-permute-start(bf16[320,512]{1,0:T(8,128)(2,1)S(1)} %collective-permute-done.refs_0_), channel_id=1, source_target_pairs={{0,2},{1,3},{2,0},{3,1},{4,6},{5,7},{6,4},{7,5},{8,10},{9,11},{10,... | collective-permute-start | bytes 983048 | tf_op jit(solution)/shard_map/ppermute | solution.py:25
  39.7 11.0 %collective-permute-start.8 = (bf16[320,512]{1,0:T(8,128)(2,1)S(1)}, bf16[320,512]{1,0:T(8,128)(2,1)S(1)}, u32[]{:S(2)}, u32[]{:S(2)}) collective-permute-start(bf16[320,512]{1,0:T(8,128)(2,1)S(1)} %collective-permute-done.1.refs_0_), channel_id=1, source_target_pairs={{0,1},{1,0},{2,3},{3,2},{4,5},{5,4},{6,7},{7,6},{8,9},{9,8},{10,11... | collective-permute-start | bytes 983048 | tf_op jit(solution)/shard_map/ppermute | solution.py:25
  40.3 10.5 %collective-permute-start.9 = (bf16[320,512]{1,0:T(8,128)(2,1)S(1)}, bf16[320,512]{1,0:T(8,128)(2,1)S(1)}, u32[]{:S(2)}, u32[]{:S(2)}) collective-permute-start(bf16[320,512]{1,0:T(8,128)(2,1)S(1)} %collective-permute-done.1.refs_0_), channel_id=1, source_target_pairs={{0,2},{1,3},{2,0},{3,1},{4,6},{5,7},{6,4},{7,5},{8,10},{9,11},{10,... | collective-permute-start | bytes 983048 | tf_op jit(solution)/shard_map/ppermute | solution.py:25
  40.8 9.9 %collective-permute-start.10 = (s32[1024]{0:T(1024)S(1)}, s32[1024]{0:T(1024)S(1)}, u32[]{:S(2)}, u32[]{:S(2)}) collective-permute-start(s32[1024]{0:T(1024)S(1)} %copy-done.4), channel_id=1, source_target_pairs={{0,16},{4,20},{8,24},{12,28},{16,0},{20,4},{24,8},{28,12},{1,17},{... | collective-permute-start | bytes 12296 | tf_op jit(solution)/shard_map/ppermute | solution.py:25
  41.6 11.3 %collective-permute-start.13 = (bf16[160,512]{1,0:T(8,128)(2,1)S(1)}, bf16[160,512]{1,0:T(8,128)(2,1)S(1)}, u32[]{:S(2)}, u32[]{:S(2)}) collective-permute-start(bf16[160,512]{1,0:T(8,128)(2,1)S(1)} %slice.25), channel_id=1, source_target_pairs={{0,2},{1,3},{2,0},{3,1},{4,6},{5,7},{6,4},{7,5},{8,10},{9,11},{10,... | collective-permute-start | bytes 491528 | tf_op jit(solution)/shard_map/ppermute | solution.py:25
  42.7 10.2 %collective-permute-start.14 = (bf16[160,512]{1,0:T(8,128)(2,1)S(1)}, bf16[160,512]{1,0:T(8,128)(2,1)S(1)}, u32[]{:S(2)}, u32[]{:S(2)}) collective-permute-start(bf16[160,512]{1,0:T(8,128)(2,1)S(1)} %slice.26), channel_id=1, source_target_pairs={{0,1},{1,0},{2,3},{3,2},{4,5},{5,4},{6,7},{7,6},{8,9},{9,8},{10,11... | collective-permute-start | bytes 491528 | tf_op jit(solution)/shard_map/ppermute | solution.py:25
  44.3 10.7 %copy-start.5 = (s32[1024]{0:T(1024)S(1)}, s32[1024]{0:T(1024)}, u32[]{:S(2)}) copy-start(s32[1024]{0:T(1024)} %q_ids.5) | copy-start | bytes 12292
  50.7 7.2 %collective-permute-start.11 = (bf16[160,512]{1,0:T(8,128)(2,1)S(1)}, bf16[160,512]{1,0:T(8,128)(2,1)S(1)}, u32[]{:S(2)}, u32[]{:S(2)}) collective-permute-start(bf16[160,512]{1,0:T(8,128)(2,1)S(1)} %slice.22), channel_id=1, source_target_pairs={{0,2},{1,3},{2,0},{3,1},{4,6},{5,7},{6,4},{7,5},{8,10},{9,11},{10,... | collective-permute-start | bytes 491528 | tf_op jit(solution)/shard_map/ppermute | solution.py:25
  51.3 6.6 %collective-permute-start.12 = (bf16[160,512]{1,0:T(8,128)(2,1)S(1)}, bf16[160,512]{1,0:T(8,128)(2,1)S(1)}, u32[]{:S(2)}, u32[]{:S(2)}) collective-permute-start(bf16[160,512]{1,0:T(8,128)(2,1)S(1)} %slice.23), channel_id=1, source_target_pairs={{0,1},{1,0},{2,3},{3,2},{4,5},{5,4},{6,7},{7,6},{8,9},{9,8},{10,11... | collective-permute-start | bytes 491528 | tf_op jit(solution)/shard_map/ppermute | solution.py:25
  61.8 10.7 %collective-permute-start.19 = (bf16[320,512]{1,0:T(8,128)(2,1)S(1)}, bf16[320,512]{1,0:T(8,128)(2,1)S(1)}, u32[]{:S(2)}, u32[]{:S(2)}) collective-permute-start(bf16[320,512]{1,0:T(8,128)(2,1)S(1)} %get-tuple-element.89), channel_id=1, source_target_pairs={{0,2},{1,3},{2,0},{3,1},{4,6},{5,7},{6,4},{7,5},{8,10},{9,11},{10,... | collective-permute-start | bytes 983048 | tf_op jit(solution)/shard_map/ppermute | solution.py:25
  63.1 11.1 %collective-permute-start.16 = (bf16[320,512]{1,0:T(8,128)(2,1)S(1)}, bf16[320,512]{1,0:T(8,128)(2,1)S(1)}, u32[]{:S(2)}, u32[]{:S(2)}) collective-permute-start(bf16[320,512]{1,0:T(8,128)(2,1)S(1)} %get-tuple-element.85), channel_id=1, source_target_pairs={{0,1},{1,0},{2,3},{3,2},{4,5},{5,4},{6,7},{7,6},{8,9},{9,8},{10,11... | collective-permute-start | bytes 983048 | tf_op jit(solution)/shard_map/ppermute | solution.py:25
  65.1 13.5 %collective-permute-start.15 = (bf16[320,512]{1,0:T(8,128)(2,1)S(1)}, bf16[320,512]{1,0:T(8,128)(2,1)S(1)}, u32[]{:S(2)}, u32[]{:S(2)}) collective-permute-start(bf16[320,512]{1,0:T(8,128)(2,1)S(1)} %get-tuple-element.83), channel_id=1, source_target_pairs={{0,1},{1,0},{2,3},{3,2},{4,5},{5,4},{6,7},{7,6},{8,9},{9,8},{10,11... | collective-permute-start | bytes 983048 | tf_op jit(solution)/shard_map/ppermute | solution.py:25
  66.4 12.2 %collective-permute-start.18 = (bf16[320,512]{1,0:T(8,128)(2,1)S(1)}, bf16[320,512]{1,0:T(8,128)(2,1)S(1)}, u32[]{:S(2)}, u32[]{:S(2)}) collective-permute-start(bf16[320,512]{1,0:T(8,128)(2,1)S(1)} %get-tuple-element.87), channel_id=1, source_target_pairs={{0,2},{1,3},{2,0},{3,1},{4,6},{5,7},{6,4},{7,5},{8,10},{9,11},{10,... | collective-permute-start | bytes 983048 | tf_op jit(solution)/shard_map/ppermute | solution.py:25
  72.6 9.9 %collective-permute-start.20 = (bf16[320,512]{1,0:T(8,128)(2,1)S(1)}, bf16[320,512]{1,0:T(8,128)(2,1)S(1)}, u32[]{:S(2)}, u32[]{:S(2)}) collective-permute-start(bf16[320,512]{1,0:T(8,128)(2,1)S(1)} %add_convert_fusion), channel_id=1, source_target_pairs={{0,1},{1,0},{2,3},{3,2},{4,5},{5,4},{6,7},{7,6},{8,9},{9,8},{10,11... | collective-permute-start | bytes 983048 | tf_op jit(solution)/shard_map/ppermute | solution.py:25
  74.3 8.2 %collective-permute-start.17 = (bf16[320,512]{1,0:T(8,128)(2,1)S(1)}, bf16[320,512]{1,0:T(8,128)(2,1)S(1)}, u32[]{:S(2)}, u32[]{:S(2)}) collective-permute-start(bf16[320,512]{1,0:T(8,128)(2,1)S(1)} %add_convert_fusion.1), channel_id=1, source_target_pairs={{0,2},{1,3},{2,0},{3,1},{4,6},{5,7},{6,4},{7,5},{8,10},{9,11},{10,... | collective-permute-start | bytes 983048 | tf_op jit(solution)/shard_map/ppermute | solution.py:25
  84.2 3.9 %collective-permute-start.21 = (f32[8,1024]{1,0:T(8,128)S(1)}, f32[8,1024]{1,0:T(8,128)S(1)}, u32[]{:S(2)}, u32[]{:S(2)}) collective-permute-start(f32[8,1024]{1,0:T(8,128)S(1)} %get-tuple-element.92.refs_0_), channel_id=1, source_target_pairs={{0,1},{1,0},{2,3},{3,2},{4,5},{5,4},{6,7},{7,6},{8,9},{9,8},{10,11... | collective-permute-start | bytes 98312 | tf_op jit(solution)/shard_map/ppermute | solution.py:25
  85.7 3.9 %collective-permute-start.22 = (f32[8,1024]{1,0:T(8,128)S(1)}, f32[8,1024]{1,0:T(8,128)S(1)}, u32[]{:S(2)}, u32[]{:S(2)}) collective-permute-start(f32[8,1024]{1,0:T(8,128)S(1)} %get-tuple-element.92.refs_0_), channel_id=1, source_target_pairs={{0,2},{1,3},{2,0},{3,1},{4,6},{5,7},{6,4},{7,5},{8,10},{9,11},{10,... | collective-permute-start | bytes 98312 | tf_op jit(solution)/shard_map/ppermute | solution.py:25
  87.0 5.3 %collective-permute-start.23 = (f32[8,1024]{1,0:T(8,128)S(1)}, f32[8,1024]{1,0:T(8,128)S(1)}, u32[]{:S(2)}, u32[]{:S(2)}) collective-permute-start(f32[8,1024]{1,0:T(8,128)S(1)} %get-tuple-element.92.refs_0_), channel_id=1, source_target_pairs={{0,3},{1,2},{2,1},{3,0},{4,7},{5,6},{6,5},{7,4},{8,11},{9,10},{10,... | collective-permute-start | bytes 98312 | tf_op jit(solution)/shard_map/ppermute | solution.py:25
  94.1 6.3 %collective-permute-start.24 = (bf16[320,256]{1,0:T(8,128)(2,1)S(1)}, bf16[320,256]{1,0:T(8,128)(2,1)S(1)}, u32[]{:S(2)}, u32[]{:S(2)}) collective-permute-start(bf16[320,256]{1,0:T(8,128)(2,1)S(1)} %get-tuple-element.95), channel_id=1, source_target_pairs={{0,3},{1,2},{2,1},{3,0},{4,7},{5,6},{6,5},{7,4},{8,11},{9,10},{10,... | collective-permute-start | bytes 491528 | tf_op jit(solution)/shard_map/ppermute | solution.py:25
  95.0 6.4 %collective-permute-start.25 = (bf16[320,256]{1,0:T(8,128)(2,1)S(1)}, bf16[320,256]{1,0:T(8,128)(2,1)S(1)}, u32[]{:S(2)}, u32[]{:S(2)}) collective-permute-start(bf16[320,256]{1,0:T(8,128)(2,1)S(1)} %get-tuple-element.96), channel_id=1, source_target_pairs={{0,1},{1,0},{2,3},{3,2},{4,5},{5,4},{6,7},{7,6},{8,9},{9,8},{10,11... | collective-permute-start | bytes 491528 | tf_op jit(solution)/shard_map/ppermute | solution.py:25
  96.4 5.8 %collective-permute-start.26 = (bf16[320,256]{1,0:T(8,128)(2,1)S(1)}, bf16[320,256]{1,0:T(8,128)(2,1)S(1)}, u32[]{:S(2)}, u32[]{:S(2)}) collective-permute-start(bf16[320,256]{1,0:T(8,128)(2,1)S(1)} %get-tuple-element.97), channel_id=1, source_target_pairs={{0,2},{1,3},{2,0},{3,1},{4,6},{5,7},{6,4},{7,5},{8,10},{9,11},{10,... | collective-permute-start | bytes 491528 | tf_op jit(solution)/shard_map/ppermute | solution.py:25
  102.5 6.1 %collective-permute-start.27 = (bf16[320,128]{1,0:T(8,128)(2,1)S(1)}, bf16[320,128]{1,0:T(8,128)(2,1)S(1)}, u32[]{:S(2)}, u32[]{:S(2)}) collective-permute-start(bf16[320,128]{1,0:T(8,128)(2,1)S(1)} %get-tuple-element.101), channel_id=1, source_target_pairs={{0,8},{4,12},{8,0},{12,4},{16,24},{20,28},{24,16},{28,20},{1,9},{5... | collective-permute-start | bytes 245768 | tf_op jit(solution)/shard_map/ppermute | solution.py:25
  106.1 5.7 %collective-permute-start.28 = (bf16[320,128]{1,0:T(8,128)(2,1)S(1)}, bf16[320,128]{1,0:T(8,128)(2,1)S(1)}, u32[]{:S(2)}, u32[]{:S(2)}) collective-permute-start(bf16[320,128]{1,0:T(8,128)(2,1)S(1)} %get-tuple-element.102), channel_id=1, source_target_pairs={{0,16},{4,20},{8,24},{12,28},{16,0},{20,4},{24,8},{28,12},{1,17},{... | collective-permute-start | bytes 245768 | tf_op jit(solution)/shard_map/ppermute | solution.py:25
  108.1 6.2 %collective-permute-start.29 = (bf16[320,128]{1,0:T(8,128)(2,1)S(1)}, bf16[320,128]{1,0:T(8,128)(2,1)S(1)}, u32[]{:S(2)}, u32[]{:S(2)}) collective-permute-start(bf16[320,128]{1,0:T(8,128)(2,1)S(1)} %get-tuple-element.103), channel_id=1, source_target_pairs={{0,24},{4,28},{8,16},{12,20},{16,8},{20,12},{24,0},{28,4},{1,25},{... | collective-permute-start | bytes 245768 | tf_op jit(solution)/shard_map/ppermute | solution.py:25
  114.5 1.5 %collective-permute-start.30 = (bf16[320,256]{1,0:T(8,128)(2,1)S(1)}, bf16[320,256]{1,0:T(8,128)(2,1)S(1)}, u32[]{:S(2)}, u32[]{:S(2)}) collective-permute-start(bf16[320,256]{1,0:T(8,128)(2,1)S(1)} %gather.1), channel_id=1, source_target_pairs={{0,4},{4,0},{8,12},{12,8},{16,20},{20,16},{24,28},{28,24},{1,5},{5... | collective-permute-start | bytes 491528 | tf_op jit(solution)/shard_map/ppermute | solution.py:25

commit v5 on v4

--- a/solution.py
+++ b/solution.py
@@ -53,7 +53,11 @@
 def prepare_body(
     crossing, w, w_merge, gain, merge_gain, owner, ids, *outs
 ):
-    w_back, w_tall, gain_wide, merge_wide, dispatch, ids_row = outs
+    w_back, w_tall, gain_wide, merge_wide, dispatch, ids_row, pick = outs
+    row = lax.broadcasted_iota(jnp.int32, pick.shape, 0)
+    col = lax.broadcasted_iota(jnp.int32, pick.shape, 1)
+    fourth = pick.shape[0] // 4
+    pick[...] = jnp.where(4 * (row % fourth) + row // fourth == col, 1.0, 0.0).astype(BF)
     ids_row[...] = ids[...]
     full = w.shape[1]
     for lo in range(0, full, PAD):
@@ -105,6 +109,7 @@
             ((full, PAD), F32),
             ((slots, count), BF),
             (ids.shape, jnp.int32),
+            ((ids.shape[1] // 2, ids.shape[1] // 2), BF),
         ],
         [],
     )
@@ -404,18 +409,28 @@
     )
 
 
+def fold_body(*refs):
+    out = refs[-1]
+    for lo in range(0, out.shape[1], PAD):
+        at = slice(lo, lo + PAD)
+        total = refs[0][:, at].astype(F32)
+        for r in refs[1:-1]:
+            total = total + r[:, at].astype(F32)
+        out[:, at] = total
+
+
+def fold(*terms):
+    return call(fold_body, "fold", list(terms), 0, [(terms[0].shape, F32)], [])[0]
+
+
 def merge_body(n_stats, n_out, source, *refs):
     stats = refs[:n_stats]
-    gain, w = refs[n_stats : n_stats + 2]
-    outs = refs[n_stats + 2 : n_stats + 2 + n_out]
-    scaled, blocks, pick = refs[-3:]
+    gain, pick, w = refs[n_stats : n_stats + 3]
+    outs = refs[n_stats + 3 : n_stats + 3 + n_out]
+    scaled, blocks = refs[-2:]
     width, rows = source.shape
     me = lax.axis_index("tp")
     own_gain = gain[pl.ds(pl.multiple_of(me * width, 16), width), :]
-    row = lax.broadcasted_iota(jnp.int32, pick.shape, 0)
-    col = lax.broadcasted_iota(jnp.int32, pick.shape, 1)
-    fourth = pick.shape[0] // 4
-    pick[...] = jnp.where(4 * (row % fourth) + row // fourth == col, 1.0, 0.0).astype(BF)
     for lo in range(0, rows, PAD):
         at = slice(lo, lo + PAD)
         means = [s[0:1, at] for s in stats]
@@ -447,19 +462,18 @@
         ).astype(BF)
 
 
-def merge(hidden, stats, gain, w, n_out):
+def merge(hidden, stats, gain, pick, w, n_out):
     width, rows = hidden.shape
     full = w.shape[0]
     return call(
         functools.partial(merge_body, len(stats), n_out),
         "merge",
-        [hidden, *stats, gain, w],
+        [hidden, *stats, gain, pick, w],
         0,
         [((full // n_out, rows // 4), BF) for _ in range(n_out)],
         [
             pltpu.VMEM((width, rows), BF),
             pltpu.VMEM((rows // 4, 4 * width), BF),
-            pltpu.VMEM((rows // 2, rows // 2), BF),
         ],
     )
 
@@ -544,7 +558,7 @@
     merged_count = row_count // 4
     cap_slots = max(2, merged_count // grp_count * 2)
     crossing = grp_count == 8
-    w_back, w_tall, gain, merge_wide, dispatch, ids_row = prepare(
+    w_back, w_tall, gain, merge_wide, dispatch, ids_row, pick = prepare(
         w_out,
         w_merge.reshape(4 * local_width, full_width),
         ln_gain,
@@ -569,9 +583,10 @@
         a = hop(tall, "tp", 1)
         b = hop(tall, "tp", 2)
         z0 = hop(h0, "grp", partner)
+        far_segment = hop(segment, "grp", partner)
         c = hop(after(a, w_back)[:mid], "tp", 2)
         d = hop(b[mid:], "tp", 1)
-        z1 = hop(after(h1, z0), "grp", partner)
+        z1 = hop(h1, "grp", partner)
         q, k, v = own_of(
             [
                 (h0, 0, 0, 0),
@@ -592,7 +607,6 @@
         zc0 = hop(ta0, "tp", 2)
         zd0 = hop(tb0, "tp", 1)
         states = near(segment, after(q, z1, ta0, tb0), k, v)
-        far_segment = hop(segment, "grp", partner)
         za1, zb1, far_segment = after((za1, zb1, far_segment), states[0][1])
         ta1, tb1 = za1[:mid], zb1[mid:]
         zc1 = hop(ta1, "tp", 2)
@@ -625,7 +639,9 @@
             side = hop(terms[side_hop], "tp", side_hop)
             passed = (terms[next_hop].astype(F32) + corners[i].astype(F32)).astype(BF)
             onward = hop(passed, "tp", next_hop)
-            groups.append((halves[i], terms[0], side, onward))
+            groups.append((fold(halves[i], terms[0], side), onward))
+        sums = [g[0] for g in groups]
+        groups = [(partial, after(onward, *sums)) for partial, onward in groups]
     else:
         groups = [
             (h, lax.psum_scatter(t, "tp", scatter_dimension=0, tiled=True))
@@ -637,7 +653,7 @@
     else:
         gathered = lax.all_gather(stats, "tp")
         all_stats = [gathered[n] for n in range(tp_count)]
-    merge_terms = merge(hidden, all_stats, merge_wide, w_tall, n_out)
+    merge_terms = merge(hidden, all_stats, merge_wide, pick, w_tall, n_out)
     if square:
         received = [hop(merge_terms[n], "tp", n) for n in (3, 1, 2)] + [merge_terms[0]]
     else:

time: 117 us -> 117 us (level)
  waiting for transfers between devices: 40.5 us -> 35.3 us
  starting transfers between devices: 39.7 us -> 44.6 us
    ppermute x31, waiting for transfers between devices: 40.5 us -> 35.3 us  [hop(): lax.ppermute(x, axis, [(i, i ^ distance) for i in range(lax.axis_size(axi...]
    ppermute x31, starting transfers between devices: 39.7 us -> 44.6 us  [hop(): lax.ppermute(x, axis, [(i, i ^ distance) for i in range(lax.axis_size(axi...]
    pallas_call x14 -> x16, Pallas kernels: 28.6 us -> 29.7 us  [call(): pl.pallas_call(body, in_specs=[place(i) for i in range(len(args))], out_s...]
  transfers between devices with their start and end apart: 31 -> 31, of which waited for: 18 -> 17; matrix products, arithmetic and copies ran while one was open for 1% -> 1% of each run, Pallas kernels for 17% -> 17%
where the time goes in v5:
time: 117 us; the launch traced here: 118 us
  starting transfers between devices  44.6 us (38%)
  waiting for transfers between devices  35.3 us (30%)
  Pallas kernels  29.7 us (25%)
  local copies, waits for them, and re-layouts  7.06 us (6%)
    ppermute x31, starting transfers between devices, hop(): lax.ppermute(x, axis, [(i, i ^ distance) for i in range(lax.axis_size(axi...  44.6 us
    ppermute x31, waiting for transfers between devices, hop(): lax.ppermute(x, axis, [(i, i ^ distance) for i in range(lax.axis_size(axi...  35.3 us
    pallas_call x16, Pallas kernels, call(): pl.pallas_call(body, in_specs=[place(i) for i in range(len(args))], out_s...  29.7 us
    unnamed x14, local copies, waits for them, and re-layouts  5.56 us
  transfers between devices with their start and end apart: 31, of which 17 were waited for; matrix products, arithmetic and copies ran while one was open for 1% of the time, Pallas kernels for 17%

profile of v5, /device:TPU:0, one launch (start us, length us, event | category | flops | bytes accessed | tf_op | source)
XLA Modules:
  0.0 117.6 jit_solution(3956226746628620079)
XLA Ops:
  0.6 3.0 %collective-permute-start.1 = (bf16[320,1024]{1,0:T(8,128)(2,1)}, bf16[320,1024]{1,0:T(8,128)(2,1)S(1)}, u32[]{:S(2)}, u32[]{:S(2)}) collective-permute-start(bf16[320,1024]{1,0:T(8,128)(2,1)} %bitcast.14), channel_id=1, source_target_pairs={{0,1},{1,0},{2,3},{3,2},{4,5},{5,4},{6,7},{7,6},{8,9},{9,8},{10,11... | collective-permute-start | bytes 1966088 | tf_op jit(solution)/shard_map/ppermute | solution.py:25
  3.6 1.5 %collective-permute-start.2 = (bf16[320,1024]{1,0:T(8,128)(2,1)}, bf16[320,1024]{1,0:T(8,128)(2,1)S(1)}, u32[]{:S(2)}, u32[]{:S(2)}) collective-permute-start(bf16[320,1024]{1,0:T(8,128)(2,1)} %bitcast.15), channel_id=1, source_target_pairs={{0,2},{1,3},{2,0},{3,1},{4,6},{5,7},{6,4},{7,5},{8,10},{9,11},{10,... | collective-permute-start | bytes 1966088 | tf_op jit(solution)/shard_map/ppermute | solution.py:25
  5.2 1.1 copy-done.3
  6.4 2.7 %collective-permute-start.5 = (bf16[320,512]{1,0:T(8,128)(2,1)S(1)}, bf16[320,512]{1,0:T(8,128)(2,1)S(1)}, u32[]{:S(2)}, u32[]{:S(2)}) collective-permute-start(bf16[320,512]{1,0:T(8,128)(2,1)S(1)} %get-tuple-element.55.refs_0_), channel_id=1, source_target_pairs={{0,16},{4,20},{8,24},{12,28},{16,0},{20,4},{24,8},{28,12},{1,17},{... | collective-permute-start | bytes 983048 | tf_op jit(solution)/shard_map/ppermute | solution.py:25
  9.0 0.7 broadcast_in_dim.16.gain
  9.7 0.7 broadcast_in_dim.17.merge_gain
  10.4 1.9 %copy-done.1 = bf16[4,320,1280]{2,1,0:T(8,128)(2,1)S(1)} copy-done((bf16[4,320,1280]{2,1,0:T(8,128)(2,1)S(1)}, bf16[4,320,1280]{2,1,0:T(8,128)(2,1)}, u32[]{:S(2)}) %copy-start.1) | copy-done | bytes 3276824
  12.3 1.1 copy-done.2
  13.5 0.7 copy-done.4
  14.2 0.7 copy-done.6
  14.9 1.7 %prepare.1 = (bf16[1280,320]{1,0:T(8,128)(2,1)S(1)}, bf16[1280,1280]{1,0:T(8,128)(2,1)S(1)}, f32[1280,128]{1,0:T(8,128)S(1)}, f32[1280,128]{1,0:T(8,128)S(1)}, b...) custom-call(bf16[320,1280]{1,0:T(8,128)(2,1)S(1)} %copy-done.2, ...), custom_call_target="tpu_custom_call" | custom-call | tf_op jit(solution)/shard_map/prepare/pallas_call | solution.py:41
  16.6 2.0 %collective-permute-done.1.refs_2_ = bf16[320,1024]{1,0:T(8,128)(2,1)S(1)} collective-permute-done((bf16[320,1024]{1,0:T(8,128)(2,1)}, bf16[320,1024]{1,0:T(8,128)(2,1)S(1)}, u32[]{:S(2)}, u32[]{:S(2)}) %collective-permute-start.1) | collective-permute-done | bytes 655392 | tf_op jit(solution)/shard_map/ppermute | solution.py:25
  18.6 1.8 %collective-permute-start.3 = (bf16[160,1024]{1,0:T(8,128)(2,1)S(1)}, bf16[160,1024]{1,0:T(8,128)(2,1)S(1)}, u32[]{:S(2)}, u32[]{:S(2)}) collective-permute-start(bf16[160,1024]{1,0:T(8,128)(2,1)S(1)} %slice.18), channel_id=1, source_target_pairs={{0,2},{1,3},{2,0},{3,1},{4,6},{5,7},{6,4},{7,5},{8,10},{9,11},{10,... | collective-permute-start | bytes 983048 | tf_op jit(solution)/shard_map/ppermute | solution.py:25
  20.5 1.6 %collective-permute-start.4 = (bf16[160,1024]{1,0:T(8,128)(2,1)S(1)}, bf16[160,1024]{1,0:T(8,128)(2,1)S(1)}, u32[]{:S(2)}, u32[]{:S(2)}) collective-permute-start(bf16[160,1024]{1,0:T(8,128)(2,1)S(1)} %slice.24), channel_id=1, source_target_pairs={{0,1},{1,0},{2,3},{3,2},{4,5},{5,4},{6,7},{7,6},{8,9},{9,8},{10,11... | collective-permute-start | bytes 983048 | tf_op jit(solution)/shard_map/ppermute | solution.py:25
  22.0 2.6 %collective-permute-start = (bf16[320,512]{1,0:T(8,128)(2,1)S(1)}, bf16[320,512]{1,0:T(8,128)(2,1)S(1)}, u32[]{:S(2)}, u32[]{:S(2)}) collective-permute-start(bf16[320,512]{1,0:T(8,128)(2,1)S(1)} %get-tuple-element.56.refs_1_.refs_0_), channel_id=1, source_target_pairs={{0,16},{4,20},{8,24},{12,28},{16,0},{20,4},{24,8},{28,12},{1,17},{... | collective-permute-start | bytes 983048 | tf_op jit(solution)/shard_map/ppermute | solution.py:25
  24.6 2.9 %collective-permute-done.3.refs_4_ = bf16[160,1024]{1,0:T(8,128)(2,1)S(1)} collective-permute-done((bf16[160,1024]{1,0:T(8,128)(2,1)S(1)}, bf16[160,1024]{1,0:T(8,128)(2,1)S(1)}, u32[]{:S(2)}, u32[]{:S(2)}) %collective-permute-start.3) | collective-permute-done | bytes 327712 | tf_op jit(solution)/shard_map/ppermute | solution.py:25
  27.6 1.3 %collective-permute-done.4.refs_5_ = bf16[160,1024]{1,0:T(8,128)(2,1)S(1)} collective-permute-done((bf16[160,1024]{1,0:T(8,128)(2,1)S(1)}, bf16[160,1024]{1,0:T(8,128)(2,1)S(1)}, u32[]{:S(2)}, u32[]{:S(2)}) %collective-permute-start.4) | collective-permute-done | bytes 327712 | tf_op jit(solution)/shard_map/ppermute | solution.py:25
  28.8 1.5 %collective-permute-start.6 = (bf16[320,512]{1,0:T(8,128)(2,1)S(1)}, bf16[320,512]{1,0:T(8,128)(2,1)S(1)}, u32[]{:S(2)}, u32[]{:S(2)}) collective-permute-start(bf16[320,512]{1,0:T(8,128)(2,1)S(1)} %collective-permute-done.5.refs_0_), channel_id=1, source_target_pairs={{0,1},{1,0},{2,3},{3,2},{4,5},{5,4},{6,7},{7,6},{8,9},{9,8},{10,11... | collective-permute-start | bytes 983048 | tf_op jit(solution)/shard_map/ppermute | solution.py:25
  30.3 0.5 collective-permute-start.7
  30.8 5.5 %project.3 = (bf16[384,1024]{1,0:T(8,128)(2,1)S(1)}, bf16[1024,512]{1,0:T(8,128)(2,1)S(1)}, bf16[384,1024]{1,0:T(8,128)(2,1)S(1)}) custom-call(bf16[320,512]{1,0:T(8,128)(2,1)S(1)} %get-tuple-element.55.refs_0_, bf16[320,512]{1,0:T(8,128)(2,1)S(1)} %get-tuple-element.56.refs_1_.refs_0_, bf16[320,1024]{1,0:T(8,128)(2,1)S(1)} %collective-permute-done.1.refs_2_, ...), custom_call_target="tpu_custom_call" | custom-call | tf_op jit(solution)/shard_map/project/pallas_call | solution.py:41
  36.4 1.6 %collective-permute-done.refs_0_ = bf16[320,512]{1,0:T(8,128)(2,1)S(1)} collective-permute-done((bf16[320,512]{1,0:T(8,128)(2,1)S(1)}, bf16[320,512]{1,0:T(8,128)(2,1)S(1)}, u32[]{:S(2)}, u32[]{:S(2)}) %collective-permute-start) | collective-permute-done | bytes 327712 | tf_op jit(solution)/shard_map/ppermute | solution.py:25
  38.0 0.5 collective-permute-start.8
  38.5 1.1 collective-permute-start.9
  39.6 2.0 %collective-permute-start.10 = (s32[1024]{0:T(1024)S(1)}, s32[1024]{0:T(1024)S(1)}, u32[]{:S(2)}, u32[]{:S(2)}) collective-permute-start(s32[1024]{0:T(1024)S(1)} %copy-done.4), channel_id=1, source_target_pairs={{0,16},{4,20},{8,24},{12,28},{16,0},{20,4},{24,8},{28,12},{1,17},{... | collective-permute-start | bytes 12296 | tf_op jit(solution)/shard_map/ppermute | solution.py:25
  41.6 1.1 collective-permute-start.13
  42.7 1.8 %collective-permute-start.14 = (bf16[160,512]{1,0:T(8,128)(2,1)S(1)}, bf16[160,512]{1,0:T(8,128)(2,1)S(1)}, u32[]{:S(2)}, u32[]{:S(2)}) collective-permute-start(bf16[160,512]{1,0:T(8,128)(2,1)S(1)} %slice.26), channel_id=1, source_target_pairs={{0,1},{1,0},{2,3},{3,2},{4,5},{5,4},{6,7},{7,6},{8,9},{9,8},{10,11... | collective-permute-start | bytes 491528 | tf_op jit(solution)/shard_map/ppermute | solution.py:25
  44.6 6.4 %near.1 = (f32[384,512]{1,0:T(8,128)S(1)}, f32[8,512]{1,0:T(8,128)S(1)}, f32[384,512]{1,0:T(8,128)S(1)}, f32[8,512]{1,0:T(8,128)S(1)}) custom-call(s32[1024]{0:T(1024)S(1)} %copy-done.4, bf16[384,1024]{1,0:T(8,128)(2,1)S(1)} %get-tuple-element.65.q, bf16[1024,512]{1,0:T(8,128)(2,1)S(1)} %get-tuple-element.61.k, bf16[384,1024]{1,0:T(8,128)(2,1)S(1)} %get-tuple-element.66.v), custom_call_target="tpu_custom_call" | custom-call | tf_op jit(solution)/shard_map/near/pallas_call | solution.py:41
  51.1 0.3 collective-permute-start.11
  51.4 1.1 collective-permute-start.12
  52.5 2.1 %project.5 = (bf16[512,512]{1,0:T(8,128)(2,1)S(1)}, bf16[384,512]{1,0:T(8,128)(2,1)S(1)}) custom-call(bf16[320,512]{1,0:T(8,128)(2,1)S(1)} %collective-permute-done.5.refs_0_, bf16[320,512]{1,0:T(8,128)(2,1)S(1)} %collective-permute-done.6.refs_1_, bf16[320,512]{1,0:T(8,128)(2,1)S(1)} %collective-permute-done.7.refs_2_, ...), custom_call_target="tpu_custom_call" | custom-call | tf_op jit(solution)/shard_map/project/pallas_call | solution.py:41
  54.6 3.0 %middle.1 = (f32[384,512]{1,0:T(8,128)S(1)}, f32[8,512]{1,0:T(8,128)S(1)}, f32[384,512]{1,0:T(8,128)S(1)}, f32[8,512]{1,0:T(8,128)S(1)}) custom-call(s32[1024]{0:T(1024)S(1)} %copy-done.5, s32[1024]{0:T(1024)S(1)} %collective-permute-done.10.k_ids, bf16[384,1024]{1,0:T(8,128)(2,1)S(1)} %get-tuple-element.65.q, bf16[512,512]{1,0:T(8,128)(2,1)S(1)} %get-tuple-element.73.k, ...), custom_call_target="tpu_custom_call" | custom-call | tf_op jit(solution)/shard_map/middle/pallas_call | solution.py:41
  57.6 2.1 %project.4 = (bf16[512,512]{1,0:T(8,128)(2,1)S(1)}, bf16[384,512]{1,0:T(8,128)(2,1)S(1)}) custom-call(bf16[320,512]{1,0:T(8,128)(2,1)S(1)} %collective-permute-done.refs_0_, bf16[320,512]{1,0:T(8,128)(2,1)S(1)} %collective-permute-done.8.refs_1_, bf16[320,512]{1,0:T(8,128)(2,1)S(1)} %collective-permute-done.9.refs_2_, ...), custom_call_target="tpu_custom_call" | custom-call | tf_op jit(solution)/shard_map/project/pallas_call | solution.py:41
  59.7 2.8 %last.1 = (bf16[320,1024]{1,0:T(8,128)(2,1)S(1)}, bf16[320,512]{1,0:T(8,128)(2,1)S(1)}, bf16[320,512]{1,0:T(8,128)(2,1)S(1)}) custom-call(s32[1024]{0:T(1024)S(1)} %copy-done.5, s32[1024]{0:T(1024)S(1)} %collective-permute-done.10.k_ids, bf16[384,1024]{1,0:T(8,128)(2,1)S(1)} %get-tuple-element.65.q, bf16[512,512]{1,0:T(8,128)(2,1)S(1)} %get-tuple-element.71.k, ...), custom_call_target="tpu_custom_call" | custom-call | tf_op jit(solution)/shard_map/last/pallas_call | solution.py:41
  62.5 1.1 collective-permute-start.19
  63.6 1.7 %collective-permute-start.16 = (bf16[320,512]{1,0:T(8,128)(2,1)S(1)}, bf16[320,512]{1,0:T(8,128)(2,1)S(1)}, u32[]{:S(2)}, u32[]{:S(2)}) collective-permute-start(bf16[320,512]{1,0:T(8,128)(2,1)S(1)} %get-tuple-element.86), channel_id=1, source_target_pairs={{0,1},{1,0},{2,3},{3,2},{4,5},{5,4},{6,7},{7,6},{8,9},{9,8},{10,11... | collective-permute-start | bytes 983048 | tf_op jit(solution)/shard_map/ppermute | solution.py:25
  65.4 1.2 %rest.1 = (bf16[320,512]{1,0:T(8,128)(2,1)S(1)}, bf16[320,512]{1,0:T(8,128)(2,1)S(1)}, bf16[320,512]{1,0:T(8,128)(2,1)S(1)}, bf16[320,512]{1,0:T(8,128)(2,1)S(1)...) custom-call(bf16[320,1024]{1,0:T(8,128)(2,1)S(1)} %get-tuple-element.82.ctx, ...), custom_call_target="tpu_custom_call" | custom-call | tf_op jit(solution)/shard_map/rest/pallas_call | solution.py:41
  66.6 0.4 collective-permute-start.18
  66.9 1.0 collective-permute-start.15
  67.9 5.3 %collective-permute-done.19 = bf16[320,512]{1,0:T(8,128)(2,1)S(1)} collective-permute-done((bf16[320,512]{1,0:T(8,128)(2,1)S(1)}, bf16[320,512]{1,0:T(8,128)(2,1)S(1)}, u32[]{:S(2)}, u32[]{:S(2)}) %collective-permute-start.19) | collective-permute-done | bytes 327712 | tf_op jit(solution)/shard_map/ppermute | solution.py:25
  73.3 1.1 collective-permute-start.20
  74.5 1.6 %collective-permute-start.17 = (bf16[320,512]{1,0:T(8,128)(2,1)S(1)}, bf16[320,512]{1,0:T(8,128)(2,1)S(1)}, u32[]{:S(2)}, u32[]{:S(2)}) collective-permute-start(bf16[320,512]{1,0:T(8,128)(2,1)S(1)} %add_convert_fusion.1), channel_id=1, source_target_pairs={{0,2},{1,3},{2,0},{3,1},{4,6},{5,7},{6,4},{7,5},{8,10},{9,11},{10,... | collective-permute-start | bytes 983048 | tf_op jit(solution)/shard_map/ppermute | solution.py:25
  76.2 1.1 collective-permute-done.18.refs_2_
  77.4 0.7 collective-permute-done.15.refs_2_
  78.1 4.1 %collective-permute-done.20.refs_3_ = bf16[320,512]{1,0:T(8,128)(2,1)S(1)} collective-permute-done((bf16[320,512]{1,0:T(8,128)(2,1)S(1)}, bf16[320,512]{1,0:T(8,128)(2,1)S(1)}, u32[]{:S(2)}, u32[]{:S(2)}) %collective-permute-start.20) | collective-permute-done | bytes 327712 | tf_op jit(solution)/shard_map/ppermute | solution.py:25
  82.2 1.4 %hidden.1 = (bf16[320,1024]{1,0:T(8,128)(2,1)}, bf16[320,1024]{1,0:T(8,128)(2,1)S(1)}, f32[8,1024]{1,0:T(8,128)S(1)}) custom-call(f32[320,512]{1,0:T(8,128)S(1)} %fold.2.refs_0_, bf16[320,512]{1,0:T(8,128)(2,1)S(1)} %collective-permute-done.17.refs_1_, f32[320,512]{1,0:T(8,128)S(1)} %fold.3.refs_2_, bf16[320,512]{1,0:T(8,128)(2,1)S(1)} %collective-permute-done.20.refs_3_), custom_call_target="tpu_custom_call" | custom-call | tf_op jit(solution)/shard_map/hidden/pallas_call | solution.py:41
  83.6 1.1 collective-permute-start.21
  84.7 1.3 %collective-permute-start.22 = (f32[8,1024]{1,0:T(8,128)S(1)}, f32[8,1024]{1,0:T(8,128)S(1)}, u32[]{:S(2)}, u32[]{:S(2)}) collective-permute-start(f32[8,1024]{1,0:T(8,128)S(1)} %get-tuple-element.95.refs_0_), channel_id=1, source_target_pairs={{0,2},{1,3},{2,0},{3,1},{4,6},{5,7},{6,4},{7,5},{8,10},{9,11},{10,... | collective-permute-start | bytes 98312 | tf_op jit(solution)/shard_map/ppermute | solution.py:25
  86.1 1.0 collective-permute-start.23
  87.1 0.8 collective-permute-done.21.refs_1_
  87.9 2.2 %collective-permute-done.22.refs_2_ = f32[8,1024]{1,0:T(8,128)S(1)} collective-permute-done((f32[8,1024]{1,0:T(8,128)S(1)}, f32[8,1024]{1,0:T(8,128)S(1)}, u32[]{:S(2)}, u32[]{:S(2)}) %collective-permute-start.22) | collective-permute-done | bytes 32800 | tf_op jit(solution)/shard_map/ppermute | solution.py:25
  90.1 1.2 collective-permute-done.23.refs_3_
  91.3 1.7 %merge.1 = (bf16[320,256]{1,0:T(8,128)(2,1)S(1)}, bf16[320,256]{1,0:T(8,128)(2,1)S(1)}, bf16[320,256]{1,0:T(8,128)(2,1)S(1)}, bf16[320,256]{1,0:T(8,128)(2,1)S(1)}) custom-call(bf16[320,1024]{1,0:T(8,128)(2,1)S(1)} %get-tuple-element.94.source, f32[8,1024]{1,0:T(8,128)S(1)} %get-tuple-element.95.refs_0_, f32[8,1024]{1,0:T(8,128)S(1)} %collective-permute-done.21.refs_1_, ...), custom_call_target="tpu_custom_call" | custom-call | tf_op jit(solution)/shard_map/merge/pallas_call | solution.py:41
  93.0 1.1 collective-permute-start.24
  94.1 1.1 collective-permute-start.25
  95.3 1.3 %collective-permute-start.26 = (bf16[320,256]{1,0:T(8,128)(2,1)S(1)}, bf16[320,256]{1,0:T(8,128)(2,1)S(1)}, u32[]{:S(2)}, u32[]{:S(2)}) collective-permute-start(bf16[320,256]{1,0:T(8,128)(2,1)S(1)} %get-tuple-element.101), channel_id=1, source_target_pairs={{0,2},{1,3},{2,0},{3,1},{4,6},{5,7},{6,4},{7,5},{8,10},{9,11},{10,... | collective-permute-start | bytes 491528 | tf_op jit(solution)/shard_map/ppermute | solution.py:25
  96.6 2.8 %collective-permute-done.24.refs_0_ = bf16[320,256]{1,0:T(8,128)(2,1)S(1)} collective-permute-done((bf16[320,256]{1,0:T(8,128)(2,1)S(1)}, bf16[320,256]{1,0:T(8,128)(2,1)S(1)}, u32[]{:S(2)}, u32[]{:S(2)}) %collective-permute-start.24) | collective-permute-done | bytes 163872 | tf_op jit(solution)/shard_map/ppermute | solution.py:25
  99.4 0.9 collective-permute-done.25.refs_1_
  100.3 0.8 collective-permute-done.26.refs_2_
  101.4 4.6 %collective-permute-start.27 = (bf16[320,128]{1,0:T(8,128)(2,1)S(1)}, bf16[320,128]{1,0:T(8,128)(2,1)S(1)}, u32[]{:S(2)}, u32[]{:S(2)}) collective-permute-start(bf16[320,128]{1,0:T(8,128)(2,1)S(1)} %get-tuple-element.105), channel_id=1, source_target_pairs={{0,8},{4,12},{8,0},{12,4},{16,24},{20,28},{24,16},{28,20},{1,9},{5... | collective-permute-start | bytes 245768 | tf_op jit(solution)/shard_map/ppermute | solution.py:25
  106.0 2.8 %collective-permute-start.28 = (bf16[320,128]{1,0:T(8,128)(2,1)S(1)}, bf16[320,128]{1,0:T(8,128)(2,1)S(1)}, u32[]{:S(2)}, u32[]{:S(2)}) collective-permute-start(bf16[320,128]{1,0:T(8,128)(2,1)S(1)} %get-tuple-element.106), channel_id=1, source_target_pairs={{0,16},{4,20},{8,24},{12,28},{16,0},{20,4},{24,8},{28,12},{1,17},{... | collective-permute-start | bytes 245768 | tf_op jit(solution)/shard_map/ppermute | solution.py:25
  108.8 3.4 %collective-permute-done.28.refs_2_ = bf16[320,128]{1,0:T(8,128)(2,1)S(1)} collective-permute-done((bf16[320,128]{1,0:T(8,128)(2,1)S(1)}, bf16[320,128]{1,0:T(8,128)(2,1)S(1)}, u32[]{:S(2)}, u32[]{:S(2)}) %collective-permute-start.28) | collective-permute-done | bytes 81952 | tf_op jit(solution)/shard_map/ppermute | solution.py:25
  112.2 2.8 %collective-permute-done.29.refs_3_ = bf16[320,128]{1,0:T(8,128)(2,1)S(1)} collective-permute-done((bf16[320,128]{1,0:T(8,128)(2,1)S(1)}, bf16[320,128]{1,0:T(8,128)(2,1)S(1)}, u32[]{:S(2)}, u32[]{:S(2)}) %collective-permute-start.29) | collective-permute-done | bytes 81952 | tf_op jit(solution)/shard_map/ppermute | solution.py:25
  115.3 1.4 %collective-permute-done.30.refs_4_ = bf16[320,256]{1,0:T(8,128)(2,1)S(1)} collective-permute-done((bf16[320,256]{1,0:T(8,128)(2,1)S(1)}, bf16[320,256]{1,0:T(8,128)(2,1)S(1)}, u32[]{:S(2)}, u32[]{:S(2)}) %collective-permute-start.30) | collective-permute-done | bytes 163872 | tf_op jit(solution)/shard_map/ppermute | solution.py:25
  116.6 1.0 settle.1
  (38 shorter events, 1.1 us)
Async XLA Ops:
  0.6 30.2 %copy-start = (bf16[3,1280,320]{1,2,0:T(8,128)(2,1)S(1)}, bf16[3,1280,320]{1,2,0:T(8,128)(2,1)}, u32[]{:S(2)}) copy-start(bf16[3,1280,320]{1,2,0:T(8,128)(2,1)} %param.11) | copy-start | bytes 7372804
  0.6 17.9 %collective-permute-start.1 = (bf16[320,1024]{1,0:T(8,128)(2,1)}, bf16[320,1024]{1,0:T(8,128)(2,1)S(1)}, u32[]{:S(2)}, u32[]{:S(2)}) collective-permute-start(bf16[320,1024]{1,0:T(8,128)(2,1)} %bitcast.14), channel_id=1, source_target_pairs={{0,1},{1,0},{2,3},{3,2},{4,5},{5,4},{6,7},{7,6},{8,9},{9,8},{10,11... | collective-permute-start | bytes 1966088 | tf_op jit(solution)/shard_map/ppermute | solution.py:25
  3.6 16.8 %collective-permute-start.2 = (bf16[320,1024]{1,0:T(8,128)(2,1)}, bf16[320,1024]{1,0:T(8,128)(2,1)S(1)}, u32[]{:S(2)}, u32[]{:S(2)}) collective-permute-start(bf16[320,1024]{1,0:T(8,128)(2,1)} %bitcast.15), channel_id=1, source_target_pairs={{0,2},{1,3},{2,0},{3,1},{4,6},{5,7},{6,4},{7,5},{8,10},{9,11},{10,... | collective-permute-start | bytes 1966088 | tf_op jit(solution)/shard_map/ppermute | solution.py:25
  5.2 1.1 copy-start.3
  6.4 18.3 %collective-permute-start.5 = (bf16[320,512]{1,0:T(8,128)(2,1)S(1)}, bf16[320,512]{1,0:T(8,128)(2,1)S(1)}, u32[]{:S(2)}, u32[]{:S(2)}) collective-permute-start(bf16[320,512]{1,0:T(8,128)(2,1)S(1)} %get-tuple-element.55.refs_0_), channel_id=1, source_target_pairs={{0,16},{4,20},{8,24},{12,28},{16,0},{20,4},{24,8},{28,12},{1,17},{... | collective-permute-start | bytes 983048 | tf_op jit(solution)/shard_map/ppermute | solution.py:25
  10.4 1.9 %copy-start.1 = (bf16[4,320,1280]{2,1,0:T(8,128)(2,1)S(1)}, bf16[4,320,1280]{2,1,0:T(8,128)(2,1)}, u32[]{:S(2)}) copy-start(bf16[4,320,1280]{2,1,0:T(8,128)(2,1)} %param.14) | copy-start | bytes 9830404
  12.3 1.1 copy-start.2
  13.5 0.7 copy-start.4
  14.2 0.7 copy-start.6
  18.6 9.0 %collective-permute-start.3 = (bf16[160,1024]{1,0:T(8,128)(2,1)S(1)}, bf16[160,1024]{1,0:T(8,128)(2,1)S(1)}, u32[]{:S(2)}, u32[]{:S(2)}) collective-permute-start(bf16[160,1024]{1,0:T(8,128)(2,1)S(1)} %slice.18), channel_id=1, source_target_pairs={{0,2},{1,3},{2,0},{3,1},{4,6},{5,7},{6,4},{7,5},{8,10},{9,11},{10,... | collective-permute-start | bytes 983048 | tf_op jit(solution)/shard_map/ppermute | solution.py:25
  20.5 8.4 %collective-permute-start.4 = (bf16[160,1024]{1,0:T(8,128)(2,1)S(1)}, bf16[160,1024]{1,0:T(8,128)(2,1)S(1)}, u32[]{:S(2)}, u32[]{:S(2)}) collective-permute-start(bf16[160,1024]{1,0:T(8,128)(2,1)S(1)} %slice.24), channel_id=1, source_target_pairs={{0,1},{1,0},{2,3},{3,2},{4,5},{5,4},{6,7},{7,6},{8,9},{9,8},{10,11... | collective-permute-start | bytes 983048 | tf_op jit(solution)/shard_map/ppermute | solution.py:25
  22.0 15.9 %collective-permute-start = (bf16[320,512]{1,0:T(8,128)(2,1)S(1)}, bf16[320,512]{1,0:T(8,128)(2,1)S(1)}, u32[]{:S(2)}, u32[]{:S(2)}) collective-permute-start(bf16[320,512]{1,0:T(8,128)(2,1)S(1)} %get-tuple-element.56.refs_1_.refs_0_), channel_id=1, source_target_pairs={{0,16},{4,20},{8,24},{12,28},{16,0},{20,4},{24,8},{28,12},{1,17},{... | collective-permute-start | bytes 983048 | tf_op jit(solution)/shard_map/ppermute | solution.py:25
  28.8 9.1 %collective-permute-start.6 = (bf16[320,512]{1,0:T(8,128)(2,1)S(1)}, bf16[320,512]{1,0:T(8,128)(2,1)S(1)}, u32[]{:S(2)}, u32[]{:S(2)}) collective-permute-start(bf16[320,512]{1,0:T(8,128)(2,1)S(1)} %collective-permute-done.5.refs_0_), channel_id=1, source_target_pairs={{0,1},{1,0},{2,3},{3,2},{4,5},{5,4},{6,7},{7,6},{8,9},{9,8},{10,11... | collective-permute-start | bytes 983048 | tf_op jit(solution)/shard_map/ppermute | solution.py:25
  30.3 7.6 %collective-permute-start.7 = (bf16[320,512]{1,0:T(8,128)(2,1)S(1)}, bf16[320,512]{1,0:T(8,128)(2,1)S(1)}, u32[]{:S(2)}, u32[]{:S(2)}) collective-permute-start(bf16[320,512]{1,0:T(8,128)(2,1)S(1)} %collective-permute-done.5.refs_0_), channel_id=1, source_target_pairs={{0,2},{1,3},{2,0},{3,1},{4,6},{5,7},{6,4},{7,5},{8,10},{9,11},{10,... | collective-permute-start | bytes 983048 | tf_op jit(solution)/shard_map/ppermute | solution.py:25
  38.0 13.0 %collective-permute-start.8 = (bf16[320,512]{1,0:T(8,128)(2,1)S(1)}, bf16[320,512]{1,0:T(8,128)(2,1)S(1)}, u32[]{:S(2)}, u32[]{:S(2)}) collective-permute-start(bf16[320,512]{1,0:T(8,128)(2,1)S(1)} %collective-permute-done.refs_0_), channel_id=1, source_target_pairs={{0,1},{1,0},{2,3},{3,2},{4,5},{5,4},{6,7},{7,6},{8,9},{9,8},{10,11... | collective-permute-start | bytes 983048 | tf_op jit(solution)/shard_map/ppermute | solution.py:25
  38.5 12.5 %collective-permute-start.9 = (bf16[320,512]{1,0:T(8,128)(2,1)S(1)}, bf16[320,512]{1,0:T(8,128)(2,1)S(1)}, u32[]{:S(2)}, u32[]{:S(2)}) collective-permute-start(bf16[320,512]{1,0:T(8,128)(2,1)S(1)} %collective-permute-done.refs_0_), channel_id=1, source_target_pairs={{0,2},{1,3},{2,0},{3,1},{4,6},{5,7},{6,4},{7,5},{8,10},{9,11},{10,... | collective-permute-start | bytes 983048 | tf_op jit(solution)/shard_map/ppermute | solution.py:25
  39.6 11.4 %collective-permute-start.10 = (s32[1024]{0:T(1024)S(1)}, s32[1024]{0:T(1024)S(1)}, u32[]{:S(2)}, u32[]{:S(2)}) collective-permute-start(s32[1024]{0:T(1024)S(1)} %copy-done.4), channel_id=1, source_target_pairs={{0,16},{4,20},{8,24},{12,28},{16,0},{20,4},{24,8},{28,12},{1,17},{... | collective-permute-start | bytes 12296 | tf_op jit(solution)/shard_map/ppermute | solution.py:25
  41.6 10.9 %collective-permute-start.13 = (bf16[160,512]{1,0:T(8,128)(2,1)S(1)}, bf16[160,512]{1,0:T(8,128)(2,1)S(1)}, u32[]{:S(2)}, u32[]{:S(2)}) collective-permute-start(bf16[160,512]{1,0:T(8,128)(2,1)S(1)} %slice.25), channel_id=1, source_target_pairs={{0,2},{1,3},{2,0},{3,1},{4,6},{5,7},{6,4},{7,5},{8,10},{9,11},{10,... | collective-permute-start | bytes 491528 | tf_op jit(solution)/shard_map/ppermute | solution.py:25
  42.7 9.7 %collective-permute-start.14 = (bf16[160,512]{1,0:T(8,128)(2,1)S(1)}, bf16[160,512]{1,0:T(8,128)(2,1)S(1)}, u32[]{:S(2)}, u32[]{:S(2)}) collective-permute-start(bf16[160,512]{1,0:T(8,128)(2,1)S(1)} %slice.26), channel_id=1, source_target_pairs={{0,1},{1,0},{2,3},{3,2},{4,5},{5,4},{6,7},{7,6},{8,9},{9,8},{10,11... | collective-permute-start | bytes 491528 | tf_op jit(solution)/shard_map/ppermute | solution.py:25
  44.6 10.0 %copy-start.5 = (s32[1024]{0:T(1024)S(1)}, s32[1024]{0:T(1024)}, u32[]{:S(2)}) copy-start(s32[1024]{0:T(1024)} %q_ids.5) | copy-start | bytes 12292
  51.1 6.5 %collective-permute-start.11 = (bf16[160,512]{1,0:T(8,128)(2,1)S(1)}, bf16[160,512]{1,0:T(8,128)(2,1)S(1)}, u32[]{:S(2)}, u32[]{:S(2)}) collective-permute-start(bf16[160,512]{1,0:T(8,128)(2,1)S(1)} %slice.22), channel_id=1, source_target_pairs={{0,2},{1,3},{2,0},{3,1},{4,6},{5,7},{6,4},{7,5},{8,10},{9,11},{10,... | collective-permute-start | bytes 491528 | tf_op jit(solution)/shard_map/ppermute | solution.py:25
  51.4 6.2 %collective-permute-start.12 = (bf16[160,512]{1,0:T(8,128)(2,1)S(1)}, bf16[160,512]{1,0:T(8,128)(2,1)S(1)}, u32[]{:S(2)}, u32[]{:S(2)}) collective-permute-start(bf16[160,512]{1,0:T(8,128)(2,1)S(1)} %slice.23), channel_id=1, source_target_pairs={{0,1},{1,0},{2,3},{3,2},{4,5},{5,4},{6,7},{7,6},{8,9},{9,8},{10,11... | collective-permute-start | bytes 491528 | tf_op jit(solution)/shard_map/ppermute | solution.py:25
  62.5 10.7 %collective-permute-start.19 = (bf16[320,512]{1,0:T(8,128)(2,1)S(1)}, bf16[320,512]{1,0:T(8,128)(2,1)S(1)}, u32[]{:S(2)}, u32[]{:S(2)}) collective-permute-start(bf16[320,512]{1,0:T(8,128)(2,1)S(1)} %get-tuple-element.91), channel_id=1, source_target_pairs={{0,2},{1,3},{2,0},{3,1},{4,6},{5,7},{6,4},{7,5},{8,10},{9,11},{10,... | collective-permute-start | bytes 983048 | tf_op jit(solution)/shard_map/ppermute | solution.py:25
  63.6 10.8 %collective-permute-start.16 = (bf16[320,512]{1,0:T(8,128)(2,1)S(1)}, bf16[320,512]{1,0:T(8,128)(2,1)S(1)}, u32[]{:S(2)}, u32[]{:S(2)}) collective-permute-start(bf16[320,512]{1,0:T(8,128)(2,1)S(1)} %get-tuple-element.86), channel_id=1, source_target_pairs={{0,1},{1,0},{2,3},{3,2},{4,5},{5,4},{6,7},{7,6},{8,9},{9,8},{10,11... | collective-permute-start | bytes 983048 | tf_op jit(solution)/shard_map/ppermute | solution.py:25
  66.6 10.7 %collective-permute-start.18 = (bf16[320,512]{1,0:T(8,128)(2,1)S(1)}, bf16[320,512]{1,0:T(8,128)(2,1)S(1)}, u32[]{:S(2)}, u32[]{:S(2)}) collective-permute-start(bf16[320,512]{1,0:T(8,128)(2,1)S(1)} %get-tuple-element.88), channel_id=1, source_target_pairs={{0,2},{1,3},{2,0},{3,1},{4,6},{5,7},{6,4},{7,5},{8,10},{9,11},{10,... | collective-permute-start | bytes 983048 | tf_op jit(solution)/shard_map/ppermute | solution.py:25
  66.9 11.1 %collective-permute-start.15 = (bf16[320,512]{1,0:T(8,128)(2,1)S(1)}, bf16[320,512]{1,0:T(8,128)(2,1)S(1)}, u32[]{:S(2)}, u32[]{:S(2)}) collective-permute-start(bf16[320,512]{1,0:T(8,128)(2,1)S(1)} %get-tuple-element.84), channel_id=1, source_target_pairs={{0,1},{1,0},{2,3},{3,2},{4,5},{5,4},{6,7},{7,6},{8,9},{9,8},{10,11... | collective-permute-start | bytes 983048 | tf_op jit(solution)/shard_map/ppermute | solution.py:25
  73.3 8.9 %collective-permute-start.20 = (bf16[320,512]{1,0:T(8,128)(2,1)S(1)}, bf16[320,512]{1,0:T(8,128)(2,1)S(1)}, u32[]{:S(2)}, u32[]{:S(2)}) collective-permute-start(bf16[320,512]{1,0:T(8,128)(2,1)S(1)} %add_convert_fusion), channel_id=1, source_target_pairs={{0,1},{1,0},{2,3},{3,2},{4,5},{5,4},{6,7},{7,6},{8,9},{9,8},{10,11... | collective-permute-start | bytes 983048 | tf_op jit(solution)/shard_map/ppermute | solution.py:25
  74.5 7.7 %collective-permute-start.17 = (bf16[320,512]{1,0:T(8,128)(2,1)S(1)}, bf16[320,512]{1,0:T(8,128)(2,1)S(1)}, u32[]{:S(2)}, u32[]{:S(2)}) collective-permute-start(bf16[320,512]{1,0:T(8,128)(2,1)S(1)} %add_convert_fusion.1), channel_id=1, source_target_pairs={{0,2},{1,3},{2,0},{3,1},{4,6},{5,7},{6,4},{7,5},{8,10},{9,11},{10,... | collective-permute-start | bytes 983048 | tf_op jit(solution)/shard_map/ppermute | solution.py:25
  83.6 4.3 %collective-permute-start.21 = (f32[8,1024]{1,0:T(8,128)S(1)}, f32[8,1024]{1,0:T(8,128)S(1)}, u32[]{:S(2)}, u32[]{:S(2)}) collective-permute-start(f32[8,1024]{1,0:T(8,128)S(1)} %get-tuple-element.95.refs_0_), channel_id=1, source_target_pairs={{0,1},{1,0},{2,3},{3,2},{4,5},{5,4},{6,7},{7,6},{8,9},{9,8},{10,11... | collective-permute-start | bytes 98312 | tf_op jit(solution)/shard_map/ppermute | solution.py:25
  84.7 5.4 %collective-permute-start.22 = (f32[8,1024]{1,0:T(8,128)S(1)}, f32[8,1024]{1,0:T(8,128)S(1)}, u32[]{:S(2)}, u32[]{:S(2)}) collective-permute-start(f32[8,1024]{1,0:T(8,128)S(1)} %get-tuple-element.95.refs_0_), channel_id=1, source_target_pairs={{0,2},{1,3},{2,0},{3,1},{4,6},{5,7},{6,4},{7,5},{8,10},{9,11},{10,... | collective-permute-start | bytes 98312 | tf_op jit(solution)/shard_map/ppermute | solution.py:25
  86.1 5.2 %collective-permute-start.23 = (f32[8,1024]{1,0:T(8,128)S(1)}, f32[8,1024]{1,0:T(8,128)S(1)}, u32[]{:S(2)}, u32[]{:S(2)}) collective-permute-start(f32[8,1024]{1,0:T(8,128)S(1)} %get-tuple-element.95.refs_0_), channel_id=1, source_target_pairs={{0,3},{1,2},{2,1},{3,0},{4,7},{5,6},{6,5},{7,4},{8,11},{9,10},{10,... | collective-permute-start | bytes 98312 | tf_op jit(solution)/shard_map/ppermute | solution.py:25
  93.0 6.3 %collective-permute-start.24 = (bf16[320,256]{1,0:T(8,128)(2,1)S(1)}, bf16[320,256]{1,0:T(8,128)(2,1)S(1)}, u32[]{:S(2)}, u32[]{:S(2)}) collective-permute-start(bf16[320,256]{1,0:T(8,128)(2,1)S(1)} %get-tuple-element.99), channel_id=1, source_target_pairs={{0,3},{1,2},{2,1},{3,0},{4,7},{5,6},{6,5},{7,4},{8,11},{9,10},{10,... | collective-permute-start | bytes 491528 | tf_op jit(solution)/shard_map/ppermute | solution.py:25
  94.1 6.2 %collective-permute-start.25 = (bf16[320,256]{1,0:T(8,128)(2,1)S(1)}, bf16[320,256]{1,0:T(8,128)(2,1)S(1)}, u32[]{:S(2)}, u32[]{:S(2)}) collective-permute-start(bf16[320,256]{1,0:T(8,128)(2,1)S(1)} %get-tuple-element.100), channel_id=1, source_target_pairs={{0,1},{1,0},{2,3},{3,2},{4,5},{5,4},{6,7},{7,6},{8,9},{9,8},{10,11... | collective-permute-start | bytes 491528 | tf_op jit(solution)/shard_map/ppermute | solution.py:25
  95.3 5.8 %collective-permute-start.26 = (bf16[320,256]{1,0:T(8,128)(2,1)S(1)}, bf16[320,256]{1,0:T(8,128)(2,1)S(1)}, u32[]{:S(2)}, u32[]{:S(2)}) collective-permute-start(bf16[320,256]{1,0:T(8,128)(2,1)S(1)} %get-tuple-element.101), channel_id=1, source_target_pairs={{0,2},{1,3},{2,0},{3,1},{4,6},{5,7},{6,4},{7,5},{8,10},{9,11},{10,... | collective-permute-start | bytes 491528 | tf_op jit(solution)/shard_map/ppermute | solution.py:25
  101.4 7.4 %collective-permute-start.27 = (bf16[320,128]{1,0:T(8,128)(2,1)S(1)}, bf16[320,128]{1,0:T(8,128)(2,1)S(1)}, u32[]{:S(2)}, u32[]{:S(2)}) collective-permute-start(bf16[320,128]{1,0:T(8,128)(2,1)S(1)} %get-tuple-element.105), channel_id=1, source_target_pairs={{0,8},{4,12},{8,0},{12,4},{16,24},{20,28},{24,16},{28,20},{1,9},{5... | collective-permute-start | bytes 245768 | tf_op jit(solution)/shard_map/ppermute | solution.py:25
  106.0 6.2 %collective-permute-start.28 = (bf16[320,128]{1,0:T(8,128)(2,1)S(1)}, bf16[320,128]{1,0:T(8,128)(2,1)S(1)}, u32[]{:S(2)}, u32[]{:S(2)}) collective-permute-start(bf16[320,128]{1,0:T(8,128)(2,1)S(1)} %get-tuple-element.106), channel_id=1, source_target_pairs={{0,16},{4,20},{8,24},{12,28},{16,0},{20,4},{24,8},{28,12},{1,17},{... | collective-permute-start | bytes 245768 | tf_op jit(solution)/shard_map/ppermute | solution.py:25
  108.8 6.2 %collective-permute-start.29 = (bf16[320,128]{1,0:T(8,128)(2,1)S(1)}, bf16[320,128]{1,0:T(8,128)(2,1)S(1)}, u32[]{:S(2)}, u32[]{:S(2)}) collective-permute-start(bf16[320,128]{1,0:T(8,128)(2,1)S(1)} %get-tuple-element.107), channel_id=1, source_target_pairs={{0,24},{4,28},{8,16},{12,20},{16,8},{20,12},{24,0},{28,4},{1,25},{... | collective-permute-start | bytes 245768 | tf_op jit(solution)/shard_map/ppermute | solution.py:25
  115.2 1.5 %collective-permute-start.30 = (bf16[320,256]{1,0:T(8,128)(2,1)S(1)}, bf16[320,256]{1,0:T(8,128)(2,1)S(1)}, u32[]{:S(2)}, u32[]{:S(2)}) collective-permute-start(bf16[320,256]{1,0:T(8,128)(2,1)S(1)} %gather.1), channel_id=1, source_target_pairs={{0,4},{4,0},{8,12},{12,8},{16,20},{20,16},{24,28},{28,24},{1,5},{5... | collective-permute-start | bytes 491528 | tf_op jit(solution)/shard_map/ppermute | solution.py:25

commit v6 on v5

--- a/solution.py
+++ b/solution.py
@@ -32,7 +32,7 @@
     return [me ^ k for k in range(count)]
 
 
-def call(body, name, args, smem, outs, scratch, loose=()):
+def call(body, name, args, smem, outs, scratch, loose=(), alias=None):
     def place(i):
         if i < smem:
             return SM
@@ -44,6 +44,7 @@
         out_specs=[VM for _ in outs],
         out_shape=[jax.ShapeDtypeStruct(s, d) for s, d in outs],
         scratch_shapes=scratch,
+        input_output_aliases=alias or {},
         compiler_params=pltpu.CompilerParams(vmem_limit_bytes=16 << 20),
         cost_estimate=pl.CostEstimate(flops=0, bytes_accessed=0, transcendentals=0),
         name=name,
@@ -289,10 +290,7 @@
 def middle_body(k_start, q_ids, k_ids, q, k, v, *refs):
     count = len(refs) // 4
     for i in range(count):
-        acc_in, top_in = refs[2 * i : 2 * i + 2]
         acc, top = refs[2 * (count + i) : 2 * (count + i) + 2]
-        acc[...] = acc_in[...]
-        top[...] = top_in[...]
         sweep(BLOCK, q_ids, k_ids, k_start, q, i * acc.shape[1], k, v, acc, top)
 
 
@@ -305,6 +303,7 @@
         2,
         [(x.shape, F32) for x in flat],
         [],
+        alias={5 + i: i for i in range(len(flat))},
     )
     return [tuple(found[2 * i : 2 * i + 2]) for i in range(len(states))]
 
@@ -329,9 +328,8 @@
         sweep(BLOCK, q_ids, k_ids, k_start, q, i * rows, k, v, acc, top)
         for h in range(heads):
             lo = h * HEAD_ROWS
-            ctx[h * HD : (h + 1) * HD, at] = (
-                acc[lo : lo + HD, :] / acc[lo + HD : lo + HD + 1, :]
-            ).astype(BF)
+            share = 1.0 / acc[lo + HD : lo + HD + 1, :]
+            ctx[h * HD : (h + 1) * HD, at] = (acc[lo : lo + HD, :] * share).astype(BF)
         outs[i][...] = multiply(w, order[-1], outs[i].shape[0], ctx[:, at])
 
 

time: 117 us -> 118 us (level); the launches traced: 118 us -> 116 us
  Pallas kernels: 29.7 us -> 27.7 us
  waiting for transfers between devices: 35.3 us -> 36.6 us
    pallas_call x16, Pallas kernels: 29.7 us -> 27.7 us  [call(): pl.pallas_call(body, in_specs=[place(i) for i in range(len(args))], out_s...]
    ppermute x31, waiting for transfers between devices: 35.3 us -> 36.6 us  [hop(): lax.ppermute(x, axis, [(i, i ^ distance) for i in range(lax.axis_size(axi...]
    unnamed x14 -> x12, local copies, waits for them, and re-layouts: 5.56 us -> 5.56 us
  transfers between devices with their start and end apart: 31 -> 31, of which waited for: 17 -> 18; matrix products, arithmetic and copies ran while one was open for 1% -> 1% of each run, Pallas kernels for 17% -> 17%
where the time goes in v6:
time: 118 us; the launch traced here: 116 us
  starting transfers between devices  43.9 us (37%)
  waiting for transfers between devices  36.6 us (31%)
  Pallas kernels  27.7 us (23%)
  local copies, waits for them, and re-layouts  7.05 us (6%)
    ppermute x31, starting transfers between devices, hop(): lax.ppermute(x, axis, [(i, i ^ distance) for i in range(lax.axis_size(axi...  43.9 us
    ppermute x31, waiting for transfers between devices, hop(): lax.ppermute(x, axis, [(i, i ^ distance) for i in range(lax.axis_size(axi...  36.6 us
    pallas_call x16, Pallas kernels, call(): pl.pallas_call(body, in_specs=[place(i) for i in range(len(args))], out_s...  27.7 us
    unnamed x12, local copies, waits for them, and re-layouts  5.56 us
  transfers between devices with their start and end apart: 31, of which 18 were waited for; matrix products, arithmetic and copies ran while one was open for 1% of the time, Pallas kernels for 17%

profile of v6, /device:TPU:0, one launch (start us, length us, event | category | flops | bytes accessed | tf_op | source)
XLA Modules:
  0.0 116.3 jit_solution(7631433127083227243)
XLA Ops:
  0.6 3.0 %collective-permute-start.1 = (bf16[320,1024]{1,0:T(8,128)(2,1)}, bf16[320,1024]{1,0:T(8,128)(2,1)S(1)}, u32[]{:S(2)}, u32[]{:S(2)}) collective-permute-start(bf16[320,1024]{1,0:T(8,128)(2,1)} %bitcast.14), channel_id=1, source_target_pairs={{0,1},{1,0},{2,3},{3,2},{4,5},{5,4},{6,7},{7,6},{8,9},{9,8},{10,11... | collective-permute-start | bytes 1966088 | tf_op jit(solution)/shard_map/ppermute | solution.py:25
  3.6 1.5 %collective-permute-start.2 = (bf16[320,1024]{1,0:T(8,128)(2,1)}, bf16[320,1024]{1,0:T(8,128)(2,1)S(1)}, u32[]{:S(2)}, u32[]{:S(2)}) collective-permute-start(bf16[320,1024]{1,0:T(8,128)(2,1)} %bitcast.15), channel_id=1, source_target_pairs={{0,2},{1,3},{2,0},{3,1},{4,6},{5,7},{6,4},{7,5},{8,10},{9,11},{10,... | collective-permute-start | bytes 1966088 | tf_op jit(solution)/shard_map/ppermute | solution.py:25
  5.2 1.1 copy-done.3
  6.4 2.7 %collective-permute-start.5 = (bf16[320,512]{1,0:T(8,128)(2,1)S(1)}, bf16[320,512]{1,0:T(8,128)(2,1)S(1)}, u32[]{:S(2)}, u32[]{:S(2)}) collective-permute-start(bf16[320,512]{1,0:T(8,128)(2,1)S(1)} %get-tuple-element.55.refs_0_), channel_id=1, source_target_pairs={{0,16},{4,20},{8,24},{12,28},{16,0},{20,4},{24,8},{28,12},{1,17},{... | collective-permute-start | bytes 983048 | tf_op jit(solution)/shard_map/ppermute | solution.py:25
  9.0 0.7 broadcast_in_dim.16.gain
  9.7 0.7 broadcast_in_dim.17.merge_gain
  10.4 1.9 %copy-done.1 = bf16[4,320,1280]{2,1,0:T(8,128)(2,1)S(1)} copy-done((bf16[4,320,1280]{2,1,0:T(8,128)(2,1)S(1)}, bf16[4,320,1280]{2,1,0:T(8,128)(2,1)}, u32[]{:S(2)}) %copy-start.1) | copy-done | bytes 3276824
  12.3 1.1 copy-done.2
  13.5 0.7 copy-done.4
  14.2 0.7 copy-done.5
  14.9 1.7 %prepare.1 = (bf16[1280,320]{1,0:T(8,128)(2,1)S(1)}, bf16[1280,1280]{1,0:T(8,128)(2,1)S(1)}, f32[1280,128]{1,0:T(8,128)S(1)}, f32[1280,128]{1,0:T(8,128)S(1)}, b...) custom-call(bf16[320,1280]{1,0:T(8,128)(2,1)S(1)} %copy-done.2, ...), custom_call_target="tpu_custom_call" | custom-call | tf_op jit(solution)/shard_map/prepare/pallas_call | solution.py:41
  16.6 2.0 %collective-permute-done.1.refs_2_ = bf16[320,1024]{1,0:T(8,128)(2,1)S(1)} collective-permute-done((bf16[320,1024]{1,0:T(8,128)(2,1)}, bf16[320,1024]{1,0:T(8,128)(2,1)S(1)}, u32[]{:S(2)}, u32[]{:S(2)}) %collective-permute-start.1) | collective-permute-done | bytes 655392 | tf_op jit(solution)/shard_map/ppermute | solution.py:25
  18.6 1.8 %collective-permute-start.3 = (bf16[160,1024]{1,0:T(8,128)(2,1)S(1)}, bf16[160,1024]{1,0:T(8,128)(2,1)S(1)}, u32[]{:S(2)}, u32[]{:S(2)}) collective-permute-start(bf16[160,1024]{1,0:T(8,128)(2,1)S(1)} %slice.18), channel_id=1, source_target_pairs={{0,2},{1,3},{2,0},{3,1},{4,6},{5,7},{6,4},{7,5},{8,10},{9,11},{10,... | collective-permute-start | bytes 983048 | tf_op jit(solution)/shard_map/ppermute | solution.py:25
  20.5 1.6 %collective-permute-start.4 = (bf16[160,1024]{1,0:T(8,128)(2,1)S(1)}, bf16[160,1024]{1,0:T(8,128)(2,1)S(1)}, u32[]{:S(2)}, u32[]{:S(2)}) collective-permute-start(bf16[160,1024]{1,0:T(8,128)(2,1)S(1)} %slice.24), channel_id=1, source_target_pairs={{0,1},{1,0},{2,3},{3,2},{4,5},{5,4},{6,7},{7,6},{8,9},{9,8},{10,11... | collective-permute-start | bytes 983048 | tf_op jit(solution)/shard_map/ppermute | solution.py:25
  22.0 2.6 %collective-permute-start = (bf16[320,512]{1,0:T(8,128)(2,1)S(1)}, bf16[320,512]{1,0:T(8,128)(2,1)S(1)}, u32[]{:S(2)}, u32[]{:S(2)}) collective-permute-start(bf16[320,512]{1,0:T(8,128)(2,1)S(1)} %get-tuple-element.56.refs_1_.refs_0_), channel_id=1, source_target_pairs={{0,16},{4,20},{8,24},{12,28},{16,0},{20,4},{24,8},{28,12},{1,17},{... | collective-permute-start | bytes 983048 | tf_op jit(solution)/shard_map/ppermute | solution.py:25
  24.6 2.9 %collective-permute-done.3.refs_4_ = bf16[160,1024]{1,0:T(8,128)(2,1)S(1)} collective-permute-done((bf16[160,1024]{1,0:T(8,128)(2,1)S(1)}, bf16[160,1024]{1,0:T(8,128)(2,1)S(1)}, u32[]{:S(2)}, u32[]{:S(2)}) %collective-permute-start.3) | collective-permute-done | bytes 327712 | tf_op jit(solution)/shard_map/ppermute | solution.py:25
  27.6 1.3 %collective-permute-done.4.refs_5_ = bf16[160,1024]{1,0:T(8,128)(2,1)S(1)} collective-permute-done((bf16[160,1024]{1,0:T(8,128)(2,1)S(1)}, bf16[160,1024]{1,0:T(8,128)(2,1)S(1)}, u32[]{:S(2)}, u32[]{:S(2)}) %collective-permute-start.4) | collective-permute-done | bytes 327712 | tf_op jit(solution)/shard_map/ppermute | solution.py:25
  28.8 1.5 %collective-permute-start.6 = (bf16[320,512]{1,0:T(8,128)(2,1)S(1)}, bf16[320,512]{1,0:T(8,128)(2,1)S(1)}, u32[]{:S(2)}, u32[]{:S(2)}) collective-permute-start(bf16[320,512]{1,0:T(8,128)(2,1)S(1)} %collective-permute-done.5.refs_0_), channel_id=1, source_target_pairs={{0,1},{1,0},{2,3},{3,2},{4,5},{5,4},{6,7},{7,6},{8,9},{9,8},{10,11... | collective-permute-start | bytes 983048 | tf_op jit(solution)/shard_map/ppermute | solution.py:25
  30.3 0.5 collective-permute-start.7
  30.8 5.5 %project.3 = (bf16[384,1024]{1,0:T(8,128)(2,1)S(1)}, bf16[1024,512]{1,0:T(8,128)(2,1)S(1)}, bf16[384,1024]{1,0:T(8,128)(2,1)S(1)}) custom-call(bf16[320,512]{1,0:T(8,128)(2,1)S(1)} %get-tuple-element.55.refs_0_, bf16[320,512]{1,0:T(8,128)(2,1)S(1)} %get-tuple-element.56.refs_1_.refs_0_, bf16[320,1024]{1,0:T(8,128)(2,1)S(1)} %collective-permute-done.1.refs_2_, ...), custom_call_target="tpu_custom_call" | custom-call | tf_op jit(solution)/shard_map/project/pallas_call | solution.py:41
  36.4 1.6 %collective-permute-done.refs_0_ = bf16[320,512]{1,0:T(8,128)(2,1)S(1)} collective-permute-done((bf16[320,512]{1,0:T(8,128)(2,1)S(1)}, bf16[320,512]{1,0:T(8,128)(2,1)S(1)}, u32[]{:S(2)}, u32[]{:S(2)}) %collective-permute-start) | collective-permute-done | bytes 327712 | tf_op jit(solution)/shard_map/ppermute | solution.py:25
  38.0 0.5 collective-permute-start.8
  38.5 1.1 collective-permute-start.9
  39.6 2.0 %collective-permute-start.10 = (s32[1024]{0:T(1024)S(1)}, s32[1024]{0:T(1024)S(1)}, u32[]{:S(2)}, u32[]{:S(2)}) collective-permute-start(s32[1024]{0:T(1024)S(1)} %copy-done.4), channel_id=1, source_target_pairs={{0,16},{4,20},{8,24},{12,28},{16,0},{20,4},{24,8},{28,12},{1,17},{... | collective-permute-start | bytes 12296 | tf_op jit(solution)/shard_map/ppermute | solution.py:25
  41.6 1.1 collective-permute-start.13
  42.7 1.8 %collective-permute-start.14 = (bf16[160,512]{1,0:T(8,128)(2,1)S(1)}, bf16[160,512]{1,0:T(8,128)(2,1)S(1)}, u32[]{:S(2)}, u32[]{:S(2)}) collective-permute-start(bf16[160,512]{1,0:T(8,128)(2,1)S(1)} %slice.26), channel_id=1, source_target_pairs={{0,1},{1,0},{2,3},{3,2},{4,5},{5,4},{6,7},{7,6},{8,9},{9,8},{10,11... | collective-permute-start | bytes 491528 | tf_op jit(solution)/shard_map/ppermute | solution.py:25
  44.6 5.6 %near.1 = (f32[384,512]{1,0:T(8,128)S(1)}, f32[8,512]{1,0:T(8,128)S(1)}, f32[384,512]{1,0:T(8,128)S(1)}, f32[8,512]{1,0:T(8,128)S(1)}) custom-call(s32[1024]{0:T(1024)S(1)} %copy-done.4, bf16[384,1024]{1,0:T(8,128)(2,1)S(1)} %get-tuple-element.65.q, bf16[1024,512]{1,0:T(8,128)(2,1)S(1)} %get-tuple-element.61.k, bf16[384,1024]{1,0:T(8,128)(2,1)S(1)} %get-tuple-element.66.v), custom_call_target="tpu_custom_call" | custom-call | tf_op jit(solution)/shard_map/near/pallas_call | solution.py:41
  50.5 1.1 collective-permute-start.12
  52.1 2.1 %project.5 = (bf16[512,512]{1,0:T(8,128)(2,1)S(1)}, bf16[384,512]{1,0:T(8,128)(2,1)S(1)}) custom-call(bf16[320,512]{1,0:T(8,128)(2,1)S(1)} %collective-permute-done.5.refs_0_, bf16[320,512]{1,0:T(8,128)(2,1)S(1)} %collective-permute-done.6.refs_1_, bf16[320,512]{1,0:T(8,128)(2,1)S(1)} %collective-permute-done.7.refs_2_, ...), custom_call_target="tpu_custom_call" | custom-call | tf_op jit(solution)/shard_map/project/pallas_call | solution.py:41
  54.2 2.9 %middle.1 = (f32[384,512]{1,0:T(8,128)S(1)}, f32[8,512]{1,0:T(8,128)S(1)}, f32[384,512]{1,0:T(8,128)S(1)}, f32[8,512]{1,0:T(8,128)S(1)}) custom-call(s32[1024]{0:T(1024)S(1)} %copy-done.4, s32[1024]{0:T(1024)S(1)} %collective-permute-done.10.k_ids, ...), custom_call_target="tpu_custom_call", output_to_operand_aliasing={{0}: (5, {}), {1}: (6, {}), {2}: (7, {}), {3}: (8, {})} | custom-call | tf_op jit(solution)/shard_map/middle/pallas_call | solution.py:41
  57.1 2.1 %project.4 = (bf16[512,512]{1,0:T(8,128)(2,1)S(1)}, bf16[384,512]{1,0:T(8,128)(2,1)S(1)}) custom-call(bf16[320,512]{1,0:T(8,128)(2,1)S(1)} %collective-permute-done.refs_0_, bf16[320,512]{1,0:T(8,128)(2,1)S(1)} %collective-permute-done.8.refs_1_, bf16[320,512]{1,0:T(8,128)(2,1)S(1)} %collective-permute-done.9.refs_2_, ...), custom_call_target="tpu_custom_call" | custom-call | tf_op jit(solution)/shard_map/project/pallas_call | solution.py:41
  59.2 1.7 %last.1 = (bf16[320,1024]{1,0:T(8,128)(2,1)S(1)}, bf16[320,512]{1,0:T(8,128)(2,1)S(1)}, bf16[320,512]{1,0:T(8,128)(2,1)S(1)}) custom-call(s32[1024]{0:T(1024)S(1)} %copy-done.4, s32[1024]{0:T(1024)S(1)} %collective-permute-done.10.k_ids, bf16[384,1024]{1,0:T(8,128)(2,1)S(1)} %get-tuple-element.65.q, bf16[512,512]{1,0:T(8,128)(2,1)S(1)} %get-tuple-element.71.k, ...), custom_call_target="tpu_custom_call" | custom-call | tf_op jit(solution)/shard_map/last/pallas_call | solution.py:41
  60.9 1.1 collective-permute-start.19
  62.0 1.3 %collective-permute-start.16 = (bf16[320,512]{1,0:T(8,128)(2,1)S(1)}, bf16[320,512]{1,0:T(8,128)(2,1)S(1)}, u32[]{:S(2)}, u32[]{:S(2)}) collective-permute-start(bf16[320,512]{1,0:T(8,128)(2,1)S(1)} %get-tuple-element.86), channel_id=1, source_target_pairs={{0,1},{1,0},{2,3},{3,2},{4,5},{5,4},{6,7},{7,6},{8,9},{9,8},{10,11... | collective-permute-start | bytes 983048 | tf_op jit(solution)/shard_map/ppermute | solution.py:25
  63.4 1.2 %rest.1 = (bf16[320,512]{1,0:T(8,128)(2,1)S(1)}, bf16[320,512]{1,0:T(8,128)(2,1)S(1)}, bf16[320,512]{1,0:T(8,128)(2,1)S(1)}, bf16[320,512]{1,0:T(8,128)(2,1)S(1)...) custom-call(bf16[320,1024]{1,0:T(8,128)(2,1)S(1)} %get-tuple-element.82.ctx, ...), custom_call_target="tpu_custom_call" | custom-call | tf_op jit(solution)/shard_map/rest/pallas_call | solution.py:41
  64.6 1.2 %collective-permute-start.18 = (bf16[320,512]{1,0:T(8,128)(2,1)S(1)}, bf16[320,512]{1,0:T(8,128)(2,1)S(1)}, u32[]{:S(2)}, u32[]{:S(2)}) collective-permute-start(bf16[320,512]{1,0:T(8,128)(2,1)S(1)} %get-tuple-element.88), channel_id=1, source_target_pairs={{0,2},{1,3},{2,0},{3,1},{4,6},{5,7},{6,4},{7,5},{8,10},{9,11},{10,... | collective-permute-start | bytes 983048 | tf_op jit(solution)/shard_map/ppermute | solution.py:25
  65.8 0.5 collective-permute-start.15
  66.3 5.3 %collective-permute-done.19 = bf16[320,512]{1,0:T(8,128)(2,1)S(1)} collective-permute-done((bf16[320,512]{1,0:T(8,128)(2,1)S(1)}, bf16[320,512]{1,0:T(8,128)(2,1)S(1)}, u32[]{:S(2)}, u32[]{:S(2)}) %collective-permute-start.19) | collective-permute-done | bytes 327712 | tf_op jit(solution)/shard_map/ppermute | solution.py:25
  71.7 1.6 %collective-permute-start.20 = (bf16[320,512]{1,0:T(8,128)(2,1)S(1)}, bf16[320,512]{1,0:T(8,128)(2,1)S(1)}, u32[]{:S(2)}, u32[]{:S(2)}) collective-permute-start(bf16[320,512]{1,0:T(8,128)(2,1)S(1)} %add_convert_fusion), channel_id=1, source_target_pairs={{0,1},{1,0},{2,3},{3,2},{4,5},{5,4},{6,7},{7,6},{8,9},{9,8},{10,11... | collective-permute-start | bytes 983048 | tf_op jit(solution)/shard_map/ppermute | solution.py:25
  73.3 1.0 collective-permute-start.17
  74.3 2.8 %collective-permute-done.18.refs_2_ = bf16[320,512]{1,0:T(8,128)(2,1)S(1)} collective-permute-done((bf16[320,512]{1,0:T(8,128)(2,1)S(1)}, bf16[320,512]{1,0:T(8,128)(2,1)S(1)}, u32[]{:S(2)}, u32[]{:S(2)}) %collective-permute-start.18) | collective-permute-done | bytes 327712 | tf_op jit(solution)/shard_map/ppermute | solution.py:25
  77.2 0.7 collective-permute-done.15.refs_2_
  78.0 3.7 %collective-permute-done.20.refs_3_ = bf16[320,512]{1,0:T(8,128)(2,1)S(1)} collective-permute-done((bf16[320,512]{1,0:T(8,128)(2,1)S(1)}, bf16[320,512]{1,0:T(8,128)(2,1)S(1)}, u32[]{:S(2)}, u32[]{:S(2)}) %collective-permute-start.20) | collective-permute-done | bytes 327712 | tf_op jit(solution)/shard_map/ppermute | solution.py:25
  81.8 1.4 %hidden.1 = (bf16[320,1024]{1,0:T(8,128)(2,1)}, bf16[320,1024]{1,0:T(8,128)(2,1)S(1)}, f32[8,1024]{1,0:T(8,128)S(1)}) custom-call(f32[320,512]{1,0:T(8,128)S(1)} %fold.2.refs_0_, bf16[320,512]{1,0:T(8,128)(2,1)S(1)} %collective-permute-done.17.refs_1_, f32[320,512]{1,0:T(8,128)S(1)} %fold.3.refs_2_, bf16[320,512]{1,0:T(8,128)(2,1)S(1)} %collective-permute-done.20.refs_3_), custom_call_target="tpu_custom_call" | custom-call | tf_op jit(solution)/shard_map/hidden/pallas_call | solution.py:41
  83.1 0.9 collective-permute-start.21
  84.1 1.6 %collective-permute-start.22 = (f32[8,1024]{1,0:T(8,128)S(1)}, f32[8,1024]{1,0:T(8,128)S(1)}, u32[]{:S(2)}, u32[]{:S(2)}) collective-permute-start(f32[8,1024]{1,0:T(8,128)S(1)} %get-tuple-element.95.refs_0_), channel_id=1, source_target_pairs={{0,2},{1,3},{2,0},{3,1},{4,6},{5,7},{6,4},{7,5},{8,10},{9,11},{10,... | collective-permute-start | bytes 98312 | tf_op jit(solution)/shard_map/ppermute | solution.py:25
  85.6 1.0 collective-permute-start.23
  86.6 0.4 collective-permute-done.21.refs_1_
  87.1 2.0 %collective-permute-done.22.refs_2_ = f32[8,1024]{1,0:T(8,128)S(1)} collective-permute-done((f32[8,1024]{1,0:T(8,128)S(1)}, f32[8,1024]{1,0:T(8,128)S(1)}, u32[]{:S(2)}, u32[]{:S(2)}) %collective-permute-start.22) | collective-permute-done | bytes 32800 | tf_op jit(solution)/shard_map/ppermute | solution.py:25
  89.0 1.8 %collective-permute-done.23.refs_3_ = f32[8,1024]{1,0:T(8,128)S(1)} collective-permute-done((f32[8,1024]{1,0:T(8,128)S(1)}, f32[8,1024]{1,0:T(8,128)S(1)}, u32[]{:S(2)}, u32[]{:S(2)}) %collective-permute-start.23) | collective-permute-done | bytes 32800 | tf_op jit(solution)/shard_map/ppermute | solution.py:25
  90.9 1.7 %merge.1 = (bf16[320,256]{1,0:T(8,128)(2,1)S(1)}, bf16[320,256]{1,0:T(8,128)(2,1)S(1)}, bf16[320,256]{1,0:T(8,128)(2,1)S(1)}, bf16[320,256]{1,0:T(8,128)(2,1)S(1)}) custom-call(bf16[320,1024]{1,0:T(8,128)(2,1)S(1)} %get-tuple-element.94.source, f32[8,1024]{1,0:T(8,128)S(1)} %get-tuple-element.95.refs_0_, f32[8,1024]{1,0:T(8,128)S(1)} %collective-permute-done.21.refs_1_, ...), custom_call_target="tpu_custom_call" | custom-call | tf_op jit(solution)/shard_map/merge/pallas_call | solution.py:41
  92.6 1.1 collective-permute-start.24
  93.7 1.3 %collective-permute-start.25 = (bf16[320,256]{1,0:T(8,128)(2,1)S(1)}, bf16[320,256]{1,0:T(8,128)(2,1)S(1)}, u32[]{:S(2)}, u32[]{:S(2)}) collective-permute-start(bf16[320,256]{1,0:T(8,128)(2,1)S(1)} %get-tuple-element.100), channel_id=1, source_target_pairs={{0,1},{1,0},{2,3},{3,2},{4,5},{5,4},{6,7},{7,6},{8,9},{9,8},{10,11... | collective-permute-start | bytes 491528 | tf_op jit(solution)/shard_map/ppermute | solution.py:25
  95.0 1.2 %collective-permute-start.26 = (bf16[320,256]{1,0:T(8,128)(2,1)S(1)}, bf16[320,256]{1,0:T(8,128)(2,1)S(1)}, u32[]{:S(2)}, u32[]{:S(2)}) collective-permute-start(bf16[320,256]{1,0:T(8,128)(2,1)S(1)} %get-tuple-element.101), channel_id=1, source_target_pairs={{0,2},{1,3},{2,0},{3,1},{4,6},{5,7},{6,4},{7,5},{8,10},{9,11},{10,... | collective-permute-start | bytes 491528 | tf_op jit(solution)/shard_map/ppermute | solution.py:25
  96.2 2.8 %collective-permute-done.24.refs_0_ = bf16[320,256]{1,0:T(8,128)(2,1)S(1)} collective-permute-done((bf16[320,256]{1,0:T(8,128)(2,1)S(1)}, bf16[320,256]{1,0:T(8,128)(2,1)S(1)}, u32[]{:S(2)}, u32[]{:S(2)}) %collective-permute-start.24) | collective-permute-done | bytes 163872 | tf_op jit(solution)/shard_map/ppermute | solution.py:25
  98.9 1.1 collective-permute-done.25.refs_1_
  100.0 0.6 collective-permute-done.26.refs_2_
  100.9 4.6 %collective-permute-start.27 = (bf16[320,128]{1,0:T(8,128)(2,1)S(1)}, bf16[320,128]{1,0:T(8,128)(2,1)S(1)}, u32[]{:S(2)}, u32[]{:S(2)}) collective-permute-start(bf16[320,128]{1,0:T(8,128)(2,1)S(1)} %get-tuple-element.105), channel_id=1, source_target_pairs={{0,8},{4,12},{8,0},{12,4},{16,24},{20,28},{24,16},{28,20},{1,9},{5... | collective-permute-start | bytes 245768 | tf_op jit(solution)/shard_map/ppermute | solution.py:25
  105.5 2.0 %collective-permute-start.28 = (bf16[320,128]{1,0:T(8,128)(2,1)S(1)}, bf16[320,128]{1,0:T(8,128)(2,1)S(1)}, u32[]{:S(2)}, u32[]{:S(2)}) collective-permute-start(bf16[320,128]{1,0:T(8,128)(2,1)S(1)} %get-tuple-element.106), channel_id=1, source_target_pairs={{0,16},{4,20},{8,24},{12,28},{16,0},{20,4},{24,8},{28,12},{1,17},{... | collective-permute-start | bytes 245768 | tf_op jit(solution)/shard_map/ppermute | solution.py:25
  107.5 0.5 collective-permute-start.29
  108.0 3.3 %collective-permute-done.28.refs_2_ = bf16[320,128]{1,0:T(8,128)(2,1)S(1)} collective-permute-done((bf16[320,128]{1,0:T(8,128)(2,1)S(1)}, bf16[320,128]{1,0:T(8,128)(2,1)S(1)}, u32[]{:S(2)}, u32[]{:S(2)}) %collective-permute-start.28) | collective-permute-done | bytes 81952 | tf_op jit(solution)/shard_map/ppermute | solution.py:25
  111.3 2.5 %collective-permute-done.29.refs_3_ = bf16[320,128]{1,0:T(8,128)(2,1)S(1)} collective-permute-done((bf16[320,128]{1,0:T(8,128)(2,1)S(1)}, bf16[320,128]{1,0:T(8,128)(2,1)S(1)}, u32[]{:S(2)}, u32[]{:S(2)}) %collective-permute-start.29) | collective-permute-done | bytes 81952 | tf_op jit(solution)/shard_map/ppermute | solution.py:25
  114.0 1.4 %collective-permute-done.30.refs_4_ = bf16[320,256]{1,0:T(8,128)(2,1)S(1)} collective-permute-done((bf16[320,256]{1,0:T(8,128)(2,1)S(1)}, bf16[320,256]{1,0:T(8,128)(2,1)S(1)}, u32[]{:S(2)}, u32[]{:S(2)}) %collective-permute-start.30) | collective-permute-done | bytes 163872 | tf_op jit(solution)/shard_map/ppermute | solution.py:25
  115.4 1.0 settle.1
  (36 shorter events, 1.8 us)
Async XLA Ops:
  0.6 30.2 %copy-start = (bf16[3,1280,320]{1,2,0:T(8,128)(2,1)S(1)}, bf16[3,1280,320]{1,2,0:T(8,128)(2,1)}, u32[]{:S(2)}) copy-start(bf16[3,1280,320]{1,2,0:T(8,128)(2,1)} %param.11) | copy-start | bytes 7372804
  0.6 17.9 %collective-permute-start.1 = (bf16[320,1024]{1,0:T(8,128)(2,1)}, bf16[320,1024]{1,0:T(8,128)(2,1)S(1)}, u32[]{:S(2)}, u32[]{:S(2)}) collective-permute-start(bf16[320,1024]{1,0:T(8,128)(2,1)} %bitcast.14), channel_id=1, source_target_pairs={{0,1},{1,0},{2,3},{3,2},{4,5},{5,4},{6,7},{7,6},{8,9},{9,8},{10,11... | collective-permute-start | bytes 1966088 | tf_op jit(solution)/shard_map/ppermute | solution.py:25
  3.6 16.8 %collective-permute-start.2 = (bf16[320,1024]{1,0:T(8,128)(2,1)}, bf16[320,1024]{1,0:T(8,128)(2,1)S(1)}, u32[]{:S(2)}, u32[]{:S(2)}) collective-permute-start(bf16[320,1024]{1,0:T(8,128)(2,1)} %bitcast.15), channel_id=1, source_target_pairs={{0,2},{1,3},{2,0},{3,1},{4,6},{5,7},{6,4},{7,5},{8,10},{9,11},{10,... | collective-permute-start | bytes 1966088 | tf_op jit(solution)/shard_map/ppermute | solution.py:25
  5.2 1.1 copy-start.3
  6.4 18.3 %collective-permute-start.5 = (bf16[320,512]{1,0:T(8,128)(2,1)S(1)}, bf16[320,512]{1,0:T(8,128)(2,1)S(1)}, u32[]{:S(2)}, u32[]{:S(2)}) collective-permute-start(bf16[320,512]{1,0:T(8,128)(2,1)S(1)} %get-tuple-element.55.refs_0_), channel_id=1, source_target_pairs={{0,16},{4,20},{8,24},{12,28},{16,0},{20,4},{24,8},{28,12},{1,17},{... | collective-permute-start | bytes 983048 | tf_op jit(solution)/shard_map/ppermute | solution.py:25
  10.4 1.9 %copy-start.1 = (bf16[4,320,1280]{2,1,0:T(8,128)(2,1)S(1)}, bf16[4,320,1280]{2,1,0:T(8,128)(2,1)}, u32[]{:S(2)}) copy-start(bf16[4,320,1280]{2,1,0:T(8,128)(2,1)} %param.14) | copy-start | bytes 9830404
  12.3 1.1 copy-start.2
  13.5 0.7 copy-start.4
  14.2 0.7 copy-start.5
  18.6 9.0 %collective-permute-start.3 = (bf16[160,1024]{1,0:T(8,128)(2,1)S(1)}, bf16[160,1024]{1,0:T(8,128)(2,1)S(1)}, u32[]{:S(2)}, u32[]{:S(2)}) collective-permute-start(bf16[160,1024]{1,0:T(8,128)(2,1)S(1)} %slice.18), channel_id=1, source_target_pairs={{0,2},{1,3},{2,0},{3,1},{4,6},{5,7},{6,4},{7,5},{8,10},{9,11},{10,... | collective-permute-start | bytes 983048 | tf_op jit(solution)/shard_map/ppermute | solution.py:25
  20.5 8.4 %collective-permute-start.4 = (bf16[160,1024]{1,0:T(8,128)(2,1)S(1)}, bf16[160,1024]{1,0:T(8,128)(2,1)S(1)}, u32[]{:S(2)}, u32[]{:S(2)}) collective-permute-start(bf16[160,1024]{1,0:T(8,128)(2,1)S(1)} %slice.24), channel_id=1, source_target_pairs={{0,1},{1,0},{2,3},{3,2},{4,5},{5,4},{6,7},{7,6},{8,9},{9,8},{10,11... | collective-permute-start | bytes 983048 | tf_op jit(solution)/shard_map/ppermute | solution.py:25
  22.0 15.9 %collective-permute-start = (bf16[320,512]{1,0:T(8,128)(2,1)S(1)}, bf16[320,512]{1,0:T(8,128)(2,1)S(1)}, u32[]{:S(2)}, u32[]{:S(2)}) collective-permute-start(bf16[320,512]{1,0:T(8,128)(2,1)S(1)} %get-tuple-element.56.refs_1_.refs_0_), channel_id=1, source_target_pairs={{0,16},{4,20},{8,24},{12,28},{16,0},{20,4},{24,8},{28,12},{1,17},{... | collective-permute-start | bytes 983048 | tf_op jit(solution)/shard_map/ppermute | solution.py:25
  28.8 9.1 %collective-permute-start.6 = (bf16[320,512]{1,0:T(8,128)(2,1)S(1)}, bf16[320,512]{1,0:T(8,128)(2,1)S(1)}, u32[]{:S(2)}, u32[]{:S(2)}) collective-permute-start(bf16[320,512]{1,0:T(8,128)(2,1)S(1)} %collective-permute-done.5.refs_0_), channel_id=1, source_target_pairs={{0,1},{1,0},{2,3},{3,2},{4,5},{5,4},{6,7},{7,6},{8,9},{9,8},{10,11... | collective-permute-start | bytes 983048 | tf_op jit(solution)/shard_map/ppermute | solution.py:25
  30.3 7.6 %collective-permute-start.7 = (bf16[320,512]{1,0:T(8,128)(2,1)S(1)}, bf16[320,512]{1,0:T(8,128)(2,1)S(1)}, u32[]{:S(2)}, u32[]{:S(2)}) collective-permute-start(bf16[320,512]{1,0:T(8,128)(2,1)S(1)} %collective-permute-done.5.refs_0_), channel_id=1, source_target_pairs={{0,2},{1,3},{2,0},{3,1},{4,6},{5,7},{6,4},{7,5},{8,10},{9,11},{10,... | collective-permute-start | bytes 983048 | tf_op jit(solution)/shard_map/ppermute | solution.py:25
  38.0 12.2 %collective-permute-start.8 = (bf16[320,512]{1,0:T(8,128)(2,1)S(1)}, bf16[320,512]{1,0:T(8,128)(2,1)S(1)}, u32[]{:S(2)}, u32[]{:S(2)}) collective-permute-start(bf16[320,512]{1,0:T(8,128)(2,1)S(1)} %collective-permute-done.refs_0_), channel_id=1, source_target_pairs={{0,1},{1,0},{2,3},{3,2},{4,5},{5,4},{6,7},{7,6},{8,9},{9,8},{10,11... | collective-permute-start | bytes 983048 | tf_op jit(solution)/shard_map/ppermute | solution.py:25
  38.5 11.7 %collective-permute-start.9 = (bf16[320,512]{1,0:T(8,128)(2,1)S(1)}, bf16[320,512]{1,0:T(8,128)(2,1)S(1)}, u32[]{:S(2)}, u32[]{:S(2)}) collective-permute-start(bf16[320,512]{1,0:T(8,128)(2,1)S(1)} %collective-permute-done.refs_0_), channel_id=1, source_target_pairs={{0,2},{1,3},{2,0},{3,1},{4,6},{5,7},{6,4},{7,5},{8,10},{9,11},{10,... | collective-permute-start | bytes 983048 | tf_op jit(solution)/shard_map/ppermute | solution.py:25
  39.6 10.6 %collective-permute-start.10 = (s32[1024]{0:T(1024)S(1)}, s32[1024]{0:T(1024)S(1)}, u32[]{:S(2)}, u32[]{:S(2)}) collective-permute-start(s32[1024]{0:T(1024)S(1)} %copy-done.4), channel_id=1, source_target_pairs={{0,16},{4,20},{8,24},{12,28},{16,0},{20,4},{24,8},{28,12},{1,17},{... | collective-permute-start | bytes 12296 | tf_op jit(solution)/shard_map/ppermute | solution.py:25
  41.6 10.4 %collective-permute-start.13 = (bf16[160,512]{1,0:T(8,128)(2,1)S(1)}, bf16[160,512]{1,0:T(8,128)(2,1)S(1)}, u32[]{:S(2)}, u32[]{:S(2)}) collective-permute-start(bf16[160,512]{1,0:T(8,128)(2,1)S(1)} %slice.25), channel_id=1, source_target_pairs={{0,2},{1,3},{2,0},{3,1},{4,6},{5,7},{6,4},{7,5},{8,10},{9,11},{10,... | collective-permute-start | bytes 491528 | tf_op jit(solution)/shard_map/ppermute | solution.py:25
  42.7 9.3 %collective-permute-start.14 = (bf16[160,512]{1,0:T(8,128)(2,1)S(1)}, bf16[160,512]{1,0:T(8,128)(2,1)S(1)}, u32[]{:S(2)}, u32[]{:S(2)}) collective-permute-start(bf16[160,512]{1,0:T(8,128)(2,1)S(1)} %slice.26), channel_id=1, source_target_pairs={{0,1},{1,0},{2,3},{3,2},{4,5},{5,4},{6,7},{7,6},{8,9},{9,8},{10,11... | collective-permute-start | bytes 491528 | tf_op jit(solution)/shard_map/ppermute | solution.py:25
  50.2 6.8 %collective-permute-start.11 = (bf16[160,512]{1,0:T(8,128)(2,1)S(1)}, bf16[160,512]{1,0:T(8,128)(2,1)S(1)}, u32[]{:S(2)}, u32[]{:S(2)}) collective-permute-start(bf16[160,512]{1,0:T(8,128)(2,1)S(1)} %slice.22), channel_id=1, source_target_pairs={{0,2},{1,3},{2,0},{3,1},{4,6},{5,7},{6,4},{7,5},{8,10},{9,11},{10,... | collective-permute-start | bytes 491528 | tf_op jit(solution)/shard_map/ppermute | solution.py:25
  50.5 6.5 %collective-permute-start.12 = (bf16[160,512]{1,0:T(8,128)(2,1)S(1)}, bf16[160,512]{1,0:T(8,128)(2,1)S(1)}, u32[]{:S(2)}, u32[]{:S(2)}) collective-permute-start(bf16[160,512]{1,0:T(8,128)(2,1)S(1)} %slice.23), channel_id=1, source_target_pairs={{0,1},{1,0},{2,3},{3,2},{4,5},{5,4},{6,7},{7,6},{8,9},{9,8},{10,11... | collective-permute-start | bytes 491528 | tf_op jit(solution)/shard_map/ppermute | solution.py:25
  60.9 10.7 %collective-permute-start.19 = (bf16[320,512]{1,0:T(8,128)(2,1)S(1)}, bf16[320,512]{1,0:T(8,128)(2,1)S(1)}, u32[]{:S(2)}, u32[]{:S(2)}) collective-permute-start(bf16[320,512]{1,0:T(8,128)(2,1)S(1)} %get-tuple-element.91), channel_id=1, source_target_pairs={{0,2},{1,3},{2,0},{3,1},{4,6},{5,7},{6,4},{7,5},{8,10},{9,11},{10,... | collective-permute-start | bytes 983048 | tf_op jit(solution)/shard_map/ppermute | solution.py:25
  62.0 11.2 %collective-permute-start.16 = (bf16[320,512]{1,0:T(8,128)(2,1)S(1)}, bf16[320,512]{1,0:T(8,128)(2,1)S(1)}, u32[]{:S(2)}, u32[]{:S(2)}) collective-permute-start(bf16[320,512]{1,0:T(8,128)(2,1)S(1)} %get-tuple-element.86), channel_id=1, source_target_pairs={{0,1},{1,0},{2,3},{3,2},{4,5},{5,4},{6,7},{7,6},{8,9},{9,8},{10,11... | collective-permute-start | bytes 983048 | tf_op jit(solution)/shard_map/ppermute | solution.py:25
  64.6 12.5 %collective-permute-start.18 = (bf16[320,512]{1,0:T(8,128)(2,1)S(1)}, bf16[320,512]{1,0:T(8,128)(2,1)S(1)}, u32[]{:S(2)}, u32[]{:S(2)}) collective-permute-start(bf16[320,512]{1,0:T(8,128)(2,1)S(1)} %get-tuple-element.88), channel_id=1, source_target_pairs={{0,2},{1,3},{2,0},{3,1},{4,6},{5,7},{6,4},{7,5},{8,10},{9,11},{10,... | collective-permute-start | bytes 983048 | tf_op jit(solution)/shard_map/ppermute | solution.py:25
  65.8 12.1 %collective-permute-start.15 = (bf16[320,512]{1,0:T(8,128)(2,1)S(1)}, bf16[320,512]{1,0:T(8,128)(2,1)S(1)}, u32[]{:S(2)}, u32[]{:S(2)}) collective-permute-start(bf16[320,512]{1,0:T(8,128)(2,1)S(1)} %get-tuple-element.84), channel_id=1, source_target_pairs={{0,1},{1,0},{2,3},{3,2},{4,5},{5,4},{6,7},{7,6},{8,9},{9,8},{10,11... | collective-permute-start | bytes 983048 | tf_op jit(solution)/shard_map/ppermute | solution.py:25
  71.7 10.0 %collective-permute-start.20 = (bf16[320,512]{1,0:T(8,128)(2,1)S(1)}, bf16[320,512]{1,0:T(8,128)(2,1)S(1)}, u32[]{:S(2)}, u32[]{:S(2)}) collective-permute-start(bf16[320,512]{1,0:T(8,128)(2,1)S(1)} %add_convert_fusion), channel_id=1, source_target_pairs={{0,1},{1,0},{2,3},{3,2},{4,5},{5,4},{6,7},{7,6},{8,9},{9,8},{10,11... | collective-permute-start | bytes 983048 | tf_op jit(solution)/shard_map/ppermute | solution.py:25
  73.3 8.4 %collective-permute-start.17 = (bf16[320,512]{1,0:T(8,128)(2,1)S(1)}, bf16[320,512]{1,0:T(8,128)(2,1)S(1)}, u32[]{:S(2)}, u32[]{:S(2)}) collective-permute-start(bf16[320,512]{1,0:T(8,128)(2,1)S(1)} %add_convert_fusion.1), channel_id=1, source_target_pairs={{0,2},{1,3},{2,0},{3,1},{4,6},{5,7},{6,4},{7,5},{8,10},{9,11},{10,... | collective-permute-start | bytes 983048 | tf_op jit(solution)/shard_map/ppermute | solution.py:25
  83.1 3.9 %collective-permute-start.21 = (f32[8,1024]{1,0:T(8,128)S(1)}, f32[8,1024]{1,0:T(8,128)S(1)}, u32[]{:S(2)}, u32[]{:S(2)}) collective-permute-start(f32[8,1024]{1,0:T(8,128)S(1)} %get-tuple-element.95.refs_0_), channel_id=1, source_target_pairs={{0,1},{1,0},{2,3},{3,2},{4,5},{5,4},{6,7},{7,6},{8,9},{9,8},{10,11... | collective-permute-start | bytes 98312 | tf_op jit(solution)/shard_map/ppermute | solution.py:25
  84.1 5.0 %collective-permute-start.22 = (f32[8,1024]{1,0:T(8,128)S(1)}, f32[8,1024]{1,0:T(8,128)S(1)}, u32[]{:S(2)}, u32[]{:S(2)}) collective-permute-start(f32[8,1024]{1,0:T(8,128)S(1)} %get-tuple-element.95.refs_0_), channel_id=1, source_target_pairs={{0,2},{1,3},{2,0},{3,1},{4,6},{5,7},{6,4},{7,5},{8,10},{9,11},{10,... | collective-permute-start | bytes 98312 | tf_op jit(solution)/shard_map/ppermute | solution.py:25
  85.6 5.2 %collective-permute-start.23 = (f32[8,1024]{1,0:T(8,128)S(1)}, f32[8,1024]{1,0:T(8,128)S(1)}, u32[]{:S(2)}, u32[]{:S(2)}) collective-permute-start(f32[8,1024]{1,0:T(8,128)S(1)} %get-tuple-element.95.refs_0_), channel_id=1, source_target_pairs={{0,3},{1,2},{2,1},{3,0},{4,7},{5,6},{6,5},{7,4},{8,11},{9,10},{10,... | collective-permute-start | bytes 98312 | tf_op jit(solution)/shard_map/ppermute | solution.py:25
  92.6 6.3 %collective-permute-start.24 = (bf16[320,256]{1,0:T(8,128)(2,1)S(1)}, bf16[320,256]{1,0:T(8,128)(2,1)S(1)}, u32[]{:S(2)}, u32[]{:S(2)}) collective-permute-start(bf16[320,256]{1,0:T(8,128)(2,1)S(1)} %get-tuple-element.99), channel_id=1, source_target_pairs={{0,3},{1,2},{2,1},{3,0},{4,7},{5,6},{6,5},{7,4},{8,11},{9,10},{10,... | collective-permute-start | bytes 491528 | tf_op jit(solution)/shard_map/ppermute | solution.py:25
  93.7 6.3 %collective-permute-start.25 = (bf16[320,256]{1,0:T(8,128)(2,1)S(1)}, bf16[320,256]{1,0:T(8,128)(2,1)S(1)}, u32[]{:S(2)}, u32[]{:S(2)}) collective-permute-start(bf16[320,256]{1,0:T(8,128)(2,1)S(1)} %get-tuple-element.100), channel_id=1, source_target_pairs={{0,1},{1,0},{2,3},{3,2},{4,5},{5,4},{6,7},{7,6},{8,9},{9,8},{10,11... | collective-permute-start | bytes 491528 | tf_op jit(solution)/shard_map/ppermute | solution.py:25
  95.0 5.7 %collective-permute-start.26 = (bf16[320,256]{1,0:T(8,128)(2,1)S(1)}, bf16[320,256]{1,0:T(8,128)(2,1)S(1)}, u32[]{:S(2)}, u32[]{:S(2)}) collective-permute-start(bf16[320,256]{1,0:T(8,128)(2,1)S(1)} %get-tuple-element.101), channel_id=1, source_target_pairs={{0,2},{1,3},{2,0},{3,1},{4,6},{5,7},{6,4},{7,5},{8,10},{9,11},{10,... | collective-permute-start | bytes 491528 | tf_op jit(solution)/shard_map/ppermute | solution.py:25
  100.9 7.0 %collective-permute-start.27 = (bf16[320,128]{1,0:T(8,128)(2,1)S(1)}, bf16[320,128]{1,0:T(8,128)(2,1)S(1)}, u32[]{:S(2)}, u32[]{:S(2)}) collective-permute-start(bf16[320,128]{1,0:T(8,128)(2,1)S(1)} %get-tuple-element.105), channel_id=1, source_target_pairs={{0,8},{4,12},{8,0},{12,4},{16,24},{20,28},{24,16},{28,20},{1,9},{5... | collective-permute-start | bytes 245768 | tf_op jit(solution)/shard_map/ppermute | solution.py:25
  105.5 5.7 %collective-permute-start.28 = (bf16[320,128]{1,0:T(8,128)(2,1)S(1)}, bf16[320,128]{1,0:T(8,128)(2,1)S(1)}, u32[]{:S(2)}, u32[]{:S(2)}) collective-permute-start(bf16[320,128]{1,0:T(8,128)(2,1)S(1)} %get-tuple-element.106), channel_id=1, source_target_pairs={{0,16},{4,20},{8,24},{12,28},{16,0},{20,4},{24,8},{28,12},{1,17},{... | collective-permute-start | bytes 245768 | tf_op jit(solution)/shard_map/ppermute | solution.py:25
  107.5 6.2 %collective-permute-start.29 = (bf16[320,128]{1,0:T(8,128)(2,1)S(1)}, bf16[320,128]{1,0:T(8,128)(2,1)S(1)}, u32[]{:S(2)}, u32[]{:S(2)}) collective-permute-start(bf16[320,128]{1,0:T(8,128)(2,1)S(1)} %get-tuple-element.107), channel_id=1, source_target_pairs={{0,24},{4,28},{8,16},{12,20},{16,8},{20,12},{24,0},{28,4},{1,25},{... | collective-permute-start | bytes 245768 | tf_op jit(solution)/shard_map/ppermute | solution.py:25
  113.9 1.5 %collective-permute-start.30 = (bf16[320,256]{1,0:T(8,128)(2,1)S(1)}, bf16[320,256]{1,0:T(8,128)(2,1)S(1)}, u32[]{:S(2)}, u32[]{:S(2)}) collective-permute-start(bf16[320,256]{1,0:T(8,128)(2,1)S(1)} %gather.1), channel_id=1, source_target_pairs={{0,4},{4,0},{8,12},{12,8},{16,20},{20,16},{24,28},{28,24},{1,5},{5... | collective-permute-start | bytes 491528 | tf_op jit(solution)/shard_map/ppermute | solution.py:25
